TPU v7x, 256 devices: a whole 4x4x8 slice. The times are simulated.
256 devices in a mesh: frame: 16 (over x_lo, y, core), head: 16 (over x_hi, z).
Axes of the slice: x: 4 (x_hi: 2, x_lo: 2; x = x_hi * 2 + x_lo), y: 4, z: 8, core: 2. Of those that a mesh axis runs over, the one named last changes fastest.
Arguments:
- query_states: bfloat16 [8192, 4096], P('frame', 'head'), may hold values from -4.6 to 4.6
- key_states: bfloat16 [8192, 4096], P('frame', 'head'), may hold values from -4.6 to 4.6
- value_states: bfloat16 [8192, 4096], P('frame', 'head'), may hold values from -24 to 24
- out_weight: bfloat16 [4096, 5120], P('head'), may hold values from -0.1875 to 0.1875
- upstream: bfloat16 [8192, 5120], P('frame'), may hold values from -72 to 72
- tile_mask: int32 [32, 5], replicated, may hold values from 0 to 1, as said below
Outputs:
- attended: bfloat16 [8192, 4096], P('frame', 'head')
- projected: bfloat16 [8192, 5120], P('frame', 'head')
- grad_query: bfloat16 [8192, 4096], P('frame', 'head')
- grad_key: bfloat16 [8192, 4096], P('frame', 'head')
- grad_value: bfloat16 [8192, 4096], P('frame', 'head')
- gram_left: float32 [32, 16, 128, 128], P('head', 'frame')
- gram_right: float32 [32, 16, 320, 320], P('head', 'frame')
Inputs may be any that keep to these rules, and one draw needn't show every extreme that they name: `tile_mask`: in every row, column 2 (the query tile's own tile) is 1.
All inputs are finite; a program needn't handle non-finite values.
Results may differ from a plain program's by a relative error of at most 0.019.
Values may be sent and summed in bfloat16 or wider, within the bound.
No kernel may reach another device: no remote copies, remote signals or barrier semaphores. Data moves between devices by JAX's collectives and lax.ppermute only.
A program may use at most 128 MiB of HBM per device.

v0:
```python
import math

import jax
import jax.numpy as jnp
from jax import lax
from jax.sharding import Mesh
from jax.sharding import PartitionSpec as P

D = 5120
HD = 128
TILE = 256
TILES_DEV = 2
CB = 320
HEAD = ("head_0", "head_1")


epsilon = 1e-06


def padded(shard, sides, width):
    for axis, dim in sides:
        devices, length = (lax.axis_size(axis), shard.shape[dim])
        up = [(i, (i + 1) % devices) for i in range(devices - 1)]
        down = [(j, i) for i, j in up]
        last = lax.slice_in_dim(shard, length - width, length, axis=dim)
        initial = lax.slice_in_dim(shard, 0, width, axis=dim)
        before = lax.ppermute(last, axis, up)
        after = lax.ppermute(initial, axis, down)
        shard = jnp.concatenate([before, shard, after], axis=dim)
    return shard


def sum_in_order(blocks, axes, sequence):
    inside = blocks.shape[1:]
    blocks = blocks.reshape(*(lax.axis_size(a) for a in axes), *inside)
    blocks = jnp.moveaxis(blocks, sequence, range(len(axes))).reshape(-1, *inside)
    for k in sequence:
        blocks = lax.psum_scatter(blocks, axes[k], scatter_dimension=0, tiled=True)
    return blocks[0]


def in_blocks(shard, dim, devices):
    lengths = shard.shape
    blocks = shard.reshape(*lengths[:dim], devices, lengths[dim] // devices, *lengths[dim + 1 :])
    return jnp.moveaxis(blocks, dim, 0)


def scatter_axes(shard, axes, sequence, dim):
    devices = lax.axis_size(axes)
    return sum_in_order(in_blocks(shard, dim, devices), axes, sequence)


def sent_and_summed(shard, axis, dim):
    blocks = in_blocks(shard, dim, lax.axis_size(axis))
    arrived = lax.all_to_all(blocks, axis, split_axis=0, concat_axis=0, tiled=True)
    return arrived.astype(jnp.float32).sum(axis=0)


def tile_allowed(tile_mask, query_tiles, key_tiles):
    tile_count = tile_mask.shape[0]
    window = tile_mask.shape[1]
    reach_tiles = (window - 1) // 2
    row_hits = (query_tiles[:, None] == jnp.arange(tile_count, dtype=jnp.int32)[None, :]).astype(
        jnp.int32
    )
    picked = jnp.sum(row_hits[:, :, None] * tile_mask[None, :, :], axis=1)
    offsets = key_tiles[None, :] - query_tiles[:, None] + reach_tiles
    col_hits = offsets[:, :, None] == jnp.arange(window, dtype=jnp.int32)[None, None, :]
    chosen = jnp.sum(jnp.where(col_hits, picked[:, None, :], 0), axis=2)
    query_inside = (query_tiles >= 0) & (query_tiles < tile_count)
    key_inside = (key_tiles >= 0) & (key_tiles < tile_count)
    return (chosen > 0) & query_inside[:, None] & key_inside[None, :]


def masked_scores(queries, key_rows, query_tile, key_tile, tile_mask):
    scaling = 1.0 / math.sqrt(queries.shape[2])
    scores = (
        jnp.einsum("thd,shd->hts", queries, key_rows, preferred_element_type=jnp.float32) * scaling
    )
    heads_here = scores.shape[0]
    query_count = queries.shape[0] // TILE
    key_count = key_rows.shape[0] // TILE
    allowed = tile_allowed(
        tile_mask,
        query_tile + jnp.arange(query_count, dtype=jnp.int32),
        key_tile + jnp.arange(key_count, dtype=jnp.int32),
    )
    blocked = scores.reshape(heads_here, query_count, TILE, key_count, TILE)
    blocked = jnp.where(allowed[None, :, None, :, None], blocked, jnp.float32(-1e30))
    return blocked.reshape(scores.shape)


def log_total(scores):
    peak = jnp.max(scores, axis=2)
    return peak + jnp.log(jnp.sum(jnp.exp(scores - peak[:, :, None]), axis=2))


def local(query_states, key_states, value_states, out_weight, upstream, tile_mask):
    tok_rows = query_states.shape[0]
    heads_here = query_states.shape[1] // HD
    scaling = 1.0 / math.sqrt(HD)
    first_tile = lax.axis_index("frame") * TILES_DEV
    queries = query_states.reshape(tok_rows, heads_here, HD)
    stacked = jnp.stack([key_states, value_states])
    extended = padded(stacked, (("frame", 1),), tok_rows)
    keys_ext = extended[0].reshape(3 * tok_rows, heads_here, HD)
    values_ext = extended[1].reshape(3 * tok_rows, heads_here, HD)
    scores = masked_scores(queries, keys_ext, first_tile, first_tile - TILES_DEV, tile_mask)
    totals = log_total(scores)
    attention = jnp.exp(scores - totals[:, :, None])
    weights = attention.astype(jnp.bfloat16)
    attended3 = jnp.einsum(
        "hts,shd->thd", weights, values_ext, preferred_element_type=jnp.float32
    ).astype(jnp.bfloat16)
    attended = attended3.reshape(tok_rows, heads_here * HD)
    partial_value = jnp.dot(attended, out_weight, preferred_element_type=jnp.float32)
    projected = (
        scatter_axes(partial_value.astype(jnp.bfloat16), HEAD, (1, 0), 1)
        .astype(jnp.float32)
        .astype(jnp.bfloat16)
    )
    grad_attended = lax.dot_general(
        upstream, out_weight, (((1,), (1,)), ((), ())), preferred_element_type=jnp.float32
    ).astype(jnp.bfloat16)
    grads3 = grad_attended.reshape(tok_rows, heads_here, HD)
    deltas = jnp.sum(grads3.astype(jnp.float32) * attended3.astype(jnp.float32), axis=2).T
    grad_probs = jnp.einsum("thd,shd->hts", grads3, values_ext, preferred_element_type=jnp.float32)
    grad_scores = (attention * (grad_probs - deltas[:, :, None])).astype(jnp.bfloat16)
    grad_query = (
        jnp.einsum("hts,shd->thd", grad_scores, keys_ext, preferred_element_type=jnp.float32)
        * scaling
    )
    grad_query = grad_query.astype(jnp.bfloat16).reshape(tok_rows, heads_here * HD)
    query_pack = jnp.stack([query_states, grad_attended])
    stat_pack = jnp.stack([totals, deltas])
    near_queries = padded(query_pack, (("frame", 1),), tok_rows)
    near_stats = padded(stat_pack, (("frame", 2),), tok_rows)
    queries_ext = near_queries[0].reshape(3 * tok_rows, heads_here, HD)
    grads_ext = near_queries[1].reshape(3 * tok_rows, heads_here, HD)
    keys_own = key_states.reshape(tok_rows, heads_here, HD)
    values_own = value_states.reshape(tok_rows, heads_here, HD)
    scores_near = masked_scores(
        queries_ext, keys_own, first_tile - TILES_DEV, first_tile, tile_mask
    )
    attention_near = jnp.exp(scores_near - near_stats[0][:, :, None])
    weights_near = attention_near.astype(jnp.bfloat16)
    grad_probs_near = jnp.einsum(
        "thd,shd->hts", grads_ext, values_own, preferred_element_type=jnp.float32
    )
    grad_scores_near = (attention_near * (grad_probs_near - near_stats[1][:, :, None])).astype(
        jnp.bfloat16
    )
    grad_keys = (
        jnp.einsum(
            "hts,thd->shd", grad_scores_near, queries_ext, preferred_element_type=jnp.float32
        )
        * scaling
    )
    grad_values = jnp.einsum(
        "hts,thd->shd", weights_near, grads_ext, preferred_element_type=jnp.float32
    )
    summed = jnp.stack([grad_keys, grad_values]).reshape(2, tok_rows, heads_here * HD)
    grad_key = summed[0].astype(jnp.bfloat16)
    grad_value = summed[1].astype(jnp.bfloat16)
    local_cols = D // lax.axis_size("frame")
    grad_cols = sent_and_summed(
        lax.dot_general(
            upstream, attended, (((0,), (0,)), ((), ())), preferred_element_type=jnp.float32
        ).astype(jnp.bfloat16),
        "frame",
        0,
    )
    blocks = grad_cols.reshape(local_cols // CB, CB, heads_here, HD)
    highest = lax.Precision.HIGHEST
    traces = jnp.einsum("bche,bche->hb", blocks, blocks, precision=highest)
    divisor = (traces + epsilon)[:, :, None, None]
    gram_left = HD * jnp.einsum("bche,bchf->hbef", blocks, blocks, precision=highest) / divisor
    gram_right = CB * jnp.einsum("bche,bdhe->hbcd", blocks, blocks, precision=highest) / divisor
    return (attended, projected, grad_query, grad_key, grad_value, gram_left, gram_right)


def solution(mesh):
    finer = Mesh(mesh.devices.reshape(mesh.shape["frame"], 2, 8), ("frame", "head_0", "head_1"))
    placed = (
        P("frame", HEAD),
        P("frame", HEAD),
        P("frame", HEAD),
        P(HEAD, None),
        P("frame", None),
        P(),
    )
    return jax.shard_map(
        local,
        mesh=finer,
        in_specs=placed,
        out_specs=(
            P("frame", HEAD),
            P("frame", HEAD),
            P("frame", HEAD),
            P("frame", HEAD),
            P("frame", HEAD),
            P(HEAD, "frame", None, None),
            P(HEAD, "frame", None, None),
        ),
        check_vma=False,
    )
```

profile of v0, /device:TPU:1, one launch (start us, length us, event | category | flops | bytes accessed | tf_op | source)
XLA Modules:
  0.0 149.6 jit_solution(9766551775362771014)
XLA Ops:
  7.2 1.2 copy.56
  10.6 5.1 %collective-permute-start.1 = (bf16[2,512,256]{1,2,0:T(8,128)(2,1)}, bf16[2,512,256]{1,2,0:T(8,128)(2,1)}, u32[]{:S(2)}, u32[]{:S(2)}) collective-permute-start(bf16[2,512,256]{1,2,0:T(8,128)(2,1)} %pad_maximum_fusion.2), channel_id=1, source_target_pairs={{16,0},{32,16},{48,32},{64,48},{80,64},{96,80},{112,96},{128,112},... | collective-permute-start | bytes 1572872 | tf_op jit(solution)/shard_map/ppermute | solution.py:28
  15.7 1.9 %collective-permute-start = (bf16[2,512,256]{1,2,0:T(8,128)(2,1)}, bf16[2,512,256]{1,2,0:T(8,128)(2,1)}, u32[]{:S(2)}, u32[]{:S(2)}) collective-permute-start(bf16[2,512,256]{1,2,0:T(8,128)(2,1)} %pad_maximum_fusion.2), channel_id=1, source_target_pairs={{0,16},{16,32},{32,48},{48,64},{64,80},{80,96},{96,112},{112,128},... | collective-permute-start | bytes 1572872 | tf_op jit(solution)/shard_map/ppermute | solution.py:27
  19.6 1.8 %copy.58 = pred[512,1536]{0,1:T(8,128)(4,1)} copy(pred[512,1536]{1,0:T(8,128)(4,1)S(1)} %bitcast.121) | data formatting | bytes 1572864 | tf_op jit(solution)/shard_map/jit(_where)/broadcast_in_dim | solution.py:89
  21.4 4.1 %convolution_convert_fusion.2 = bf16[512,256]{0,1:T(8,128)(2,1)S(1)} fusion(bf16[512,5120]{1,0:T(8,128)(2,1)} %param.10, bf16[256,5120]{1,0:T(8,128)(2,1)S(1)} %copy-done), kind=kOutput, calls=%fused_computation.29 | convolution fusion | flops 1342308352 | bytes 8126464 | tf_op jit(solution)/shard_map/dot_general | solution.py:122
  25.6 1.4 pad_maximum_fusion
  27.2 1.5 %fusion.47 = (f32[2,512]{1,0:T(2,128)S(1)}, f32[2,512,1536]{1,2,0:T(8,128)S(1)}) fusion(bf16[1536,2,128]{0,2,1:T(8,128)(2,1)S(1)} %bitcast.139, pred[512,1536]{0,1:T(8,128)(4,1)S(1)} %copy-done.11, bf16[512,256]{1,0:T(8,128)(2,1)S(1)} %copy-done.13), kind=kOutput, calls=%fused_computation.77 | convolution fusion | flops 407370752 | bytes 8130560 | tf_op jit(solution)/shard_map/thd,shd->hts/dot_general | solution.py:78
  29.6 1.2 multiply_reduce_fusion
  32.1 4.0 %convolution_convert_fusion = bf16[512,5120]{1,0:T(8,128)(2,1)} fusion(bf16[512,256]{0,1:T(8,128)(2,1)S(1)} %bitcast.127, bf16[256,5120]{1,0:T(8,128)(2,1)S(1)} %copy-done), kind=kOutput, calls=%fused_computation | convolution fusion | flops 1344798720 | bytes 8126464 | tf_op jit(solution)/shard_map/dot_general | solution.py:116
  36.0 8.0 %copy.62 = bf16[512,5120]{0,1:T(8,128)(2,1)} copy(bf16[512,5120]{1,0:T(8,128)(2,1)} %convolution_convert_fusion) | data formatting | bytes 10485760 | tf_op jit(solution)/shard_map/convert_element_type | solution.py:118
  44.0 5.4 %copy.63 = bf16[8,2,512,320]{2,3,1,0:T(8,128)(2,1)} copy(bf16[8,2,512,320]{2,3,0,1:T(8,128)(2,1)} %bitcast.117) | data formatting | bytes 10485760 | tf_op jit(solution)/shard_map/transpose | solution.py:36
  50.4 3.2 %collective-permute-start.3 = (bf16[2,512,256]{1,2,0:T(8,128)(2,1)}, bf16[2,512,256]{1,2,0:T(8,128)(2,1)}, u32[]{:S(2)}, u32[]{:S(2)}) collective-permute-start(bf16[2,512,256]{1,2,0:T(8,128)(2,1)} %pad_maximum_fusion.3), channel_id=1, source_target_pairs={{16,0},{32,16},{48,32},{64,48},{80,64},{96,80},{112,96},{128,112},... | collective-permute-start | bytes 1572872 | tf_op jit(solution)/shard_map/ppermute | solution.py:28
  53.6 2.4 %collective-permute-start.2 = (bf16[2,512,256]{1,2,0:T(8,128)(2,1)}, bf16[2,512,256]{1,2,0:T(8,128)(2,1)}, u32[]{:S(2)}, u32[]{:S(2)}) collective-permute-start(bf16[2,512,256]{1,2,0:T(8,128)(2,1)} %pad_maximum_fusion.3), channel_id=1, source_target_pairs={{0,16},{16,32},{32,48},{48,64},{64,80},{80,96},{96,112},{112,128},... | collective-permute-start | bytes 1572872 | tf_op jit(solution)/shard_map/ppermute | solution.py:27
  57.2 1.8 %copy.69 = pred[1536,512]{1,0:T(8,128)(4,1)} copy(pred[1536,512]{0,1:T(8,128)(4,1)S(1)} %bitcast.122) | data formatting | bytes 1572864 | tf_op jit(solution)/shard_map/jit(_where)/broadcast_in_dim | solution.py:89
  59.0 2.7 %collective-permute-start.5 = (f32[2,2,512]{2,1,0:T(2,128)S(1)}, f32[2,2,512]{2,1,0:T(2,128)S(1)}, u32[]{:S(2)}, u32[]{:S(2)}) collective-permute-start(f32[2,2,512]{2,1,0:T(2,128)S(1)} %pad_maximum_fusion.5), channel_id=1, source_target_pairs={{16,0},{32,16},{48,32},{64,48},{80,64},{96,80},{112,96},{128,112},... | collective-permute-start | bytes 24584 | tf_op jit(solution)/shard_map/ppermute | solution.py:28
  61.7 3.0 %collective-permute-start.4 = (f32[2,2,512]{2,1,0:T(2,128)S(1)}, f32[2,2,512]{2,1,0:T(2,128)S(1)}, u32[]{:S(2)}, u32[]{:S(2)}) collective-permute-start(f32[2,2,512]{2,1,0:T(2,128)S(1)} %pad_maximum_fusion.5), channel_id=1, source_target_pairs={{0,16},{16,32},{32,48},{48,64},{64,80},{80,96},{96,112},{112,128},... | collective-permute-start | bytes 24584 | tf_op jit(solution)/shard_map/ppermute | solution.py:27
  64.7 5.7 %fusion = bf16[5120,256]{0,1:T(8,128)(2,1)} fusion(bf16[512,256]{0,1:T(8,128)(2,1)} %bitcast.128, bf16[512,5120]{1,0:T(8,128)(2,1)} %param.10), kind=kOutput, calls=%fused_computation.8 | convolution fusion | flops 1343488000 | bytes 8126464 | tf_op jit(solution)/shard_map/dot_general | solution.py:167
  70.4 4.4 %copy.74 = bf16[5120,256]{1,0:T(8,128)(2,1)} copy(bf16[5120,256]{0,1:T(8,128)(2,1)} %fusion) | data formatting | bytes 5242880 | tf_op jit(solution)/shard_map/convert_element_type | solution.py:169
  74.8 10.2 %all-to-all-start = ((bf16[16,320,256]{2,1,0:T(8,128)(2,1)}), bf16[16,320,256]{2,1,0:T(8,128)(2,1)}, u32[]{:S(2)}, u32[]{:S(2)}) async-start(bf16[16,320,256]{2,1,0:T(8,128)(2,1)} %bitcast.118), calls=%async_computation.2 | async-start | bytes 5242880 | tf_op jit(solution)/shard_map/all_to_all | solution.py:55
  85.0 2.6 %pad_maximum_fusion.1 = bf16[2,1536,256]{1,2,0:T(8,128)(2,1)} fusion(bf16[2,512,256]{1,2,0:T(8,128)(2,1)} %collective-permute-done.3, bf16[1,512,256]{1,2,0:T(8,128)(2,1)} %bitcast.131, bf16[1,512,256]{1,2,0:T(8,128)(2,1)} %bitcast.134, bf16[2,512,256]{1,2,0:T(8,128)(2,1)} %collective-permute-done.2), kind=kLoop, calls=%fused_computation.17 | loop fusion | flops 6291456 | bytes 3145728 | tf_op jit(solution)/shard_map/concatenate | solution.py:29
  87.7 5.8 %fusion.19 = bf16[2,128,512]{2,1,0:T(8,128)(2,1)} fusion(bf16[1536,2,128]{0,2,1:T(8,128)(2,1)} %bitcast.140, f32[2,512,1536]{1,2,0:T(8,128)} %copy-done.1, bf16[512,2,128]{0,2,1:T(8,128)(2,1)} %bitcast.132, bf16[1536,2,128]{0,2,1:T(8,128)(2,1)S(1)} %bitcast.124, f32[2,512]{1,0:T(2,128)S(1)} %bitcast.149, f32[2,512]{1,0:T(2,128)S(1)} %log_add_fusion), kind=kOutput, calls=%fused_computation.27 | convolution fusion | flops 811859968 | bytes 8396800 | tf_op jit(solution)/shard_map/hts,shd->thd/dot_general | solution.py:130
  93.5 2.4 %fusion.45 = (bf16[1,1536,256]{1,2,0:T(8,128)(2,1)}, bf16[1,1536,256]{1,2,0:T(8,128)(2,1)S(1)}) fusion(bf16[2,1536,256]{1,2,0:T(8,128)(2,1)} %pad_maximum_fusion.1), kind=kLoop, calls=%fused_computation.75 | loop fusion | bytes 3145728 | tf_op jit(solution)/shard_map/slice | solution.py:139
  95.8 4.6 %fusion.33 = f32[2,1536,512]{2,1,0:T(8,128)} fusion(bf16[1536,2,128]{0,2,1:T(8,128)(2,1)S(1)} %bitcast.125, bf16[512,256]{1,0:T(8,128)(2,1)} %param.7), kind=kOutput, calls=%fused_computation.43 | convolution fusion | flops 402653184 | bytes 7340032 | tf_op jit(solution)/shard_map/thd,shd->hts/dot_general | solution.py:78
  100.5 1.8 %copy.79 = bf16[512,256]{1,0:T(8,128)(2,1)} copy(bf16[512,256]{0,1:T(8,128)(2,1)} %bitcast.129) | data formatting | bytes 524288
  102.3 1.8 %copy.80 = bf16[512,256]{1,0:T(8,128)(2,1)} copy(bf16[512,256]{0,1:T(8,128)(2,1)} %bitcast.144) | data formatting | bytes 524288
  104.1 7.1 %fusion.15 = bf16[2,128,512]{2,1,0:T(8,128)(2,1)} fusion(bf16[1536,2,128]{0,2,1:T(8,128)(2,1)S(1)} %bitcast.126, f32[2,1536,512]{2,1,0:T(8,128)} %fusion.33, bf16[1536,2,128]{0,2,1:T(8,128)(2,1)} %bitcast.141, f32[2,1536]{1,0:T(2,128)S(1)} %get-tuple-element.33, f32[2,1536]{1,0:T(2,128)S(1)} %get-tuple-element.32, pred[1536,512]{1,0:T(8,128)(4,1)} %copy.69, ...), kind=kOutput, calls=%fused_computation.25 | convolution fusion | flops 815005696 | bytes 9199616 | tf_op jit(solution)/shard_map/hts,thd->shd/dot_general | solution.py:154
  111.1 7.3 %reduce-scatter.3.cloned.1.call-done = bf16[2,512,320]{1,2,0:T(8,128)(2,1)} async-done(((bf16[16,512,320]{1,2,0:T(8,128)(2,1)}), bf16[2,512,320]{1,2,0:T(8,128)(2,1)}) %reduce-scatter.3.cloned.1.call-update) | async-done | bytes 655376 | tf_op jit(solution)/shard_map/reduce_scatter | solution.py:38
  118.5 5.2 %fusion.16 = bf16[2,128,512]{2,1,0:T(8,128)(2,1)S(1)} fusion(bf16[1536,2,128]{0,2,1:T(8,128)(2,1)} %bitcast.142, f32[2,1536,512]{2,1,0:T(8,128)} %fusion.33, f32[2,1536]{1,0:T(2,128)S(1)} %get-tuple-element.32, pred[1536,512]{1,0:T(8,128)(4,1)} %copy.69), kind=kOutput, calls=%fused_computation.26 | convolution fusion | flops 409075712 | bytes 8138752 | tf_op jit(solution)/shard_map/hts,thd->shd/dot_general | solution.py:159
  125.4 2.1 %convert_reduce_fusion = f32[320,256]{1,0:T(8,128)S(1)} fusion(bf16[16,320,256]{2,1,0:T(8,128)(2,1)} %all-to-all-done), kind=kLoop, calls=%fused_computation.10 | loop fusion | flops 2539520 | bytes 2949120 | tf_op jit(solution)/shard_map/reduce_sum | solution.py:56
  128.1 1.5 fusion.24
  129.6 1.9 %fusion.12 = f32[2,1,320,320]{3,2,1,0:T(8,128)} fusion(f32[2]{0:T(128)S(1)} %broadcast_add_fusion, f32[320,256]{1,0:T(8,128)S(1)} %convert_reduce_fusion), kind=kOutput, calls=%fused_computation.22 | convolution fusion | flops 314982400 | bytes 1146888 | tf_op jit(solution)/shard_map/bche,bdhe->hbcd/dot_general | solution.py:178
  131.5 11.3 %reduce-scatter.5.cloned.1.call-done = bf16[1,512,320]{1,2,0:T(8,128)(2,1)} async-done(((bf16[2,512,320]{1,2,0:T(8,128)(2,1)}), bf16[1,512,320]{1,2,0:T(8,128)(2,1)}) %reduce-scatter.5.cloned.1.call-update) | async-done | bytes 327696 | tf_op jit(solution)/shard_map/reduce_scatter | solution.py:38
  (76 shorter events, 10.9 us)
Async XLA Ops:
  7.2 14.2 %copy-start = (bf16[256,5120]{1,0:T(8,128)(2,1)S(1)}, bf16[256,5120]{1,0:T(8,128)(2,1)}, u32[]{:S(2)}) copy-start(bf16[256,5120]{1,0:T(8,128)(2,1)} %param.9) | copy-start | bytes 7864324
  7.2 111.2 %reduce-scatter.3.cloned.1.call-start = ((), (), s32[]{:S(2)}) async-start(), calls=%async_computation.3 | async-start | bytes 5898240 | tf_op jit(solution)/shard_map/reduce_scatter | solution.py:38
  8.5 10.7 %copy-start.7 = (bf16[512,256]{0,1:T(8,128)(2,1)}, bf16[512,256]{0,1:T(8,128)(2,1)S(1)}, u32[]{:S(2)}) copy-start(bf16[512,256]{0,1:T(8,128)(2,1)S(1)} %copy.56) | copy-start | bytes 786436
  9.7 9.5 %copy-start.9 = (bf16[512,256]{0,1:T(8,128)(2,1)}, bf16[512,256]{0,1:T(8,128)(2,1)S(1)}, u32[]{:S(2)}) copy-start(bf16[512,256]{0,1:T(8,128)(2,1)S(1)} %copy.57) | copy-start | bytes 786436
  10.6 15.0 %collective-permute-start.1 = (bf16[2,512,256]{1,2,0:T(8,128)(2,1)}, bf16[2,512,256]{1,2,0:T(8,128)(2,1)}, u32[]{:S(2)}, u32[]{:S(2)}) collective-permute-start(bf16[2,512,256]{1,2,0:T(8,128)(2,1)} %pad_maximum_fusion.2), channel_id=1, source_target_pairs={{16,0},{32,16},{48,32},{64,48},{80,64},{96,80},{112,96},{128,112},... | collective-permute-start | bytes 1572872 | tf_op jit(solution)/shard_map/ppermute | solution.py:28
  15.7 9.9 %collective-permute-start = (bf16[2,512,256]{1,2,0:T(8,128)(2,1)}, bf16[2,512,256]{1,2,0:T(8,128)(2,1)}, u32[]{:S(2)}, u32[]{:S(2)}) collective-permute-start(bf16[2,512,256]{1,2,0:T(8,128)(2,1)} %pad_maximum_fusion.2), channel_id=1, source_target_pairs={{0,16},{16,32},{32,48},{48,64},{64,80},{80,96},{96,112},{112,128},... | collective-permute-start | bytes 1572872 | tf_op jit(solution)/shard_map/ppermute | solution.py:27
  21.4 4.2 %copy-start.8 = (bf16[512,256]{0,1:T(8,128)(2,1)S(1)}, bf16[512,256]{0,1:T(8,128)(2,1)}, u32[]{:S(2)}) copy-start(bf16[512,256]{0,1:T(8,128)(2,1)} %copy-done.7) | copy-start | bytes 786436
  21.4 4.2 %copy-start.10 = (bf16[512,256]{0,1:T(8,128)(2,1)S(1)}, bf16[512,256]{0,1:T(8,128)(2,1)}, u32[]{:S(2)}) copy-start(bf16[512,256]{0,1:T(8,128)(2,1)} %copy-done.9) | copy-start | bytes 786436
  25.5 24.0 %copy-start.5 = (bf16[512,256]{0,1:T(8,128)(2,1)}, bf16[512,256]{0,1:T(8,128)(2,1)S(1)}, u32[]{:S(2)}) copy-start(bf16[512,256]{0,1:T(8,128)(2,1)S(1)} %convolution_convert_fusion.2) | copy-start | bytes 786436
  25.5 1.6 %copy-start.11 = (pred[512,1536]{0,1:T(8,128)(4,1)S(1)}, pred[512,1536]{0,1:T(8,128)(4,1)}, u32[]{:S(2)}) copy-start(pred[512,1536]{0,1:T(8,128)(4,1)} %copy.58) | copy-start | bytes 2359300
  25.5 1.6 %copy-start.13 = (bf16[512,256]{1,0:T(8,128)(2,1)S(1)}, bf16[512,256]{1,0:T(8,128)(2,1)}, u32[]{:S(2)}) copy-start(bf16[512,256]{1,0:T(8,128)(2,1)} %param.6) | copy-start | bytes 786436
  27.1 1.6 %copy-start.12 = (bf16[1,1536,256]{1,2,0:T(8,128)(2,1)}, bf16[1,1536,256]{1,2,0:T(8,128)(2,1)S(1)}, u32[]{:S(2)}) copy-start(bf16[1,1536,256]{1,2,0:T(8,128)(2,1)S(1)} %get-tuple-element.30) | copy-start | bytes 2359300
  27.2 2.5 %copy-start.2 = (bf16[1,1536,256]{1,2,0:T(8,128)(2,1)}, bf16[1,1536,256]{1,2,0:T(8,128)(2,1)S(1)}, u32[]{:S(2)}) copy-start(bf16[1,1536,256]{1,2,0:T(8,128)(2,1)S(1)} %get-tuple-element.31) | copy-start | bytes 2359300
  28.7 2.6 %copy-start.1 = (f32[2,512,1536]{1,2,0:T(8,128)}, f32[2,512,1536]{1,2,0:T(8,128)S(1)}, u32[]{:S(2)}) copy-start(f32[2,512,1536]{1,2,0:T(8,128)S(1)} %get-tuple-element.35) | copy-start | bytes 18874372
  31.4 0.7 copy-start.4
  49.4 6.7 %copy-start.15 = (s32[32,5]{0,1:T(8,128)S(1)}, s32[32,5]{0,1:T(8,128)}, u32[]{:S(2)}) copy-start(s32[32,5]{0,1:T(8,128)} %param.11) | copy-start | bytes 1924
  49.5 7.2 %copy-start.6 = (bf16[512,256]{0,1:T(8,128)(2,1)}, bf16[512,256]{0,1:T(8,128)(2,1)S(1)}, u32[]{:S(2)}) copy-start(bf16[512,256]{0,1:T(8,128)(2,1)S(1)} %copy.68) | copy-start | bytes 786436
  50.4 34.6 %collective-permute-start.3 = (bf16[2,512,256]{1,2,0:T(8,128)(2,1)}, bf16[2,512,256]{1,2,0:T(8,128)(2,1)}, u32[]{:S(2)}, u32[]{:S(2)}) collective-permute-start(bf16[2,512,256]{1,2,0:T(8,128)(2,1)} %pad_maximum_fusion.3), channel_id=1, source_target_pairs={{16,0},{32,16},{48,32},{64,48},{80,64},{96,80},{112,96},{128,112},... | collective-permute-start | bytes 1572872 | tf_op jit(solution)/shard_map/ppermute | solution.py:28
  53.6 31.4 %collective-permute-start.2 = (bf16[2,512,256]{1,2,0:T(8,128)(2,1)}, bf16[2,512,256]{1,2,0:T(8,128)(2,1)}, u32[]{:S(2)}, u32[]{:S(2)}) collective-permute-start(bf16[2,512,256]{1,2,0:T(8,128)(2,1)} %pad_maximum_fusion.3), channel_id=1, source_target_pairs={{0,16},{16,32},{32,48},{48,64},{64,80},{80,96},{96,112},{112,128},... | collective-permute-start | bytes 1572872 | tf_op jit(solution)/shard_map/ppermute | solution.py:27
  59.0 45.1 %collective-permute-start.5 = (f32[2,2,512]{2,1,0:T(2,128)S(1)}, f32[2,2,512]{2,1,0:T(2,128)S(1)}, u32[]{:S(2)}, u32[]{:S(2)}) collective-permute-start(f32[2,2,512]{2,1,0:T(2,128)S(1)} %pad_maximum_fusion.5), channel_id=1, source_target_pairs={{16,0},{32,16},{48,32},{64,48},{80,64},{96,80},{112,96},{128,112},... | collective-permute-start | bytes 24584 | tf_op jit(solution)/shard_map/ppermute | solution.py:28
  61.7 42.3 %collective-permute-start.4 = (f32[2,2,512]{2,1,0:T(2,128)S(1)}, f32[2,2,512]{2,1,0:T(2,128)S(1)}, u32[]{:S(2)}, u32[]{:S(2)}) collective-permute-start(f32[2,2,512]{2,1,0:T(2,128)S(1)} %pad_maximum_fusion.5), channel_id=1, source_target_pairs={{0,16},{16,32},{32,48},{48,64},{64,80},{80,96},{96,112},{112,128},... | collective-permute-start | bytes 24584 | tf_op jit(solution)/shard_map/ppermute | solution.py:27
  74.8 12.9 %copy-start.3 = (bf16[1,1536,256]{1,2,0:T(8,128)(2,1)S(1)}, bf16[1,1536,256]{1,2,0:T(8,128)(2,1)}, u32[]{:S(2)}) copy-start(bf16[1,1536,256]{1,2,0:T(8,128)(2,1)} %copy-done.2) | copy-start | bytes 2359300
  74.8 50.6 %all-to-all-start = ((bf16[16,320,256]{2,1,0:T(8,128)(2,1)}), bf16[16,320,256]{2,1,0:T(8,128)(2,1)}, u32[]{:S(2)}, u32[]{:S(2)}) async-start(bf16[16,320,256]{2,1,0:T(8,128)(2,1)} %bitcast.118), calls=%async_computation.2 | async-start | bytes 5242880 | tf_op jit(solution)/shard_map/all_to_all | solution.py:55
  85.0 57.8 %reduce-scatter.5.cloned.1.call-start = ((), (), s32[]{:S(2)}) async-start(), calls=%async_computation.4 | async-start | bytes 983040 | tf_op jit(solution)/shard_map/reduce_scatter | solution.py:38
  118.5 6.1 %copy-start.14 = (bf16[2,128,512]{2,1,0:T(8,128)(2,1)S(1)}, bf16[2,128,512]{2,1,0:T(8,128)(2,1)}, u32[]{:S(2)}) copy-start(bf16[2,128,512]{2,1,0:T(8,128)(2,1)} %fusion.15) | copy-start | bytes 786436
Sparse Core Ops, SparseCore 0:
  49.5 68.8 reduce-scatter.2
  121.5 21.1 reduce-scatter.4
where the time goes:
time: 150 us
  matrix products  42.5 us (28%)
  local copies, waits for them, and re-layouts  34.6 us (23%)
  starting transfers between devices  28.5 us (19%)
  waiting for transfers between devices  18.6 us (12%)
  between operations  14.5 us (10%)
  other arithmetic  10.9 us (7%)
    reduce_scatter x2, waiting for transfers between devices, sum_in_order(): blocks = lax.psum_scatter(blocks, axes[k], scatter_dimension=0, tiled=True)  18.5 us
    ppermute x3, starting transfers between devices, padded(): after = lax.ppermute(initial, axis, down)  11 us
    all_to_all x1, starting transfers between devices, sent_and_summed(): lax.all_to_all(blocks, axis, split_axis=0, concat_axis=0, tiled=True)  10.2 us
    unnamed x41, local copies, waits for them, and re-layouts  9.91 us
    convert_element_type x1, local copies, waits for them, and re-layouts, local(): partial_value.astype(jnp.bfloat16)  7.98 us
    ppermute x3, starting transfers between devices, padded(): before = lax.ppermute(last, axis, up)  7.31 us
    dot_general x1, matrix products, local(): jnp.einsum('hts,thd->shd', grad_scores_near, queries_ext, preferred_eleme...  7.06 us
    dot_general x2, matrix products, masked_scores(): jnp.einsum('thd,shd->hts', queries, key_rows, preferred_element_type=jnp....  6.13 us
  transfers between devices with their start and end apart: 9, of which 2 were waited for; matrix products, arithmetic and copies ran while one was open for 41% of the time, Pallas kernels for 0%

commit v1 on v0

v1 whole, which is shorter than its diff:
```python
import math

import jax
import jax.numpy as jnp
from jax import lax
from jax.experimental import pallas as pl
from jax.experimental.pallas import tpu as pltpu
from jax.sharding import Mesh
from jax.sharding import PartitionSpec as P


D = 5120
HD = 128
TILE = 256
TILES_DEV = 2
CB = 320
TOK = 512
NT = 32
WIN = 5
GROUP = 2 * CB
GROUPS = D // GROUP
FRAME = ("xlo", "y", "core")
HEAD = ("xhi", "zq", "zp")
NEAR = ("xhi", "zp")

epsilon = 1e-06
SCALING = 1.0 / math.sqrt(HD)
LOG2E = 1.0 / math.log(2.0)
NEG = -1e30
VMEM_BYTES = 16 * 1024 * 1024
PLANE = 8


def dot_nt(a, b, precision=None):
    return lax.dot_general(
        a, b, (((1,), (1,)), ((), ())), precision=precision, preferred_element_type=jnp.float32
    )


def dot_nn(a, b):
    return jnp.dot(a, b, preferred_element_type=jnp.float32)


def eye(n):
    rows = lax.broadcasted_iota(jnp.int32, (n, n), 0)
    cols = lax.broadcasted_iota(jnp.int32, (n, n), 1)
    return (rows == cols).astype(jnp.float32).astype(jnp.bfloat16)


def allowed(ids, mask, i, j):
    tile = ids[0] * TILES_DEV + i
    key_tile = tile + (j - 2)
    return (mask[j, tile] == 1) & (key_tile >= 0) & (key_tile < NT)


def extend(pieces, target):
    for place, piece in enumerate(pieces):
        target[place * TOK : (place + 1) * TOK] = piece[...]


def forward_kernel(ids, mask, q, kl, k, kr, vl, v, vr, att, copy, stat, kx, vx):
    extend((kl, k, kr), kx)
    extend((vl, v, vr), vx)
    first_lane = lax.broadcasted_iota(jnp.int32, (8, HD), 1) == 0
    pick = jnp.where(first_lane, jnp.float32(1), jnp.float32(0))
    for i in range(TILES_DEV):
        rows = slice(i * TILE, (i + 1) * TILE)
        parts = []
        for j in range(WIN):
            keys = kx[(i + j) * TILE : (i + j + 1) * TILE]
            part = dot_nt(q[rows], keys) * jnp.float32(SCALING * LOG2E)
            parts.append(jnp.where(allowed(ids, mask, i, j), part, jnp.float32(NEG)))
        peak = parts[0]
        for part in parts[1:]:
            peak = jnp.maximum(peak, part)
        peak = jnp.max(peak, axis=1, keepdims=True)
        out = jnp.zeros((TILE, HD), jnp.float32)
        total = jnp.zeros((TILE, TILE), jnp.float32)
        for j in range(WIN):
            weight = jnp.exp2(parts[j] - peak)
            total = total + weight
            values = vx[(i + j) * TILE : (i + j + 1) * TILE]
            out = out + dot_nn(weight.astype(jnp.bfloat16), values)
        total = jnp.sum(total, axis=1, keepdims=True)
        att[rows] = (out / total).astype(jnp.bfloat16)
        copy[rows] = att[rows]
        log_total = peak + jnp.log(total) * jnp.float32(LOG2E)
        spread = jnp.broadcast_to(log_total, (TILE, HD))
        stat[0, :, rows] = dot_nt(pick, spread, lax.Precision.HIGHEST)


def backward_kernel(
    ids, mask, q, kl, k, kr, vl, v, vr, g, att, stat, dq, dl, do, dr, kx, vx, dsx, kt
):
    extend((kl, k, kr), kx)
    extend((vl, v, vr), vx)
    unit = eye(HD)
    for e in range(6):
        block = slice(e * TILE, (e + 1) * TILE)
        kt[:, block] = dot_nt(unit, kx[block]).astype(jnp.bfloat16)
    products = g[...].astype(jnp.float32) * att[...].astype(jnp.float32)
    ones = jnp.ones((8, HD), jnp.float32)
    deltas = dot_nt(ones, products, lax.Precision.HIGHEST)[0:1]
    totals = stat[0, 0:1, :]
    for e in range(6):
        keys = kx[e * TILE : (e + 1) * TILE]
        values = vx[e * TILE : (e + 1) * TILE]
        tiles = [i for i in range(TILES_DEV) if 0 <= e - i < WIN]
        dk = jnp.zeros((TILE, HD), jnp.float32)
        dv = jnp.zeros((TILE, HD), jnp.float32)
        for i in tiles:
            rows = slice(i * TILE, (i + 1) * TILE)
            ok = allowed(ids, mask, i, e - i)
            level = jnp.where(ok, totals[:, rows], jnp.float32(-NEG))
            scores = dot_nt(keys, q[rows]) * jnp.float32(SCALING * LOG2E)
            weight = jnp.exp2(scores - level)
            probs = dot_nt(values, g[rows])
            ds = (weight * (probs - deltas[:, rows])).astype(jnp.bfloat16)
            dsx[e * TILE : (e + 1) * TILE, rows] = ds
            dk = dk + dot_nn(ds, q[rows])
            dv = dv + dot_nn(weight.astype(jnp.bfloat16), g[rows])
        dk = dk * jnp.float32(SCALING)
        part = (e % 2) * TILE
        target = (dl, do, dr)[e // 2]
        target[part : part + TILE] = dk.astype(target.dtype)
        target[TOK + part : TOK + part + TILE] = dv.astype(target.dtype)
    wide = eye(TILE)
    for i in range(TILES_DEV):
        rows = slice(i * TILE, (i + 1) * TILE)
        window = slice(i * TILE, (i + WIN) * TILE)
        turned = dot_nn(kt[:, window], dsx[window, rows]) * jnp.float32(SCALING)
        dq[rows] = dot_nt(wide, turned.astype(jnp.bfloat16)).astype(jnp.bfloat16)


def attention_specs():
    narrow = pl.BlockSpec((TOK, HD), lambda h, *_: (0, h))
    second = pl.BlockSpec((TOK, HD), lambda h, *_: (0, 2 + h))
    double = pl.BlockSpec((2 * TOK, HD), lambda h, *_: (0, h))
    stat = pl.BlockSpec((1, 8, TOK), lambda h, *_: (h, 0, 0))
    pieces = [narrow, narrow, narrow, second, narrow, second]
    return narrow, double, stat, pieces


def attention_forward(ids, mask, q, keys, values):
    narrow, _, stat, pieces = attention_specs()
    return pl.pallas_call(
        forward_kernel,
        grid_spec=pltpu.PrefetchScalarGridSpec(
            num_scalar_prefetch=2,
            grid=(2,),
            in_specs=[narrow] + pieces,
            out_specs=[narrow, narrow, stat],
            scratch_shapes=[pltpu.VMEM((3 * TOK, HD), jnp.bfloat16)] * 2,
        ),
        out_shape=[
            jax.ShapeDtypeStruct((TOK, 2 * HD), jnp.bfloat16),
            jax.ShapeDtypeStruct((TOK, 2 * HD), jnp.bfloat16),
            jax.ShapeDtypeStruct((2, 8, TOK), jnp.float32),
        ],
        cost_estimate=pl.CostEstimate(
            flops=700_000_000, bytes_accessed=2_400_000, transcendentals=1_300_000
        ),
        compiler_params=pltpu.CompilerParams(vmem_limit_bytes=VMEM_BYTES),
        name="attention_forward",
    )(ids, mask, q, *keys, *values)


def attention_backward(ids, mask, q, keys, values, g, att, stats):
    narrow, double, stat, pieces = attention_specs()
    return pl.pallas_call(
        backward_kernel,
        grid_spec=pltpu.PrefetchScalarGridSpec(
            num_scalar_prefetch=2,
            grid=(2,),
            in_specs=[narrow] + pieces + [narrow, narrow, stat],
            out_specs=[narrow, double, double, double],
            scratch_shapes=[pltpu.VMEM((3 * TOK, HD), jnp.bfloat16)] * 2
            + [
                pltpu.VMEM((3 * TOK, TOK), jnp.bfloat16),
                pltpu.VMEM((HD, 3 * TOK), jnp.bfloat16),
            ],
        ),
        out_shape=[
            jax.ShapeDtypeStruct((TOK, 2 * HD), jnp.bfloat16),
            jax.ShapeDtypeStruct((2 * TOK, 2 * HD), jnp.bfloat16),
            jax.ShapeDtypeStruct((2 * TOK, 2 * HD), jnp.float32),
            jax.ShapeDtypeStruct((2 * TOK, 2 * HD), jnp.bfloat16),
        ],
        cost_estimate=pl.CostEstimate(
            flops=1_800_000_000, bytes_accessed=5_000_000, transcendentals=1_300_000
        ),
        compiler_params=pltpu.CompilerParams(vmem_limit_bytes=VMEM_BYTES),
        name="attention_backward",
    )(ids, mask, q, *keys, *values, g, att, stats)


def pack_kernel(ids, w, out):
    unit = eye(HD)
    for t in range(GROUP // HD):
        turned = dot_nt(unit, w[:, t * HD : (t + 1) * HD]).astype(jnp.bfloat16)
        for half in range(2):
            row = t * HD + half * 64
            out[0, row // CB, 0, row % CB : row % CB + 64] = turned[half * 64 : half * 64 + 64]


def pack_weights(ids, w):
    return pl.pallas_call(
        pack_kernel,
        grid_spec=pltpu.PrefetchScalarGridSpec(
            num_scalar_prefetch=1,
            grid=(GROUPS,),
            in_specs=[pl.BlockSpec((HD, GROUP), lambda s, ids: (ids[1], s))],
            out_specs=pl.BlockSpec((1, 2, 1, CB, HD), lambda s, ids: (s // 4, 0, s % 4, 0, 0)),
        ),
        out_shape=jax.ShapeDtypeStruct((2, 2, 4, CB, HD), jnp.bfloat16),
        cost_estimate=pl.CostEstimate(
            flops=170_000_000, bytes_accessed=2_600_000, transcendentals=0
        ),
        compiler_params=pltpu.CompilerParams(vmem_limit_bytes=VMEM_BYTES),
        name="pack_weights",
    )(ids, w)


def project_kernel(ids, mine, other, a0, a1, a2, a3, o0, o1, o2, o3, wide):
    core = ids[1]
    here = ids[2]
    far = ids[3]
    for p, out in ((2, o2), (1, o1), (3, o3), (0, o0)):
        total = jnp.zeros((CB, TOK), jnp.float32)
        for r, a in enumerate((a0, a1, a2, a3)):
            source = here ^ r
            block = far ^ p
            wide[p, r, :, pl.ds(pl.multiple_of(core * HD, HD), HD)] = mine[source, block]
            wide[p, r, :, pl.ds(pl.multiple_of((1 - core) * HD, HD), HD)] = other[source, block]
            total = total + dot_nt(wide[p, r], a[...])
        out[...] = total.astype(jnp.bfloat16)


def project(ids, mine, other, gathered):
    whole = pl.BlockSpec(memory_space=pltpu.VMEM)
    return pl.pallas_call(
        project_kernel,
        in_specs=[pl.BlockSpec(memory_space=pltpu.SMEM)] + [whole] * 6,
        out_specs=[whole] * 4,
        scratch_shapes=[pltpu.VMEM((4, 4, CB, 2 * HD), jnp.bfloat16)],
        out_shape=[jax.ShapeDtypeStruct((CB, TOK), jnp.bfloat16)] * 4,
        cost_estimate=pl.CostEstimate(
            flops=1_340_000_000, bytes_accessed=5_000_000, transcendentals=0
        ),
        compiler_params=pltpu.CompilerParams(vmem_limit_bytes=VMEM_BYTES),
        name="project",
    )(ids, mine, other, *gathered)


def upstream_kernel(ids, up, w, att, g, mine, other, turned, pair, acc):
    core = ids[1]
    step = pl.program_id(0)

    @pl.when(step == 0)
    def _():
        turned[...] = dot_nt(eye(2 * HD), att[...]).astype(jnp.bfloat16)
        acc[...] = jnp.zeros_like(acc)

    acc[...] += dot_nt(up[...], w[...])
    grad = dot_nn(turned[...], up[...]).astype(jnp.bfloat16)
    unit = eye(HD)
    for t in range(GROUP // HD):
        block = slice(t * HD, (t + 1) * HD)
        pair[block] = dot_nt(unit, grad[:, block]).astype(jnp.bfloat16)
    mine[0] = pair[pl.ds(pl.multiple_of(core * CB, CB), CB)]
    other[0] = pair[pl.ds(pl.multiple_of((1 - core) * CB, CB), CB)]

    @pl.when(step == GROUPS - 1)
    def _():
        g[...] = acc[...].astype(jnp.bfloat16)


def use_upstream(ids, up, w, att):
    part = pl.BlockSpec((1, CB, 2 * HD), lambda s, ids: (s ^ ids[4], 0, 0))
    whole = pl.BlockSpec((TOK, 2 * HD), lambda s, ids: (0, 0))
    return pl.pallas_call(
        upstream_kernel,
        grid_spec=pltpu.PrefetchScalarGridSpec(
            num_scalar_prefetch=1,
            grid=(GROUPS,),
            in_specs=[
                pl.BlockSpec((TOK, GROUP), lambda s, ids: (0, s)),
                pl.BlockSpec((2 * HD, GROUP), lambda s, ids: (0, s)),
                whole,
            ],
            out_specs=[whole, part, part],
            scratch_shapes=[
                pltpu.VMEM((2 * HD, TOK), jnp.bfloat16),
                pltpu.VMEM((GROUP, 2 * HD), jnp.bfloat16),
                pltpu.VMEM((TOK, 2 * HD), jnp.float32),
            ],
        ),
        out_shape=[jax.ShapeDtypeStruct((TOK, 2 * HD), jnp.bfloat16)]
        + [jax.ShapeDtypeStruct((GROUPS, CB, 2 * HD), jnp.bfloat16)] * 2,
        cost_estimate=pl.CostEstimate(
            flops=3_000_000_000, bytes_accessed=11_000_000, transcendentals=0
        ),
        compiler_params=pltpu.CompilerParams(vmem_limit_bytes=VMEM_BYTES),
        name="use_upstream",
    )(ids, up, w, att)


def merge_kernel(mine, near, *outs):
    for p, out in enumerate(outs):
        total = mine[p].astype(jnp.float32) + near[p].astype(jnp.float32)
        out[...] = total.astype(jnp.bfloat16)


def merge(mine, near):
    whole = pl.BlockSpec(memory_space=pltpu.VMEM)
    return pl.pallas_call(
        merge_kernel,
        in_specs=[whole] * 2,
        out_specs=[whole] * PLANE,
        out_shape=[jax.ShapeDtypeStruct((CB, 2 * HD), jnp.bfloat16)] * PLANE,
        cost_estimate=pl.CostEstimate(
            flops=1_000_000, bytes_accessed=4_000_000, transcendentals=0
        ),
        compiler_params=pltpu.CompilerParams(vmem_limit_bytes=VMEM_BYTES),
        name="merge",
    )(mine, near)


def gram_kernel(*refs):
    parts, (left, right) = refs[:PLANE], refs[PLANE:]
    highest = lax.Precision.HIGHEST
    total = parts[0][...].astype(jnp.float32)
    for part in parts[1:]:
        total = total + part[...].astype(jnp.float32)
    for h in range(2):
        block = total[:, h * HD : (h + 1) * HD]
        squares = jnp.sum(block * block, axis=0, keepdims=True)
        trace = jnp.sum(squares, axis=1, keepdims=True)
        inverse = 1.0 / (trace + epsilon)
        turned = block.T
        left[h, 0] = dot_nt(turned, turned, highest) * (inverse * HD)
        right[h, 0] = dot_nt(block, block, highest) * (inverse * CB)


def gram(parts):
    whole = pl.BlockSpec(memory_space=pltpu.VMEM)
    return pl.pallas_call(
        gram_kernel,
        in_specs=[whole] * PLANE,
        out_specs=[whole] * 2,
        out_shape=[
            jax.ShapeDtypeStruct((2, 1, HD, HD), jnp.float32),
            jax.ShapeDtypeStruct((2, 1, CB, CB), jnp.float32),
        ],
        cost_estimate=pl.CostEstimate(
            flops=400_000_000, bytes_accessed=2_000_000, transcendentals=0
        ),
        compiler_params=pltpu.CompilerParams(vmem_limit_bytes=VMEM_BYTES),
        name="gram",
    )(*parts)


def pair_kernel(k, v, out, sems):
    first = pltpu.make_async_copy(k, out.at[:, 0 : 2 * HD], sems.at[0])
    second = pltpu.make_async_copy(v, out.at[:, 2 * HD : 4 * HD], sems.at[1])
    first.start()
    second.start()
    first.wait()
    second.wait()


def pair_up(k, v):
    return pl.pallas_call(
        pair_kernel,
        in_specs=[pl.BlockSpec(memory_space=pl.ANY)] * 2,
        out_specs=pl.BlockSpec(memory_space=pltpu.VMEM),
        scratch_shapes=[pltpu.SemaphoreType.DMA((2,))],
        out_shape=jax.ShapeDtypeStruct((TOK, 4 * HD), jnp.bfloat16),
        cost_estimate=pl.CostEstimate(flops=0, bytes_accessed=1_000_000, transcendentals=0),
        compiler_params=pltpu.CompilerParams(vmem_limit_bytes=VMEM_BYTES),
        name="pair_up",
    )(k, v)


def in_hbm(x):
    return pltpu.with_memory_space_constraint(x, pltpu.HBM)


def local(query_states, key_states, value_states, out_weight, upstream, tile_mask):
    frame = lax.axis_index(FRAME).astype(jnp.int32)
    core = lax.axis_index("core").astype(jnp.int32)
    here = lax.axis_index(NEAR).astype(jnp.int32)
    far = lax.axis_index("zq").astype(jnp.int32)
    plane = lax.axis_index(("xlo", "y")).astype(jnp.int32)
    ids = jnp.stack([frame, core, here, far, plane])
    frames = lax.axis_size(FRAME)
    up = [(i, i + 1) for i in range(frames - 1)]
    down = [(j, i) for i, j in up]
    cores = [(0, 1), (1, 0)]
    mask = tile_mask.T
    query_states = in_hbm(query_states)
    key_states = in_hbm(key_states)
    value_states = in_hbm(value_states)
    out_weight = in_hbm(out_weight)
    upstream = in_hbm(upstream)

    both = pair_up(key_states, value_states)
    before = lax.ppermute(both, FRAME, up)
    after = lax.ppermute(both, FRAME, down)
    keys = (before, key_states, after)
    values = (before, value_states, after)

    strips = pack_weights(ids, out_weight).reshape(4, 4, CB, HD)
    strips_mine = lax.all_to_all(strips, NEAR, 0, 0, tiled=True)
    strips_other = lax.ppermute(strips_mine, "core", cores)

    attended, att, stats = attention_forward(ids, mask, query_states, keys, values)
    gathered = [att] * 4
    for p in (3, 2, 1):
        pairs = [(i, i ^ p) for i in range(4)]
        gathered[p] = lax.ppermute(att, NEAR, pairs)

    grad_attended, half_mine, half_other = use_upstream(ids, upstream, out_weight, att)
    half_near = lax.ppermute(half_other, "core", cores)
    halves = merge(half_mine, half_near)
    grad_parts = [halves[0]]
    for p in (6, 7, 5, 4, 2, 3, 1):
        pairs = [(i, i ^ p) for i in range(PLANE)]
        grad_parts.append(lax.ppermute(halves[p], ("xlo", "y"), pairs))

    partials = project(ids, strips_mine, strips_other, gathered)
    projected = partials[0].astype(jnp.float32)
    for p in (2, 1, 3):
        pairs = [(i, i ^ p) for i in range(4)]
        arrived = lax.ppermute(partials[p], "zq", pairs)
        projected = projected + arrived.astype(jnp.float32)
    projected = projected.astype(jnp.bfloat16).T

    grad_query, left, own, right = attention_backward(
        ids, mask, query_states, keys, values, grad_attended, att, stats
    )
    from_right = lax.ppermute(left, FRAME, down)
    from_left = lax.ppermute(right, FRAME, up)
    summed = own + from_right.astype(jnp.float32) + from_left.astype(jnp.float32)
    grad_key = summed[:TOK].astype(jnp.bfloat16)
    grad_value = summed[TOK:].astype(jnp.bfloat16)

    gram_left, gram_right = gram(grad_parts)
    return (attended, projected, grad_query, grad_key, grad_value, gram_left, gram_right)


def solution(mesh):
    fine = Mesh(mesh.devices.reshape(2, 4, 2, 2, 4, 2), FRAME + HEAD)
    placed = (
        P(FRAME, HEAD),
        P(FRAME, HEAD),
        P(FRAME, HEAD),
        P(HEAD, None),
        P(FRAME, None),
        P(),
    )
    return jax.shard_map(
        local,
        mesh=fine,
        in_specs=placed,
        out_specs=(
            P(FRAME, HEAD),
            P(FRAME, HEAD),
            P(FRAME, HEAD),
            P(FRAME, HEAD),
            P(FRAME, HEAD),
            P(HEAD, FRAME, None, None),
            P(HEAD, FRAME, None, None),
        ),
        check_vma=False,
    )
```

time: 150 us -> 135 us (0.900)
  matrix products: 42.5 us -> 0 us
  Pallas kernels: 0 us -> 39 us
  local copies, waits for them, and re-layouts: 34.6 us -> 2 us
  starting transfers between devices: 28.5 us -> 50.7 us
  waiting for transfers between devices: 18.6 us -> 40.7 us
  between operations: 14.5 us -> 0.76 us
  other arithmetic: 10.9 us -> 1.05 us
    dot_general x11 -> x0, matrix products: 42.5 us -> none  [the longest x1 7.06 us: local(): jnp.einsum('hts,thd->shd', grad_scores_near, queries_ext, preferred_eleme...]
    ppermute x6 -> x19, waiting for transfers between devices: 0.02 us -> 40.7 us  [the longest x3 18.5 us: local(): arrived = lax.ppermute(partials[p], 'zq', pairs)]
    pallas_call x0 -> x8, Pallas kernels: none -> 39 us  [the longest x1 10.4 us: use_upstream(): pl.pallas_call(upstream_kernel, grid_spec=pltpu.PrefetchScalarGridSpec(nu...]
    ppermute x6 -> x19, starting transfers between devices: 18.3 us -> 44.4 us  [the longest x7 20.3 us: local(): grad_parts.append(lax.ppermute(halves[p], ('xlo', 'y'), pairs))]
    reduce_scatter x2 -> x0, waiting for transfers between devices: 18.5 us -> none  [sum_in_order(): blocks = lax.psum_scatter(blocks, axes[k], scatter_dimension=0, tiled=True)]
    convert_element_type x2 -> x0, local copies, waits for them, and re-layouts: 12.4 us -> none  [the longest x1 7.98 us: local(): partial_value.astype(jnp.bfloat16)]
    unnamed x41 -> x6, local copies, waits for them, and re-layouts: 9.91 us -> 1.09 us
    transpose x1 -> x0, local copies, waits for them, and re-layouts: 5.35 us -> none  [sum_in_order(): jnp.moveaxis(blocks, sequence, range(len(axes))).reshape(-1, *inside)]
  transfers between devices with their start and end apart: 9 -> 20, of which waited for: 2 -> 6; matrix products, arithmetic and copies ran while one was open for 41% -> 1% of each run, Pallas kernels for 0% -> 24%
where the time goes in v1:
time: 135 us; the launch traced here: 134 us
  starting transfers between devices  50.7 us (38%)
  waiting for transfers between devices  40.7 us (30%)
  Pallas kernels  39 us (29%)
  local copies, waits for them, and re-layouts  2 us (1%)
    ppermute x7, starting transfers between devices, local(): grad_parts.append(lax.ppermute(halves[p], ('xlo', 'y'), pairs))  20.3 us
    ppermute x3, waiting for transfers between devices, local(): arrived = lax.ppermute(partials[p], 'zq', pairs)  18.5 us
    pallas_call x1, Pallas kernels, use_upstream(): pl.pallas_call(upstream_kernel, grid_spec=pltpu.PrefetchScalarGridSpec(nu...  10.4 us
    ppermute x3, waiting for transfers between devices, local(): gathered[p] = lax.ppermute(att, NEAR, pairs)  9.65 us
    pallas_call x1, Pallas kernels, attention_backward(): pl.pallas_call(backward_kernel, grid_spec=pltpu.PrefetchScalarGridSpec(nu...  8.48 us
    ppermute x3, starting transfers between devices, local(): arrived = lax.ppermute(partials[p], 'zq', pairs)  7.73 us
    pallas_call x1, Pallas kernels, pack_weights(): pl.pallas_call(pack_kernel, grid_spec=pltpu.PrefetchScalarGridSpec(num_sc...  6.78 us
    all_to_all x1, starting transfers between devices, local(): strips_mine = lax.all_to_all(strips, NEAR, 0, 0, tiled=True)  6.32 us
  transfers between devices with their start and end apart: 20, of which 6 were waited for; matrix products, arithmetic and copies ran while one was open for 1% of the time, Pallas kernels for 24%

profile of v1, /device:TPU:1, one launch (start us, length us, event | category | flops | bytes accessed | tf_op | source)
XLA Modules:
  0.0 134.2 jit_solution(14359691631600043510)
XLA Ops:
  0.7 6.8 %pack_weights.1 = bf16[2,2,4,320,128]{4,3,2,1,0:T(8,128)(2,1)} custom-call(s32[5]{0:T(128)S(1)} %stack.23.ids, bf16[256,5120]{1,0:T(8,128)(2,1)} %w.3), custom_call_target="tpu_custom_call" | custom-call | flops 170000000 | bytes 2600000 | tf_op jit(solution)/shard_map/pack_weights/pallas_call | solution.py:207
  7.5 6.3 %all-to-all-start = ((bf16[4,4,320,128]{3,2,1,0:T(8,128)(2,1)}), bf16[4,4,320,128]{3,2,1,0:T(8,128)(2,1)S(1)}, u32[]{:S(2)}, u32[]{:S(2)}) async-start(bf16[4,4,320,128]{3,2,1,0:T(8,128)(2,1)} %bitcast.6), calls=%async_computation | async-start | bytes 2621440 | tf_op jit(solution)/shard_map/all_to_all | solution.py:414
  13.8 1.0 pair_up.1
  14.9 4.0 %collective-permute-start = (bf16[512,512]{1,0:T(8,128)(2,1)S(1)}, bf16[512,512]{1,0:T(8,128)(2,1)S(1)}, u32[]{:S(2)}, u32[]{:S(2)}) collective-permute-start(bf16[512,512]{1,0:T(8,128)(2,1)S(1)} %pair_up.1), channel_id=1, source_target_pairs={{0,16},{16,32},{32,48},{48,64},{64,80},{80,96},{96,112},{112,128},... | collective-permute-start | bytes 1572872 | tf_op jit(solution)/shard_map/ppermute | solution.py:408
  18.9 1.9 %collective-permute-start.1 = (bf16[512,512]{1,0:T(8,128)(2,1)S(1)}, bf16[512,512]{1,0:T(8,128)(2,1)S(1)}, u32[]{:S(2)}, u32[]{:S(2)}) collective-permute-start(bf16[512,512]{1,0:T(8,128)(2,1)S(1)} %pair_up.1), channel_id=1, source_target_pairs={{16,0},{32,16},{48,32},{64,48},{80,64},{96,80},{112,96},{128,112},... | collective-permute-start | bytes 1572872 | tf_op jit(solution)/shard_map/ppermute | solution.py:409
  20.9 4.2 %collective-permute-done.kl.vl = bf16[512,512]{1,0:T(8,128)(2,1)S(1)} collective-permute-done((bf16[512,512]{1,0:T(8,128)(2,1)S(1)}, bf16[512,512]{1,0:T(8,128)(2,1)S(1)}, u32[]{:S(2)}, u32[]{:S(2)}) %collective-permute-start) | collective-permute-done | bytes 524320 | tf_op jit(solution)/shard_map/ppermute | solution.py:408
  25.0 4.7 %collective-permute-done.1.kr.vr = bf16[512,512]{1,0:T(8,128)(2,1)S(1)} collective-permute-done((bf16[512,512]{1,0:T(8,128)(2,1)S(1)}, bf16[512,512]{1,0:T(8,128)(2,1)S(1)}, u32[]{:S(2)}, u32[]{:S(2)}) %collective-permute-start.1) | collective-permute-done | bytes 524320 | tf_op jit(solution)/shard_map/ppermute | solution.py:409
  29.7 6.1 %attention_forward.1 = (bf16[512,256]{1,0:T(8,128)(2,1)}, bf16[512,256]{1,0:T(8,128)(2,1)S(1)}, f32[2,8,512]{2,1,0:T(8,128)S(1)}) custom-call(s32[5]{0:T(128)S(1)} %stack.23.ids, s32[5,32]{1,0:T(8,128)S(1)} %bitcast.9, bf16[512,256]{1,0:T(8,128)(2,1)} %q.3, bf16[512,512]{1,0:T(8,128)(2,1)S(1)} %collective-permute-done.kl.vl, bf16[512,256]{1,0:T(8,128)(2,1)} %k.5, ...), custom_call_target="tpu_custom_call" | custom-call | flops 700000000 | bytes 2400000 | tf_op jit(solution)/shard_map/attention_forward/pallas_call | solution.py:146
  35.8 10.4 %use_upstream.1 = (bf16[512,256]{1,0:T(8,128)(2,1)S(1)}, bf16[8,320,256]{2,1,0:T(8,128)(2,1)S(1)}, bf16[8,320,256]{2,1,0:T(8,128)(2,1)}) custom-call(s32[5]{0:T(128)S(1)} %stack.23.ids, bf16[512,5120]{1,0:T(8,128)(2,1)} %up.1, bf16[256,5120]{1,0:T(8,128)(2,1)} %w.3, bf16[512,256]{1,0:T(8,128)(2,1)S(1)} %get-tuple-element.32.a0.att), custom_call_target="tpu_custom_call" | custom-call | flops 3000000000 | bytes 11000000 | tf_op jit(solution)/shard_map/use_upstream/pallas_call | solution.py:281
  46.2 1.1 copy-done
  47.3 0.5 collective-permute-start.2
  47.8 1.7 %collective-permute-start.3 = (bf16[512,256]{1,0:T(8,128)(2,1)S(1)}, bf16[512,256]{1,0:T(8,128)(2,1)S(1)}, u32[]{:S(2)}, u32[]{:S(2)}) collective-permute-start(bf16[512,256]{1,0:T(8,128)(2,1)S(1)} %get-tuple-element.32.a0.att), channel_id=1, source_target_pairs={{0,1},{1,0},{8,9},{9,8},{2,3},{3,2},{10,11},{11,10},{4,5},{5,4},{1... | collective-permute-start | bytes 786440 | tf_op jit(solution)/shard_map/ppermute | solution.py:421
  49.6 8.5 %attention_backward.1 = (bf16[512,256]{1,0:T(8,128)(2,1)}, bf16[1024,256]{1,0:T(8,128)(2,1)S(1)}, f32[1024,256]{1,0:T(8,128)S(1)}, bf16[1024,256]{1,0:T(8,128)(2,1)S(1)}) custom-call(s32[5]{0:T(128)S(1)} %stack.23.ids, s32[5,32]{1,0:T(8,128)S(1)} %bitcast.10, bf16[512,256]{1,0:T(8,128)(2,1)} %q.3, bf16[512,512]{1,0:T(8,128)(2,1)S(1)} %collective-permute-done.kl.vl, ...), custom_call_target="tpu_custom_call" | custom-call | flops 1800000000 | bytes 5000000 | tf_op jit(solution)/shard_map/attention_backward/pallas_call | solution.py:170
  58.0 3.4 %collective-permute-start.10 = (bf16[1024,256]{1,0:T(8,128)(2,1)S(1)}, bf16[1024,256]{1,0:T(8,128)(2,1)S(1)}, u32[]{:S(2)}, u32[]{:S(2)}) collective-permute-start(bf16[1024,256]{1,0:T(8,128)(2,1)S(1)} %get-tuple-element.42), channel_id=1, source_target_pairs={{0,16},{16,32},{32,48},{48,64},{64,80},{80,96},{96,112},{112,128},... | collective-permute-start | bytes 1572872 | tf_op jit(solution)/shard_map/ppermute | solution.py:443
  61.4 1.9 %collective-permute-start.9 = (bf16[1024,256]{1,0:T(8,128)(2,1)S(1)}, bf16[1024,256]{1,0:T(8,128)(2,1)S(1)}, u32[]{:S(2)}, u32[]{:S(2)}) collective-permute-start(bf16[1024,256]{1,0:T(8,128)(2,1)S(1)} %get-tuple-element.41), channel_id=1, source_target_pairs={{16,0},{32,16},{48,32},{64,48},{80,64},{96,80},{112,96},{128,112},... | collective-permute-start | bytes 1572872 | tf_op jit(solution)/shard_map/ppermute | solution.py:442
  63.4 2.5 %collective-permute-start.4 = (bf16[512,256]{1,0:T(8,128)(2,1)S(1)}, bf16[512,256]{1,0:T(8,128)(2,1)S(1)}, u32[]{:S(2)}, u32[]{:S(2)}) collective-permute-start(bf16[512,256]{1,0:T(8,128)(2,1)S(1)} %get-tuple-element.32.a0.att), channel_id=1, source_target_pairs={{0,8},{1,9},{8,0},{9,1},{2,10},{3,11},{10,2},{11,3},{4,12},{5,13},... | collective-permute-start | bytes 786440 | tf_op jit(solution)/shard_map/ppermute | solution.py:421
  66.2 1.6 %merge.1 = (bf16[320,256]{1,0:T(8,128)(2,1)S(1)}, bf16[320,256]{1,0:T(8,128)(2,1)S(1)}, bf16[320,256]{1,0:T(8,128)(2,1)S(1)}, bf16[320,256]{1,0:T(8,128)(2,1)S(1...) custom-call(bf16[8,320,256]{2,1,0:T(8,128)(2,1)S(1)} %copy-done.1, ...), custom_call_target="tpu_custom_call" | custom-call | flops 1000000 | bytes 4000000 | tf_op jit(solution)/shard_map/merge/pallas_call | solution.py:316
  67.9 9.6 %collective-permute-done.4.a2 = bf16[512,256]{1,0:T(8,128)(2,1)S(1)} collective-permute-done((bf16[512,256]{1,0:T(8,128)(2,1)S(1)}, bf16[512,256]{1,0:T(8,128)(2,1)S(1)}, u32[]{:S(2)}, u32[]{:S(2)}) %collective-permute-start.4) | collective-permute-done | bytes 262176 | tf_op jit(solution)/shard_map/ppermute | solution.py:421
  77.5 1.1 collective-permute-start.12
  78.6 3.3 %collective-permute-start.13 = (bf16[320,256]{1,0:T(8,128)(2,1)S(1)}, bf16[320,256]{1,0:T(8,128)(2,1)S(1)}, u32[]{:S(2)}, u32[]{:S(2)}) collective-permute-start(bf16[320,256]{1,0:T(8,128)(2,1)S(1)} %get-tuple-element.47), channel_id=1, source_target_pairs={{0,224},{32,192},{64,160},{96,128},{128,96},{160,64},{192,32},{224... | collective-permute-start | bytes 491528 | tf_op jit(solution)/shard_map/ppermute | solution.py:429
  81.9 12.2 %collective-permute-start.14 = (bf16[320,256]{1,0:T(8,128)(2,1)S(1)}, bf16[320,256]{1,0:T(8,128)(2,1)S(1)}, u32[]{:S(2)}, u32[]{:S(2)}) collective-permute-start(bf16[320,256]{1,0:T(8,128)(2,1)S(1)} %get-tuple-element.48), channel_id=1, source_target_pairs={{0,160},{32,128},{64,224},{96,192},{128,32},{160,0},{192,96},{224,... | collective-permute-start | bytes 491528 | tf_op jit(solution)/shard_map/ppermute | solution.py:429
  94.1 2.1 %project.1 = (bf16[320,512]{1,0:T(8,128)(2,1)S(1)}, bf16[320,512]{1,0:T(8,128)(2,1)S(1)}, bf16[320,512]{1,0:T(8,128)(2,1)S(1)}, bf16[320,512]{1,0:T(8,128)(2,1)S(1)}) custom-call(s32[5]{0:T(128)S(1)} %stack.23.ids, bf16[4,4,320,128]{3,2,1,0:T(8,128)(2,1)S(1)} %all-to-all-done.mine, bf16[4,4,320,128]{3,2,1,0:T(8,128)(2,1)S(1)} %collective-permute-done.2.other, ...), custom_call_target="tpu_custom_call" | custom-call | flops 1340000000 | bytes 5000000 | tf_op jit(solution)/shard_map/project/pallas_call | solution.py:241
  96.4 1.6 %collective-permute-start.16 = (bf16[320,256]{1,0:T(8,128)(2,1)S(1)}, bf16[320,256]{1,0:T(8,128)(2,1)S(1)}, u32[]{:S(2)}, u32[]{:S(2)}) collective-permute-start(bf16[320,256]{1,0:T(8,128)(2,1)S(1)} %get-tuple-element.50), channel_id=1, source_target_pairs={{0,64},{32,96},{64,0},{96,32},{128,192},{160,224},{192,128},{224,1... | collective-permute-start | bytes 491528 | tf_op jit(solution)/shard_map/ppermute | solution.py:429
  98.0 6.0 %collective-permute-start.6 = (bf16[320,512]{1,0:T(8,128)(2,1)S(1)}, bf16[320,512]{1,0:T(8,128)(2,1)S(1)}, u32[]{:S(2)}, u32[]{:S(2)}) collective-permute-start(bf16[320,512]{1,0:T(8,128)(2,1)S(1)} %get-tuple-element.34), channel_id=1, source_target_pairs={{0,4},{2,6},{4,0},{6,2},{1,5},{3,7},{5,1},{7,3},{8,12},{10,14},{12... | collective-permute-start | bytes 983048 | tf_op jit(solution)/shard_map/ppermute | solution.py:435
  104.0 1.2 collective-permute-start.7
  105.9 2.0 %collective-permute-start.17 = (bf16[320,256]{1,0:T(8,128)(2,1)S(1)}, bf16[320,256]{1,0:T(8,128)(2,1)S(1)}, u32[]{:S(2)}, u32[]{:S(2)}) collective-permute-start(bf16[320,256]{1,0:T(8,128)(2,1)S(1)} %get-tuple-element.51), channel_id=1, source_target_pairs={{0,96},{32,64},{64,32},{96,0},{128,224},{160,192},{192,160},{224,1... | collective-permute-start | bytes 491528 | tf_op jit(solution)/shard_map/ppermute | solution.py:429
  107.9 0.8 fusion.1
  108.7 2.9 %collective-permute-done.17.refs_6_ = bf16[320,256]{1,0:T(8,128)(2,1)S(1)} collective-permute-done((bf16[320,256]{1,0:T(8,128)(2,1)S(1)}, bf16[320,256]{1,0:T(8,128)(2,1)S(1)}, u32[]{:S(2)}, u32[]{:S(2)}) %collective-permute-start.17) | collective-permute-done | bytes 163872 | tf_op jit(solution)/shard_map/ppermute | solution.py:429
  111.7 0.7 collective-permute-done.18.refs_7_
  112.4 2.4 %gram.1 = (f32[2,1,128,128]{3,2,1,0:T(8,128)}, f32[2,1,320,320]{3,2,1,0:T(8,128)}) custom-call(bf16[320,256]{1,0:T(8,128)(2,1)S(1)} %get-tuple-element.45.refs_0_, bf16[320,256]{1,0:T(8,128)(2,1)S(1)} %collective-permute-done.12.refs_1_, bf16[320,256]{1,0:T(8,128)(2,1)S(1)} %collective-permute-done.13.refs_2_, ...), custom_call_target="tpu_custom_call" | custom-call | flops 400000000 | bytes 2000000 | tf_op jit(solution)/shard_map/gram/pallas_call | solution.py:347
  114.8 18.5 %collective-permute-done.7 = bf16[320,512]{1,0:T(8,128)(2,1)S(1)} collective-permute-done((bf16[320,512]{1,0:T(8,128)(2,1)S(1)}, bf16[320,512]{1,0:T(8,128)(2,1)S(1)}, u32[]{:S(2)}, u32[]{:S(2)}) %collective-permute-start.7) | collective-permute-done | bytes 327712 | tf_op jit(solution)/shard_map/ppermute | solution.py:435
  133.3 0.9 fusion
  (26 shorter events, 1.3 us)
Async XLA Ops:
  7.5 22.2 %copy-start.2 = (s32[32,5]{0,1:T(8,128)S(1)}, s32[32,5]{0,1:T(8,128)}, u32[]{:S(2)}) copy-start(s32[32,5]{0,1:T(8,128)} %param.11) | copy-start | bytes 1924
  7.5 39.8 %all-to-all-start = ((bf16[4,4,320,128]{3,2,1,0:T(8,128)(2,1)}), bf16[4,4,320,128]{3,2,1,0:T(8,128)(2,1)S(1)}, u32[]{:S(2)}, u32[]{:S(2)}) async-start(bf16[4,4,320,128]{3,2,1,0:T(8,128)(2,1)} %bitcast.6), calls=%async_computation | async-start | bytes 2621440 | tf_op jit(solution)/shard_map/all_to_all | solution.py:414
  14.9 10.2 %collective-permute-start = (bf16[512,512]{1,0:T(8,128)(2,1)S(1)}, bf16[512,512]{1,0:T(8,128)(2,1)S(1)}, u32[]{:S(2)}, u32[]{:S(2)}) collective-permute-start(bf16[512,512]{1,0:T(8,128)(2,1)S(1)} %pair_up.1), channel_id=1, source_target_pairs={{0,16},{16,32},{32,48},{48,64},{64,80},{80,96},{96,112},{112,128},... | collective-permute-start | bytes 1572872 | tf_op jit(solution)/shard_map/ppermute | solution.py:408
  18.9 10.8 %collective-permute-start.1 = (bf16[512,512]{1,0:T(8,128)(2,1)S(1)}, bf16[512,512]{1,0:T(8,128)(2,1)S(1)}, u32[]{:S(2)}, u32[]{:S(2)}) collective-permute-start(bf16[512,512]{1,0:T(8,128)(2,1)S(1)} %pair_up.1), channel_id=1, source_target_pairs={{16,0},{32,16},{48,32},{64,48},{80,64},{96,80},{112,96},{128,112},... | collective-permute-start | bytes 1572872 | tf_op jit(solution)/shard_map/ppermute | solution.py:409
  46.2 1.1 copy-start
  47.3 18.5 %collective-permute-start.11 = (bf16[8,320,256]{2,1,0:T(8,128)(2,1)}, bf16[8,320,256]{2,1,0:T(8,128)(2,1)}, u32[]{:S(2)}, u32[]{:S(2)}) collective-permute-start(bf16[8,320,256]{2,1,0:T(8,128)(2,1)} %get-tuple-element.44), channel_id=1, source_target_pairs={{0,16},{16,0},{1,17},{17,1},{2,18},{18,2},{3,19},{19,3},{4,20},{20... | collective-permute-start | bytes 3932168 | tf_op jit(solution)/shard_map/ppermute | solution.py:424
  47.3 34.6 %collective-permute-start.2 = (bf16[4,4,320,128]{3,2,1,0:T(8,128)(2,1)S(1)}, bf16[4,4,320,128]{3,2,1,0:T(8,128)(2,1)S(1)}, u32[]{:S(2)}, u32[]{:S(2)}) collective-permute-start(bf16[4,4,320,128]{3,2,1,0:T(8,128)(2,1)S(1)} %all-to-all-done.mine), channel_id=1, source_target_pairs={{0,16},{16,0},{1,17},{17,1},{2,18},{18,2},{3,19},{19,3},{4,20},{20... | collective-permute-start | bytes 3932168 | tf_op jit(solution)/shard_map/ppermute | solution.py:415
  47.8 15.5 %collective-permute-start.3 = (bf16[512,256]{1,0:T(8,128)(2,1)S(1)}, bf16[512,256]{1,0:T(8,128)(2,1)S(1)}, u32[]{:S(2)}, u32[]{:S(2)}) collective-permute-start(bf16[512,256]{1,0:T(8,128)(2,1)S(1)} %get-tuple-element.32.a0.att), channel_id=1, source_target_pairs={{0,1},{1,0},{8,9},{9,8},{2,3},{3,2},{10,11},{11,10},{4,5},{5,4},{1... | collective-permute-start | bytes 786440 | tf_op jit(solution)/shard_map/ppermute | solution.py:421
  49.6 16.7 %copy-start.1 = (bf16[8,320,256]{2,1,0:T(8,128)(2,1)S(1)}, bf16[8,320,256]{2,1,0:T(8,128)(2,1)}, u32[]{:S(2)}) copy-start(bf16[8,320,256]{2,1,0:T(8,128)(2,1)} %copy-done) | copy-start | bytes 3932164
  58.0 38.2 %collective-permute-start.10 = (bf16[1024,256]{1,0:T(8,128)(2,1)S(1)}, bf16[1024,256]{1,0:T(8,128)(2,1)S(1)}, u32[]{:S(2)}, u32[]{:S(2)}) collective-permute-start(bf16[1024,256]{1,0:T(8,128)(2,1)S(1)} %get-tuple-element.42), channel_id=1, source_target_pairs={{0,16},{16,32},{32,48},{48,64},{64,80},{80,96},{96,112},{112,128},... | collective-permute-start | bytes 1572872 | tf_op jit(solution)/shard_map/ppermute | solution.py:443
  61.4 35.0 %collective-permute-start.9 = (bf16[1024,256]{1,0:T(8,128)(2,1)S(1)}, bf16[1024,256]{1,0:T(8,128)(2,1)S(1)}, u32[]{:S(2)}, u32[]{:S(2)}) collective-permute-start(bf16[1024,256]{1,0:T(8,128)(2,1)S(1)} %get-tuple-element.41), channel_id=1, source_target_pairs={{16,0},{32,16},{48,32},{64,48},{80,64},{96,80},{112,96},{128,112},... | collective-permute-start | bytes 1572872 | tf_op jit(solution)/shard_map/ppermute | solution.py:442
  63.4 14.2 %collective-permute-start.4 = (bf16[512,256]{1,0:T(8,128)(2,1)S(1)}, bf16[512,256]{1,0:T(8,128)(2,1)S(1)}, u32[]{:S(2)}, u32[]{:S(2)}) collective-permute-start(bf16[512,256]{1,0:T(8,128)(2,1)S(1)} %get-tuple-element.32.a0.att), channel_id=1, source_target_pairs={{0,8},{1,9},{8,0},{9,1},{2,10},{3,11},{10,2},{11,3},{4,12},{5,13},... | collective-permute-start | bytes 786440 | tf_op jit(solution)/shard_map/ppermute | solution.py:421
  65.8 12.8 %collective-permute-start.5 = (bf16[512,256]{1,0:T(8,128)(2,1)S(1)}, bf16[512,256]{1,0:T(8,128)(2,1)S(1)}, u32[]{:S(2)}, u32[]{:S(2)}) collective-permute-start(bf16[512,256]{1,0:T(8,128)(2,1)S(1)} %get-tuple-element.32.a0.att), channel_id=1, source_target_pairs={{0,9},{1,8},{8,1},{9,0},{2,11},{3,10},{10,3},{11,2},{4,13},{5,12},... | collective-permute-start | bytes 786440 | tf_op jit(solution)/shard_map/ppermute | solution.py:421
  77.5 20.5 %collective-permute-start.12 = (bf16[320,256]{1,0:T(8,128)(2,1)S(1)}, bf16[320,256]{1,0:T(8,128)(2,1)S(1)}, u32[]{:S(2)}, u32[]{:S(2)}) collective-permute-start(bf16[320,256]{1,0:T(8,128)(2,1)S(1)} %get-tuple-element.46), channel_id=1, source_target_pairs={{0,192},{32,224},{64,128},{96,160},{128,64},{160,96},{192,0},{224,... | collective-permute-start | bytes 491528 | tf_op jit(solution)/shard_map/ppermute | solution.py:429
  78.6 25.4 %collective-permute-start.13 = (bf16[320,256]{1,0:T(8,128)(2,1)S(1)}, bf16[320,256]{1,0:T(8,128)(2,1)S(1)}, u32[]{:S(2)}, u32[]{:S(2)}) collective-permute-start(bf16[320,256]{1,0:T(8,128)(2,1)S(1)} %get-tuple-element.47), channel_id=1, source_target_pairs={{0,224},{32,192},{64,160},{96,128},{128,96},{160,64},{192,32},{224... | collective-permute-start | bytes 491528 | tf_op jit(solution)/shard_map/ppermute | solution.py:429
  81.9 23.3 %collective-permute-start.14 = (bf16[320,256]{1,0:T(8,128)(2,1)S(1)}, bf16[320,256]{1,0:T(8,128)(2,1)S(1)}, u32[]{:S(2)}, u32[]{:S(2)}) collective-permute-start(bf16[320,256]{1,0:T(8,128)(2,1)S(1)} %get-tuple-element.48), channel_id=1, source_target_pairs={{0,160},{32,128},{64,224},{96,192},{128,32},{160,0},{192,96},{224,... | collective-permute-start | bytes 491528 | tf_op jit(solution)/shard_map/ppermute | solution.py:429
  96.3 9.6 %collective-permute-start.15 = (bf16[320,256]{1,0:T(8,128)(2,1)S(1)}, bf16[320,256]{1,0:T(8,128)(2,1)S(1)}, u32[]{:S(2)}, u32[]{:S(2)}) collective-permute-start(bf16[320,256]{1,0:T(8,128)(2,1)S(1)} %get-tuple-element.49), channel_id=1, source_target_pairs={{0,128},{32,160},{64,192},{96,224},{128,0},{160,32},{192,64},{224,... | collective-permute-start | bytes 491528 | tf_op jit(solution)/shard_map/ppermute | solution.py:429
  96.4 11.5 %collective-permute-start.16 = (bf16[320,256]{1,0:T(8,128)(2,1)S(1)}, bf16[320,256]{1,0:T(8,128)(2,1)S(1)}, u32[]{:S(2)}, u32[]{:S(2)}) collective-permute-start(bf16[320,256]{1,0:T(8,128)(2,1)S(1)} %get-tuple-element.50), channel_id=1, source_target_pairs={{0,64},{32,96},{64,0},{96,32},{128,192},{160,224},{192,128},{224,1... | collective-permute-start | bytes 491528 | tf_op jit(solution)/shard_map/ppermute | solution.py:429
  98.0 16.8 %collective-permute-start.6 = (bf16[320,512]{1,0:T(8,128)(2,1)S(1)}, bf16[320,512]{1,0:T(8,128)(2,1)S(1)}, u32[]{:S(2)}, u32[]{:S(2)}) collective-permute-start(bf16[320,512]{1,0:T(8,128)(2,1)S(1)} %get-tuple-element.34), channel_id=1, source_target_pairs={{0,4},{2,6},{4,0},{6,2},{1,5},{3,7},{5,1},{7,3},{8,12},{10,14},{12... | collective-permute-start | bytes 983048 | tf_op jit(solution)/shard_map/ppermute | solution.py:435
  104.0 29.3 %collective-permute-start.7 = (bf16[320,512]{1,0:T(8,128)(2,1)S(1)}, bf16[320,512]{1,0:T(8,128)(2,1)S(1)}, u32[]{:S(2)}, u32[]{:S(2)}) collective-permute-start(bf16[320,512]{1,0:T(8,128)(2,1)S(1)} %get-tuple-element.35), channel_id=1, source_target_pairs={{0,2},{2,0},{4,6},{6,4},{1,3},{3,1},{5,7},{7,5},{8,10},{10,8},{12,... | collective-permute-start | bytes 983048 | tf_op jit(solution)/shard_map/ppermute | solution.py:435
  105.2 28.1 %collective-permute-start.8 = (bf16[320,512]{1,0:T(8,128)(2,1)S(1)}, bf16[320,512]{1,0:T(8,128)(2,1)S(1)}, u32[]{:S(2)}, u32[]{:S(2)}) collective-permute-start(bf16[320,512]{1,0:T(8,128)(2,1)S(1)} %get-tuple-element.36), channel_id=1, source_target_pairs={{0,6},{2,4},{4,2},{6,0},{1,7},{3,5},{5,3},{7,1},{8,14},{10,12},{12... | collective-permute-start | bytes 983048 | tf_op jit(solution)/shard_map/ppermute | solution.py:435
  105.9 5.8 %collective-permute-start.17 = (bf16[320,256]{1,0:T(8,128)(2,1)S(1)}, bf16[320,256]{1,0:T(8,128)(2,1)S(1)}, u32[]{:S(2)}, u32[]{:S(2)}) collective-permute-start(bf16[320,256]{1,0:T(8,128)(2,1)S(1)} %get-tuple-element.51), channel_id=1, source_target_pairs={{0,96},{32,64},{64,32},{96,0},{128,224},{160,192},{192,160},{224,1... | collective-permute-start | bytes 491528 | tf_op jit(solution)/shard_map/ppermute | solution.py:429
  107.9 4.5 %collective-permute-start.18 = (bf16[320,256]{1,0:T(8,128)(2,1)S(1)}, bf16[320,256]{1,0:T(8,128)(2,1)S(1)}, u32[]{:S(2)}, u32[]{:S(2)}) collective-permute-start(bf16[320,256]{1,0:T(8,128)(2,1)S(1)} %get-tuple-element.52), channel_id=1, source_target_pairs={{0,32},{32,0},{64,96},{96,64},{128,160},{160,128},{192,224},{224,1... | collective-permute-start | bytes 491528 | tf_op jit(solution)/shard_map/ppermute | solution.py:429

commit v2 on v1

v2 whole, which is shorter than its diff:
```python
import functools
import math

import jax
import jax.numpy as jnp
from jax import lax
from jax.experimental import pallas as pl
from jax.experimental.pallas import tpu as pltpu
from jax.sharding import Mesh
from jax.sharding import PartitionSpec as P


D = 5120
HD = 128
TILE = 256
TILES_DEV = 2
CB = 320
TOK = 512
NT = 32
WIN = 5
GROUP = 2 * CB
STRIP = 4 * CB
STRIPS = D // STRIP
FRAME = ("xlo", "y", "core")
HEAD = ("xhi", "zq", "zp")
NEAR = ("xhi", "zp")


epsilon = 1e-06
SCALING = 1.0 / math.sqrt(HD)
LOG2E = 1.0 / math.log(2.0)
NEG = -1e30
VMEM_BYTES = 16 * 1024 * 1024
PLANE = 8
ORDER = (2, 1, 3, 0)


def dot_nt(a, b, precision=None):
    return lax.dot_general(
        a, b, (((1,), (1,)), ((), ())), precision=precision, preferred_element_type=jnp.float32
    )


def dot_nn(a, b):
    return jnp.dot(a, b, preferred_element_type=jnp.float32)


def eye(n):
    rows = lax.broadcasted_iota(jnp.int32, (n, n), 0)
    cols = lax.broadcasted_iota(jnp.int32, (n, n), 1)
    return (rows == cols).astype(jnp.float32).astype(jnp.bfloat16)


def allowed(ids, mask, i, j):
    tile = ids[0] * TILES_DEV + i
    key_tile = tile + (j - 2)
    return (mask[j, tile] == 1) & (key_tile >= 0) & (key_tile < NT)


def extend(k, v, before, after, kx, vx):
    head = pl.program_id(0)
    lanes = pl.ds(pl.multiple_of(head * HD, HD), HD)
    value_lanes = pl.ds(pl.multiple_of((2 + head) * HD, HD), HD)
    kx[0:TOK] = before[:, lanes]
    kx[TOK : 2 * TOK] = k[...]
    kx[2 * TOK : 3 * TOK] = after[:, lanes]
    vx[0:TOK] = before[:, value_lanes]
    vx[TOK : 2 * TOK] = v[...]
    vx[2 * TOK : 3 * TOK] = after[:, value_lanes]
    return lanes


def forward_kernel(ids, mask, q, k, v, before, after, att, copy, stat, kx, vx):
    head = pl.program_id(0)
    lanes = extend(k, v, before, after, kx, vx)
    first_lane = lax.broadcasted_iota(jnp.int32, (8, HD), 1) == 0
    pick = jnp.where(first_lane, jnp.float32(1), jnp.float32(0))
    for i in range(TILES_DEV):
        rows = slice(i * TILE, (i + 1) * TILE)
        parts = []
        for j in range(WIN):
            keys = kx[(i + j) * TILE : (i + j + 1) * TILE]
            part = dot_nt(q[rows], keys) * jnp.float32(SCALING * LOG2E)
            parts.append(jnp.where(allowed(ids, mask, i, j), part, jnp.float32(NEG)))
        peak = parts[0]
        for part in parts[1:]:
            peak = jnp.maximum(peak, part)
        peak = jnp.max(peak, axis=1, keepdims=True)
        out = jnp.zeros((TILE, HD), jnp.float32)
        total = jnp.zeros((TILE, TILE), jnp.float32)
        for j in range(WIN):
            weight = jnp.exp2(parts[j] - peak)
            total = total + weight
            values = vx[(i + j) * TILE : (i + j + 1) * TILE]
            out = out + dot_nn(weight.astype(jnp.bfloat16), values)
        total = jnp.sum(total, axis=1, keepdims=True)
        result = (out / total).astype(jnp.bfloat16)
        att[rows] = result
        copy[rows, lanes] = result
        log_total = peak + jnp.log(total) * jnp.float32(LOG2E)
        spread = jnp.broadcast_to(log_total, (TILE, HD))
        stat[head, :, rows] = dot_nt(pick, spread, lax.Precision.HIGHEST)


def backward_kernel(
    ids, mask, q, k, v, before, after, grads, att, stat, dq, dl, do, dr, kx, vx, g, dsx, kt
):
    head = pl.program_id(0)
    lanes = extend(k, v, before, after, kx, vx)
    g[...] = grads[:, lanes]
    unit = eye(HD)
    for e in range(6):
        block = slice(e * TILE, (e + 1) * TILE)
        kt[:, block] = dot_nt(unit, kx[block]).astype(jnp.bfloat16)
    products = g[...].astype(jnp.float32) * att[:, lanes].astype(jnp.float32)
    ones = jnp.ones((8, HD), jnp.float32)
    deltas = dot_nt(ones, products, lax.Precision.HIGHEST)[0:1]
    totals = stat[head, 0:1, :]
    for e in range(6):
        keys = kx[e * TILE : (e + 1) * TILE]
        values = vx[e * TILE : (e + 1) * TILE]
        tiles = [i for i in range(TILES_DEV) if 0 <= e - i < WIN]
        dk = jnp.zeros((TILE, HD), jnp.float32)
        dv = jnp.zeros((TILE, HD), jnp.float32)
        for i in tiles:
            rows = slice(i * TILE, (i + 1) * TILE)
            ok = allowed(ids, mask, i, e - i)
            level = jnp.where(ok, totals[:, rows], jnp.float32(-NEG))
            scores = dot_nt(keys, q[rows]) * jnp.float32(SCALING * LOG2E)
            weight = jnp.exp2(scores - level)
            probs = dot_nt(values, g[rows])
            ds = (weight * (probs - deltas[:, rows])).astype(jnp.bfloat16)
            dsx[e * TILE : (e + 1) * TILE, rows] = ds
            dk = dk + dot_nn(ds, q[rows])
            dv = dv + dot_nn(weight.astype(jnp.bfloat16), g[rows])
        dk = dk * jnp.float32(SCALING)
        part = (e % 2) * TILE
        target = (dl, do, dr)[e // 2]
        target[part : part + TILE, lanes] = dk.astype(target.dtype)
        target[TOK + part : TOK + part + TILE, lanes] = dv.astype(target.dtype)
    wide = eye(TILE)
    for i in range(TILES_DEV):
        rows = slice(i * TILE, (i + 1) * TILE)
        window = slice(i * TILE, (i + WIN) * TILE)
        turned = dot_nn(kt[:, window], dsx[window, rows]) * jnp.float32(SCALING)
        dq[rows] = dot_nt(wide, turned.astype(jnp.bfloat16)).astype(jnp.bfloat16)


def attention_specs():
    narrow = pl.BlockSpec((TOK, HD), lambda h, *_: (0, h))
    whole = pl.BlockSpec(memory_space=pltpu.VMEM)
    return narrow, whole


def attention_forward(ids, mask, q, k, v, before, after):
    narrow, whole = attention_specs()
    return pl.pallas_call(
        forward_kernel,
        grid_spec=pltpu.PrefetchScalarGridSpec(
            num_scalar_prefetch=2,
            grid=(2,),
            in_specs=[narrow] * 3 + [whole] * 2,
            out_specs=[narrow, whole, whole],
            scratch_shapes=[pltpu.VMEM((3 * TOK, HD), jnp.bfloat16)] * 2,
        ),
        out_shape=[
            jax.ShapeDtypeStruct((TOK, 2 * HD), jnp.bfloat16),
            jax.ShapeDtypeStruct((TOK, 2 * HD), jnp.bfloat16),
            jax.ShapeDtypeStruct((2, 8, TOK), jnp.float32),
        ],
        cost_estimate=pl.CostEstimate(
            flops=700_000_000, bytes_accessed=2_400_000, transcendentals=1_300_000
        ),
        compiler_params=pltpu.CompilerParams(vmem_limit_bytes=VMEM_BYTES),
        name="attention_forward",
    )(ids, mask, q, k, v, before, after)


def attention_backward(ids, mask, q, k, v, before, after, g, att, stats):
    narrow, whole = attention_specs()
    return pl.pallas_call(
        backward_kernel,
        grid_spec=pltpu.PrefetchScalarGridSpec(
            num_scalar_prefetch=2,
            grid=(2,),
            in_specs=[narrow] * 3 + [whole] * 5,
            out_specs=[narrow, whole, whole, whole],
            scratch_shapes=[pltpu.VMEM((3 * TOK, HD), jnp.bfloat16)] * 2
            + [
                pltpu.VMEM((TOK, HD), jnp.bfloat16),
                pltpu.VMEM((3 * TOK, TOK), jnp.bfloat16),
                pltpu.VMEM((HD, 3 * TOK), jnp.bfloat16),
            ],
        ),
        out_shape=[
            jax.ShapeDtypeStruct((TOK, 2 * HD), jnp.bfloat16),
            jax.ShapeDtypeStruct((2 * TOK, 2 * HD), jnp.bfloat16),
            jax.ShapeDtypeStruct((2 * TOK, 2 * HD), jnp.float32),
            jax.ShapeDtypeStruct((2 * TOK, 2 * HD), jnp.bfloat16),
        ],
        cost_estimate=pl.CostEstimate(
            flops=1_800_000_000, bytes_accessed=5_000_000, transcendentals=1_300_000
        ),
        compiler_params=pltpu.CompilerParams(vmem_limit_bytes=VMEM_BYTES),
        name="attention_backward",
    )(ids, mask, q, k, v, before, after, g, att, stats)


def pack_kernel(ids, w, o0, o1, o2, o3, buf, strips, sems):
    here = ids[2]
    far = ids[3]
    rows = pl.ds(pl.multiple_of(ids[1] * HD, HD), HD)
    copies = []
    for c in range(STRIPS):
        lanes = slice(c * STRIP, (c + 1) * STRIP)
        copies.append(pltpu.make_async_copy(w.at[rows, lanes], buf.at[:, lanes], sems.at[c]))
    for copy in copies:
        copy.start()
    for xhi in range(2):
        copies[2 * xhi].wait()
        copies[2 * xhi + 1].wait()
        for place, p in enumerate(ORDER):
            start = pl.multiple_of((xhi * 4 + (far ^ p)) * GROUP, GROUP)
            both = buf[:, pl.ds(start, GROUP)]
            for zp in range(2):
                strips[xhi * 2 + zp, :, place * CB : (place + 1) * CB] = both[
                    :, zp * CB : (zp + 1) * CB
                ]
    for p, out in enumerate((o0, o1, o2, o3)):
        out[...] = strips[here ^ p]


def pack_weights(ids, w):
    return pl.pallas_call(
        pack_kernel,
        in_specs=[pl.BlockSpec(memory_space=pltpu.SMEM), pl.BlockSpec(memory_space=pl.ANY)],
        out_specs=[pl.BlockSpec(memory_space=pltpu.VMEM)] * 4,
        scratch_shapes=[
            pltpu.VMEM((HD, D), jnp.bfloat16),
            pltpu.VMEM((4, HD, STRIP), jnp.bfloat16),
            pltpu.SemaphoreType.DMA((STRIPS,)),
        ],
        out_shape=[jax.ShapeDtypeStruct((HD, STRIP), jnp.bfloat16)] * 4,
        cost_estimate=pl.CostEstimate(flops=0, bytes_accessed=2_600_000, transcendentals=0),
        compiler_params=pltpu.CompilerParams(vmem_limit_bytes=VMEM_BYTES),
        name="pack_weights",
    )(ids, w)


def project_kernel(part, ids, *refs):
    mine, other, gathered, outs = refs[:4], refs[4:8], refs[8:12], refs[12:14]
    near, wide, flat = refs[14:]
    core = ids[1]
    lanes = slice(part * GROUP, (part + 1) * GROUP)
    for r in range(4):
        base = r * 2 * HD
        near[:, base : base + 2 * HD] = gathered[r][...]
        wide[pl.ds(pl.multiple_of(base + core * HD, HD), HD)] = mine[r][:, lanes]
        wide[pl.ds(pl.multiple_of(base + (1 - core) * HD, HD), HD)] = other[r][:, lanes]
    grown = dot_nn(near[...], wide[...]).astype(jnp.bfloat16)
    unit = eye(HD)
    for t in range(GROUP // HD):
        cols = slice(t * HD, (t + 1) * HD)
        flat[cols] = dot_nt(unit, grown[:, cols]).astype(jnp.bfloat16)
    for place, out in enumerate(outs):
        out[...] = flat[place * CB : (place + 1) * CB]


def project(ids, mine, other, gathered, part):
    whole = pl.BlockSpec(memory_space=pltpu.VMEM)
    return pl.pallas_call(
        functools.partial(project_kernel, part),
        in_specs=[pl.BlockSpec(memory_space=pltpu.SMEM)] + [whole] * 12,
        out_specs=[whole] * 2,
        scratch_shapes=[
            pltpu.VMEM((TOK, 8 * HD), jnp.bfloat16),
            pltpu.VMEM((8 * HD, GROUP), jnp.bfloat16),
            pltpu.VMEM((GROUP, TOK), jnp.bfloat16),
        ],
        out_shape=[jax.ShapeDtypeStruct((CB, TOK), jnp.bfloat16)] * 2,
        cost_estimate=pl.CostEstimate(
            flops=670_000_000, bytes_accessed=3_000_000, transcendentals=0
        ),
        compiler_params=pltpu.CompilerParams(vmem_limit_bytes=VMEM_BYTES),
        name="project",
    )(ids, *mine, *other, *gathered)


def weight_grad_kernel(ids, up, att, mine, other, buf, turned, sems):
    first_core = ids[1] == 0
    plane = ids[4]
    copies = [
        pltpu.make_async_copy(up.at[:, c * STRIP : (c + 1) * STRIP], buf.at[c], sems.at[c])
        for c in range(STRIPS)
    ]
    for copy in copies:
        copy.start()
    turned[...] = dot_nt(eye(2 * HD), att[...]).astype(jnp.bfloat16)
    for c, copy in enumerate(copies):
        copy.wait()
        halves = [
            dot_nn(turned[...], buf[c, :, base : base + GROUP]).astype(jnp.bfloat16)
            for base in (0, GROUP)
        ]
        lanes = pl.ds(pl.multiple_of((c ^ (plane // 2)) * GROUP, GROUP), GROUP)
        for target, low in ((mine, first_core), (other, jnp.logical_not(first_core))):
            first, second = (jnp.where(low, x[:, 0:CB], x[:, CB:GROUP]) for x in halves)
            straight = (plane & 1) == 0
            target[:, lanes] = jnp.concatenate(
                [jnp.where(straight, first, second), jnp.where(straight, second, first)], axis=1
            )


def weight_grad(ids, up, att):
    whole = pl.BlockSpec(memory_space=pltpu.VMEM)
    return pl.pallas_call(
        weight_grad_kernel,
        in_specs=[
            pl.BlockSpec(memory_space=pltpu.SMEM),
            pl.BlockSpec(memory_space=pl.ANY),
            whole,
        ],
        out_specs=[whole, whole],
        scratch_shapes=[
            pltpu.VMEM((STRIPS, TOK, STRIP), jnp.bfloat16),
            pltpu.VMEM((2 * HD, TOK), jnp.bfloat16),
            pltpu.SemaphoreType.DMA((STRIPS,)),
        ],
        out_shape=[jax.ShapeDtypeStruct((2 * HD, PLANE * CB), jnp.bfloat16)] * 2,
        cost_estimate=pl.CostEstimate(
            flops=1_700_000_000, bytes_accessed=8_000_000, transcendentals=0
        ),
        compiler_params=pltpu.CompilerParams(vmem_limit_bytes=VMEM_BYTES),
        name="weight_grad",
    )(ids, up, att)


def merge_kernel(mine, near, keep, send):
    for target, lanes in ((keep, slice(0, STRIP)), (send, slice(STRIP, 2 * STRIP))):
        total = mine[:, lanes].astype(jnp.float32) + near[:, lanes].astype(jnp.float32)
        target[...] = total.astype(jnp.bfloat16)


def merge(mine, near):
    whole = pl.BlockSpec(memory_space=pltpu.VMEM)
    return pl.pallas_call(
        merge_kernel,
        in_specs=[whole] * 2,
        out_specs=[whole] * 2,
        out_shape=[jax.ShapeDtypeStruct((2 * HD, STRIP), jnp.bfloat16)] * 2,
        cost_estimate=pl.CostEstimate(
            flops=1_000_000, bytes_accessed=4_000_000, transcendentals=0
        ),
        compiler_params=pltpu.CompilerParams(vmem_limit_bytes=VMEM_BYTES),
        name="merge",
    )(mine, near)


def merge_planes_kernel(keep, came, *outs):
    for p, out in enumerate(outs):
        lanes = slice(p * CB, (p + 1) * CB)
        total = keep[:, lanes].astype(jnp.float32) + came[:, lanes].astype(jnp.float32)
        out[...] = total.astype(jnp.bfloat16)


def merge_planes(keep, came):
    whole = pl.BlockSpec(memory_space=pltpu.VMEM)
    return pl.pallas_call(
        merge_planes_kernel,
        in_specs=[whole] * 2,
        out_specs=[whole] * 4,
        out_shape=[jax.ShapeDtypeStruct((2 * HD, CB), jnp.bfloat16)] * 4,
        cost_estimate=pl.CostEstimate(
            flops=1_000_000, bytes_accessed=2_000_000, transcendentals=0
        ),
        compiler_params=pltpu.CompilerParams(vmem_limit_bytes=VMEM_BYTES),
        name="merge_planes",
    )(keep, came)


def gram_kernel(*refs):
    parts, (left, right) = refs[:4], refs[4:]
    highest = lax.Precision.HIGHEST
    total = parts[0][...].astype(jnp.float32)
    for part in parts[1:]:
        total = total + part[...].astype(jnp.float32)
    for h in range(2):
        block = total[h * HD : (h + 1) * HD]
        squares = jnp.sum(block * block, axis=0, keepdims=True)
        trace = jnp.sum(squares, axis=1, keepdims=True)
        inverse = 1.0 / (trace + epsilon)
        turned = block.T
        left[h, 0] = dot_nt(block, block, highest) * (inverse * HD)
        right[h, 0] = dot_nt(turned, turned, highest) * (inverse * CB)


def gram(parts):
    whole = pl.BlockSpec(memory_space=pltpu.VMEM)
    return pl.pallas_call(
        gram_kernel,
        in_specs=[whole] * 4,
        out_specs=[whole] * 2,
        out_shape=[
            jax.ShapeDtypeStruct((2, 1, HD, HD), jnp.float32),
            jax.ShapeDtypeStruct((2, 1, CB, CB), jnp.float32),
        ],
        cost_estimate=pl.CostEstimate(
            flops=400_000_000, bytes_accessed=2_000_000, transcendentals=0
        ),
        compiler_params=pltpu.CompilerParams(vmem_limit_bytes=VMEM_BYTES),
        name="gram",
    )(*parts)


def pair_kernel(k, v, out, sems):
    first = pltpu.make_async_copy(k, out.at[:, 0 : 2 * HD], sems.at[0])
    second = pltpu.make_async_copy(v, out.at[:, 2 * HD : 4 * HD], sems.at[1])
    first.start()
    second.start()
    first.wait()
    second.wait()


def pair_up(k, v):
    return pl.pallas_call(
        pair_kernel,
        in_specs=[pl.BlockSpec(memory_space=pl.ANY)] * 2,
        out_specs=pl.BlockSpec(memory_space=pltpu.VMEM),
        scratch_shapes=[pltpu.SemaphoreType.DMA((2,))],
        out_shape=jax.ShapeDtypeStruct((TOK, 4 * HD), jnp.bfloat16),
        cost_estimate=pl.CostEstimate(flops=0, bytes_accessed=1_000_000, transcendentals=0),
        compiler_params=pltpu.CompilerParams(vmem_limit_bytes=VMEM_BYTES),
        name="pair_up",
    )(k, v)


def in_hbm(x):
    return pltpu.with_memory_space_constraint(x, pltpu.HBM)


def local(query_states, key_states, value_states, out_weight, upstream, tile_mask):
    frame = lax.axis_index(FRAME).astype(jnp.int32)
    core = lax.axis_index("core").astype(jnp.int32)
    here = lax.axis_index(NEAR).astype(jnp.int32)
    far = lax.axis_index("zq").astype(jnp.int32)
    plane = lax.axis_index(("xlo", "y")).astype(jnp.int32)
    ids = jnp.stack([frame, core, here, far, plane])
    frames = lax.axis_size(FRAME)
    up = [(i, i + 1) for i in range(frames - 1)]
    down = [(j, i) for i, j in up]
    cores = [(0, 1), (1, 0)]
    mask = tile_mask.T
    query_states = in_hbm(query_states)
    key_states = in_hbm(key_states)
    value_states = in_hbm(value_states)

    both = pair_up(key_states, value_states)
    before = lax.ppermute(both, FRAME, up)
    after = lax.ppermute(both, FRAME, down)

    grad_attended = lax.dot_general(
        upstream, out_weight, (((1,), (1,)), ((), ())), preferred_element_type=jnp.float32
    ).astype(jnp.bfloat16)
    strips_mine = list(pack_weights(ids, in_hbm(out_weight)))
    for p in (3, 2, 1):
        pairs = [(i, i ^ p) for i in range(4)]
        strips_mine[p] = lax.ppermute(strips_mine[p], NEAR, pairs)
    strips_other = []
    for p in range(4):
        strips_other.append(lax.ppermute(strips_mine[p], "core", cores))

    attended, att, stats = attention_forward(
        ids, mask, query_states, key_states, value_states, before, after
    )
    gathered = [att] * 4
    for p in (3, 2, 1):
        pairs = [(i, i ^ p) for i in range(4)]
        gathered[p] = lax.ppermute(att, NEAR, pairs)

    half_mine, half_other = weight_grad(ids, in_hbm(upstream), att)
    half_near = lax.ppermute(half_other, "core", cores)
    keep, send = merge(half_mine, half_near)
    came = lax.ppermute(send, "xlo", cores)
    quarters = merge_planes(keep, came)
    grad_parts = [quarters[0]]
    for p in (2, 3, 1):
        pairs = [(i, i ^ p) for i in range(4)]
        grad_parts.append(lax.ppermute(quarters[p], "y", pairs))

    partials = []
    arrived = []
    for place, p in enumerate(ORDER):
        if place % 2 == 0:
            partials += project(ids, strips_mine, strips_other, gathered, place // 2)
        if p:
            pairs = [(i, i ^ p) for i in range(4)]
            arrived.append(lax.ppermute(partials[place], "zq", pairs))
    projected = partials[3].astype(jnp.float32)
    for partial in arrived:
        projected = projected + partial.astype(jnp.float32)
    projected = projected.astype(jnp.bfloat16).T

    grad_query, left, own, right = attention_backward(
        ids,
        mask,
        query_states,
        key_states,
        value_states,
        before,
        after,
        grad_attended,
        att,
        stats,
    )
    from_right = lax.ppermute(left, FRAME, down)
    from_left = lax.ppermute(right, FRAME, up)
    summed = own + from_right.astype(jnp.float32) + from_left.astype(jnp.float32)
    grad_key = summed[:TOK].astype(jnp.bfloat16)
    grad_value = summed[TOK:].astype(jnp.bfloat16)

    gram_left, gram_right = gram(grad_parts)
    return (attended, projected, grad_query, grad_key, grad_value, gram_left, gram_right)


def solution(mesh):
    fine = Mesh(mesh.devices.reshape(2, 4, 2, 2, 4, 2), FRAME + HEAD)
    placed = (
        P(FRAME, HEAD),
        P(FRAME, HEAD),
        P(FRAME, HEAD),
        P(HEAD, None),
        P(FRAME, None),
        P(),
    )
    return jax.shard_map(
        local,
        mesh=fine,
        in_specs=placed,
        out_specs=(
            P(FRAME, HEAD),
            P(FRAME, HEAD),
            P(FRAME, HEAD),
            P(FRAME, HEAD),
            P(FRAME, HEAD),
            P(HEAD, FRAME, None, None),
            P(HEAD, FRAME, None, None),
        ),
        check_vma=False,
    )
```

time: 135 us -> 127 us (0.941)
  the two profiles are of different devices: /device:TPU:1 before, /device:TPU:7 now
where the time goes in v2:
time: 127 us
  waiting for transfers between devices  51.3 us (40%)
  starting transfers between devices  41.1 us (32%)
  Pallas kernels  29.5 us (23%)
  local copies, waits for them, and re-layouts  1.61 us (1%)
  matrix products  1.56 us (1%)
    ppermute x3, waiting for transfers between devices, local(): arrived.append(lax.ppermute(partials[place], 'zq', pairs))  20.9 us
    ppermute x3, waiting for transfers between devices, local(): strips_mine[p] = lax.ppermute(strips_mine[p], NEAR, pairs)  12.6 us
    ppermute x3, waiting for transfers between devices, local(): gathered[p] = lax.ppermute(att, NEAR, pairs)  11.7 us
    pallas_call x1, Pallas kernels, attention_backward(): pl.pallas_call(backward_kernel, grid_spec=pltpu.PrefetchScalarGridSpec(nu...  8.37 us
    ppermute x3, starting transfers between devices, local(): arrived.append(lax.ppermute(partials[place], 'zq', pairs))  7.3 us
    ppermute x1, starting transfers between devices, local(): half_near = lax.ppermute(half_other, 'core', cores)  6.2 us
    pallas_call x1, Pallas kernels, attention_forward(): pl.pallas_call(forward_kernel, grid_spec=pltpu.PrefetchScalarGridSpec(num...  5.93 us
    pallas_call x1, Pallas kernels, weight_grad(): pl.pallas_call(weight_grad_kernel, in_specs=[pl.BlockSpec(memory_space=pl...  5.13 us
  transfers between devices with their start and end apart: 22, of which 8 were waited for; matrix products, arithmetic and copies ran while one was open for 3% of the time, Pallas kernels for 12%

profile of v2, /device:TPU:7, one launch (start us, length us, event | category | flops | bytes accessed | tf_op | source)
XLA Modules:
  0.0 126.9 jit_solution(236464020142432992)
XLA Ops:
  0.6 1.0 pair_up.1
  1.7 2.6 %collective-permute-start.1 = (bf16[512,512]{1,0:T(8,128)(2,1)S(1)}, bf16[512,512]{1,0:T(8,128)(2,1)S(1)}, u32[]{:S(2)}, u32[]{:S(2)}) collective-permute-start(bf16[512,512]{1,0:T(8,128)(2,1)S(1)} %pair_up.1), channel_id=1, source_target_pairs={{16,0},{32,16},{48,32},{64,48},{80,64},{96,80},{112,96},{128,112},... | collective-permute-start | bytes 1572872 | tf_op jit(solution)/shard_map/ppermute | solution.py:459
  4.3 3.1 %collective-permute-start = (bf16[512,512]{1,0:T(8,128)(2,1)S(1)}, bf16[512,512]{1,0:T(8,128)(2,1)S(1)}, u32[]{:S(2)}, u32[]{:S(2)}) collective-permute-start(bf16[512,512]{1,0:T(8,128)(2,1)S(1)} %pair_up.1), channel_id=1, source_target_pairs={{0,16},{16,32},{32,48},{48,64},{64,80},{80,96},{96,112},{112,128},... | collective-permute-start | bytes 1572872 | tf_op jit(solution)/shard_map/ppermute | solution.py:458
  7.5 4.8 %collective-permute-done.1.after = bf16[512,512]{1,0:T(8,128)(2,1)S(1)} collective-permute-done((bf16[512,512]{1,0:T(8,128)(2,1)S(1)}, bf16[512,512]{1,0:T(8,128)(2,1)S(1)}, u32[]{:S(2)}, u32[]{:S(2)}) %collective-permute-start.1) | collective-permute-done | bytes 524320 | tf_op jit(solution)/shard_map/ppermute | solution.py:459
  12.3 1.2 collective-permute-done.before
  14.2 5.9 %attention_forward.1 = (bf16[512,256]{1,0:T(8,128)(2,1)}, bf16[512,256]{1,0:T(8,128)(2,1)S(1)}, f32[2,8,512]{2,1,0:T(8,128)S(1)}) custom-call(s32[5]{0:T(128)S(1)} %stack.23.ids, s32[5,32]{1,0:T(8,128)S(1)} %bitcast.10, bf16[512,256]{1,0:T(8,128)(2,1)} %q.3, bf16[512,256]{1,0:T(8,128)(2,1)} %k.5, bf16[512,256]{1,0:T(8,128)(2,1)} %v.5, ...), custom_call_target="tpu_custom_call" | custom-call | flops 700000000 | bytes 2400000 | tf_op jit(solution)/shard_map/attention_forward/pallas_call | solution.py:157
  20.1 5.1 %weight_grad.1 = (bf16[256,2560]{1,0:T(8,128)(2,1)S(1)}, bf16[256,2560]{1,0:T(8,128)(2,1)S(1)}) custom-call(s32[5]{0:T(128)S(1)} %stack.23.ids, bf16[512,5120]{1,0:T(8,128)(2,1)} %up.1, bf16[512,256]{1,0:T(8,128)(2,1)S(1)} %get-tuple-element.37.refs_8_.att), custom_call_target="tpu_custom_call" | custom-call | flops 1700000000 | bytes 8000000 | tf_op jit(solution)/shard_map/weight_grad/pallas_call | solution.py:316
  25.3 6.2 %collective-permute-start.17 = (bf16[256,2560]{1,0:T(8,128)(2,1)S(1)}, bf16[256,2560]{1,0:T(8,128)(2,1)S(1)}, u32[]{:S(2)}, u32[]{:S(2)}) collective-permute-start(bf16[256,2560]{1,0:T(8,128)(2,1)S(1)} %get-tuple-element.48), channel_id=1, source_target_pairs={{0,16},{16,0},{1,17},{17,1},{2,18},{18,2},{3,19},{19,3},{4,20},{20... | collective-permute-start | bytes 3932168 | tf_op jit(solution)/shard_map/ppermute | solution.py:481
  31.5 2.2 %pack_weights.1 = (bf16[128,1280]{1,0:T(8,128)(2,1)S(1)}, bf16[128,1280]{1,0:T(8,128)(2,1)S(1)}, bf16[128,1280]{1,0:T(8,128)(2,1)S(1)}, bf16[128,1280]{1,0:T(8,128)(2,1)S(1)}) custom-call(s32[5]{0:T(128)S(1)} %stack.23.ids, bf16[256,5120]{1,0:T(8,128)(2,1)} %w.1), custom_call_target="tpu_custom_call" | custom-call | bytes 2600000 | tf_op jit(solution)/shard_map/pack_weights/pallas_call | solution.py:234
  33.7 1.7 %collective-permute-start.2 = (bf16[128,1280]{1,0:T(8,128)(2,1)S(1)}, bf16[128,1280]{1,0:T(8,128)(2,1)S(1)}, u32[]{:S(2)}, u32[]{:S(2)}) collective-permute-start(bf16[128,1280]{1,0:T(8,128)(2,1)S(1)} %get-tuple-element.34), channel_id=1, source_target_pairs={{0,1},{1,0},{8,9},{9,8},{2,3},{3,2},{10,11},{11,10},{4,5},{5,4},{1... | collective-permute-start | bytes 983048 | tf_op jit(solution)/shard_map/ppermute | solution.py:467
  36.2 2.0 %collective-permute-start.4 = (bf16[128,1280]{1,0:T(8,128)(2,1)S(1)}, bf16[128,1280]{1,0:T(8,128)(2,1)S(1)}, u32[]{:S(2)}, u32[]{:S(2)}) collective-permute-start(bf16[128,1280]{1,0:T(8,128)(2,1)S(1)} %get-tuple-element.36), channel_id=1, source_target_pairs={{0,9},{1,8},{8,1},{9,0},{2,11},{3,10},{10,3},{11,2},{4,13},{5,12},... | collective-permute-start | bytes 983048 | tf_op jit(solution)/shard_map/ppermute | solution.py:467
  38.9 4.3 %collective-permute-done.2.refs_1_ = bf16[128,1280]{1,0:T(8,128)(2,1)S(1)} collective-permute-done((bf16[128,1280]{1,0:T(8,128)(2,1)S(1)}, bf16[128,1280]{1,0:T(8,128)(2,1)S(1)}, u32[]{:S(2)}, u32[]{:S(2)}) %collective-permute-start.2) | collective-permute-done | bytes 327712 | tf_op jit(solution)/shard_map/ppermute | solution.py:467
  43.2 1.3 collective-permute-start.6
  44.5 8.3 %collective-permute-done.3.refs_2_ = bf16[128,1280]{1,0:T(8,128)(2,1)S(1)} collective-permute-done((bf16[128,1280]{1,0:T(8,128)(2,1)S(1)}, bf16[128,1280]{1,0:T(8,128)(2,1)S(1)}, u32[]{:S(2)}, u32[]{:S(2)}) %collective-permute-start.3) | collective-permute-done | bytes 327712 | tf_op jit(solution)/shard_map/ppermute | solution.py:467
  52.8 1.3 %collective-permute-start.7 = (bf16[128,1280]{1,0:T(8,128)(2,1)S(1)}, bf16[128,1280]{1,0:T(8,128)(2,1)S(1)}, u32[]{:S(2)}, u32[]{:S(2)}) collective-permute-start(bf16[128,1280]{1,0:T(8,128)(2,1)S(1)} %collective-permute-done.3.refs_2_), channel_id=1, source_target_pairs={{0,16},{16,0},{1,17},{17,1},{2,18},{18,2},{3,19},{19,3},{4,20},{20... | collective-permute-start | bytes 983048 | tf_op jit(solution)/shard_map/ppermute | solution.py:470
  54.1 1.6 %convolution_convert_fusion.grads = bf16[512,256]{1,0:T(8,128)(2,1)S(1)} fusion(bf16[512,5120]{1,0:T(8,128)(2,1)S(1)} %copy-done.3, bf16[256,5120]{1,0:T(8,128)(2,1)S(1)} %copy-done.2), kind=kOutput, calls=%fused_computation | convolution fusion | flops 1342308352 | bytes 8126464 | tf_op jit(solution)/shard_map/dot_general | solution.py:461
  55.6 8.4 %attention_backward.1 = (bf16[512,256]{1,0:T(8,128)(2,1)}, bf16[1024,256]{1,0:T(8,128)(2,1)S(1)}, f32[1024,256]{1,0:T(8,128)S(1)}, bf16[1024,256]{1,0:T(8,128)(2,1)S(1)}) custom-call(s32[5]{0:T(128)S(1)} %stack.23.ids, s32[5,32]{1,0:T(8,128)S(1)} %bitcast.11, bf16[512,256]{1,0:T(8,128)(2,1)} %q.3, bf16[512,256]{1,0:T(8,128)(2,1)} %k.5, bf16[512,256]{1,0:T(8,128)(2,1)} %v.5, ...), custom_call_target="tpu_custom_call" | custom-call | flops 1800000000 | bytes 5000000 | tf_op jit(solution)/shard_map/attention_backward/pallas_call | solution.py:181
  64.0 2.4 %collective-permute-start.15 = (bf16[1024,256]{1,0:T(8,128)(2,1)S(1)}, bf16[1024,256]{1,0:T(8,128)(2,1)S(1)}, u32[]{:S(2)}, u32[]{:S(2)}) collective-permute-start(bf16[1024,256]{1,0:T(8,128)(2,1)S(1)} %get-tuple-element.45), channel_id=1, source_target_pairs={{16,0},{32,16},{48,32},{64,48},{80,64},{96,80},{112,96},{128,112},... | collective-permute-start | bytes 1572872 | tf_op jit(solution)/shard_map/ppermute | solution.py:515
  66.4 3.2 %collective-permute-start.16 = (bf16[1024,256]{1,0:T(8,128)(2,1)S(1)}, bf16[1024,256]{1,0:T(8,128)(2,1)S(1)}, u32[]{:S(2)}, u32[]{:S(2)}) collective-permute-start(bf16[1024,256]{1,0:T(8,128)(2,1)S(1)} %get-tuple-element.46), channel_id=1, source_target_pairs={{0,16},{16,32},{32,48},{48,64},{64,80},{80,96},{96,112},{112,128},... | collective-permute-start | bytes 1572872 | tf_op jit(solution)/shard_map/ppermute | solution.py:516
  69.6 1.0 collective-permute-start.11
  70.6 1.9 %collective-permute-start.10 = (bf16[512,256]{1,0:T(8,128)(2,1)S(1)}, bf16[512,256]{1,0:T(8,128)(2,1)S(1)}, u32[]{:S(2)}, u32[]{:S(2)}) collective-permute-start(bf16[512,256]{1,0:T(8,128)(2,1)S(1)} %get-tuple-element.37.refs_8_.att), channel_id=1, source_target_pairs={{0,8},{1,9},{8,0},{9,1},{2,10},{3,11},{10,2},{11,3},{4,12},{5,13},... | collective-permute-start | bytes 786440 | tf_op jit(solution)/shard_map/ppermute | solution.py:478
  72.5 1.4 %collective-permute-start.9 = (bf16[512,256]{1,0:T(8,128)(2,1)S(1)}, bf16[512,256]{1,0:T(8,128)(2,1)S(1)}, u32[]{:S(2)}, u32[]{:S(2)}) collective-permute-start(bf16[512,256]{1,0:T(8,128)(2,1)S(1)} %get-tuple-element.37.refs_8_.att), channel_id=1, source_target_pairs={{0,1},{1,0},{8,9},{9,8},{2,3},{3,2},{10,11},{11,10},{4,5},{5,4},{1... | collective-permute-start | bytes 786440 | tf_op jit(solution)/shard_map/ppermute | solution.py:478
  74.1 6.0 %collective-permute-done.11.refs_11_ = bf16[512,256]{1,0:T(8,128)(2,1)S(1)} collective-permute-done((bf16[512,256]{1,0:T(8,128)(2,1)S(1)}, bf16[512,256]{1,0:T(8,128)(2,1)S(1)}, u32[]{:S(2)}, u32[]{:S(2)}) %collective-permute-start.11) | collective-permute-done | bytes 262176 | tf_op jit(solution)/shard_map/ppermute | solution.py:478
  80.2 5.7 %collective-permute-done.10.refs_10_ = bf16[512,256]{1,0:T(8,128)(2,1)S(1)} collective-permute-done((bf16[512,256]{1,0:T(8,128)(2,1)S(1)}, bf16[512,256]{1,0:T(8,128)(2,1)S(1)}, u32[]{:S(2)}, u32[]{:S(2)}) %collective-permute-start.10) | collective-permute-done | bytes 262176 | tf_op jit(solution)/shard_map/ppermute | solution.py:478
  85.9 2.0 %project.3 = (bf16[320,512]{1,0:T(8,128)(2,1)S(1)}, bf16[320,512]{1,0:T(8,128)(2,1)S(1)}) custom-call(s32[5]{0:T(128)S(1)} %stack.23.ids, bf16[128,1280]{1,0:T(8,128)(2,1)S(1)} %get-tuple-element.33.refs_0_, bf16[128,1280]{1,0:T(8,128)(2,1)S(1)} %collective-permute-done.2.refs_1_, bf16[128,1280]{1,0:T(8,128)(2,1)S(1)} %collective-permute-done.3.refs_2_, ...), custom_call_target="tpu_custom_call" | custom-call | flops 670000000 | bytes 3000000 | tf_op jit(solution)/shard_map/project/pallas_call | solution.py:271
  87.8 6.0 %collective-permute-start.12 = (bf16[320,512]{1,0:T(8,128)(2,1)S(1)}, bf16[320,512]{1,0:T(8,128)(2,1)S(1)}, u32[]{:S(2)}, u32[]{:S(2)}) collective-permute-start(bf16[320,512]{1,0:T(8,128)(2,1)S(1)} %get-tuple-element.39), channel_id=1, source_target_pairs={{0,4},{2,6},{4,0},{6,2},{1,5},{3,7},{5,1},{7,3},{8,12},{10,14},{12... | collective-permute-start | bytes 983048 | tf_op jit(solution)/shard_map/ppermute | solution.py:497
  93.8 1.2 collective-permute-start.13
  95.0 1.9 %project.2 = (bf16[320,512]{1,0:T(8,128)(2,1)S(1)}, bf16[320,512]{1,0:T(8,128)(2,1)S(1)}) custom-call(s32[5]{0:T(128)S(1)} %stack.23.ids, bf16[128,1280]{1,0:T(8,128)(2,1)S(1)} %get-tuple-element.33.refs_0_, bf16[128,1280]{1,0:T(8,128)(2,1)S(1)} %collective-permute-done.2.refs_1_, bf16[128,1280]{1,0:T(8,128)(2,1)S(1)} %collective-permute-done.3.refs_2_, ...), custom_call_target="tpu_custom_call" | custom-call | flops 670000000 | bytes 3000000 | tf_op jit(solution)/shard_map/project/pallas_call | solution.py:271
  98.5 3.9 %collective-permute-start.20 = (bf16[256,320]{1,0:T(8,128)(2,1)S(1)}, bf16[256,320]{1,0:T(8,128)(2,1)S(1)}, u32[]{:S(2)}, u32[]{:S(2)}) collective-permute-start(bf16[256,320]{1,0:T(8,128)(2,1)S(1)} %get-tuple-element.53), channel_id=1, source_target_pairs={{0,96},{32,64},{64,32},{96,0},{1,97},{33,65},{65,33},{97,1},{2,98}... | collective-permute-start | bytes 491528 | tf_op jit(solution)/shard_map/ppermute | solution.py:488
  103.0 20.7 %collective-permute-done.13 = bf16[320,512]{1,0:T(8,128)(2,1)S(1)} collective-permute-done((bf16[320,512]{1,0:T(8,128)(2,1)S(1)}, bf16[320,512]{1,0:T(8,128)(2,1)S(1)}, u32[]{:S(2)}, u32[]{:S(2)}) %collective-permute-start.13) | collective-permute-done | bytes 327712 | tf_op jit(solution)/shard_map/ppermute | solution.py:497
  123.6 0.9 fusion
  124.6 2.3 %gram.1 = (f32[2,1,128,128]{3,2,1,0:T(8,128)}, f32[2,1,320,320]{3,2,1,0:T(8,128)}) custom-call(bf16[256,320]{1,0:T(8,128)(2,1)S(1)} %get-tuple-element.51.refs_0_, bf16[256,320]{1,0:T(8,128)(2,1)S(1)} %collective-permute-done.19.refs_1_, bf16[256,320]{1,0:T(8,128)(2,1)S(1)} %collective-permute-done.20.refs_2_, ...), custom_call_target="tpu_custom_call" | custom-call | flops 400000000 | bytes 2000000 | tf_op jit(solution)/shard_map/gram/pallas_call | solution.py:399
  (35 shorter events, 4.7 us)
Async XLA Ops:
  1.7 10.6 %collective-permute-start.1 = (bf16[512,512]{1,0:T(8,128)(2,1)S(1)}, bf16[512,512]{1,0:T(8,128)(2,1)S(1)}, u32[]{:S(2)}, u32[]{:S(2)}) collective-permute-start(bf16[512,512]{1,0:T(8,128)(2,1)S(1)} %pair_up.1), channel_id=1, source_target_pairs={{16,0},{32,16},{48,32},{64,48},{80,64},{96,80},{112,96},{128,112},... | collective-permute-start | bytes 1572872 | tf_op jit(solution)/shard_map/ppermute | solution.py:459
  4.3 9.2 %collective-permute-start = (bf16[512,512]{1,0:T(8,128)(2,1)S(1)}, bf16[512,512]{1,0:T(8,128)(2,1)S(1)}, u32[]{:S(2)}, u32[]{:S(2)}) collective-permute-start(bf16[512,512]{1,0:T(8,128)(2,1)S(1)} %pair_up.1), channel_id=1, source_target_pairs={{0,16},{16,32},{32,48},{48,64},{64,80},{80,96},{96,112},{112,128},... | collective-permute-start | bytes 1572872 | tf_op jit(solution)/shard_map/ppermute | solution.py:458
  13.5 0.7 copy-start
  20.1 33.9 %copy-start.3 = (bf16[512,5120]{1,0:T(8,128)(2,1)S(1)}, bf16[512,5120]{1,0:T(8,128)(2,1)}, u32[]{:S(2)}) copy-start(bf16[512,5120]{1,0:T(8,128)(2,1)} %up.1) | copy-start | bytes 15728644
  25.2 28.8 %copy-start.2 = (bf16[256,5120]{1,0:T(8,128)(2,1)S(1)}, bf16[256,5120]{1,0:T(8,128)(2,1)}, u32[]{:S(2)}) copy-start(bf16[256,5120]{1,0:T(8,128)(2,1)} %w.1) | copy-start | bytes 7864324
  25.3 47.2 %collective-permute-start.17 = (bf16[256,2560]{1,0:T(8,128)(2,1)S(1)}, bf16[256,2560]{1,0:T(8,128)(2,1)S(1)}, u32[]{:S(2)}, u32[]{:S(2)}) collective-permute-start(bf16[256,2560]{1,0:T(8,128)(2,1)S(1)} %get-tuple-element.48), channel_id=1, source_target_pairs={{0,16},{16,0},{1,17},{17,1},{2,18},{18,2},{3,19},{19,3},{4,20},{20... | collective-permute-start | bytes 3932168 | tf_op jit(solution)/shard_map/ppermute | solution.py:481
  33.7 9.6 %collective-permute-start.2 = (bf16[128,1280]{1,0:T(8,128)(2,1)S(1)}, bf16[128,1280]{1,0:T(8,128)(2,1)S(1)}, u32[]{:S(2)}, u32[]{:S(2)}) collective-permute-start(bf16[128,1280]{1,0:T(8,128)(2,1)S(1)} %get-tuple-element.34), channel_id=1, source_target_pairs={{0,1},{1,0},{8,9},{9,8},{2,3},{3,2},{10,11},{11,10},{4,5},{5,4},{1... | collective-permute-start | bytes 983048 | tf_op jit(solution)/shard_map/ppermute | solution.py:467
  35.4 17.4 %collective-permute-start.3 = (bf16[128,1280]{1,0:T(8,128)(2,1)S(1)}, bf16[128,1280]{1,0:T(8,128)(2,1)S(1)}, u32[]{:S(2)}, u32[]{:S(2)}) collective-permute-start(bf16[128,1280]{1,0:T(8,128)(2,1)S(1)} %get-tuple-element.35), channel_id=1, source_target_pairs={{0,8},{1,9},{8,0},{9,1},{2,10},{3,11},{10,2},{11,3},{4,12},{5,13},... | collective-permute-start | bytes 983048 | tf_op jit(solution)/shard_map/ppermute | solution.py:467
  36.2 17.8 %collective-permute-start.4 = (bf16[128,1280]{1,0:T(8,128)(2,1)S(1)}, bf16[128,1280]{1,0:T(8,128)(2,1)S(1)}, u32[]{:S(2)}, u32[]{:S(2)}) collective-permute-start(bf16[128,1280]{1,0:T(8,128)(2,1)S(1)} %get-tuple-element.36), channel_id=1, source_target_pairs={{0,9},{1,8},{8,1},{9,0},{2,11},{3,10},{10,3},{11,2},{4,13},{5,12},... | collective-permute-start | bytes 983048 | tf_op jit(solution)/shard_map/ppermute | solution.py:467
  38.2 17.5 %copy-start.1 = (s32[32,5]{0,1:T(8,128)S(1)}, s32[32,5]{0,1:T(8,128)}, u32[]{:S(2)}) copy-start(s32[32,5]{0,1:T(8,128)} %param.11) | copy-start | bytes 1924
  38.2 25.8 %collective-permute-start.5 = (bf16[128,1280]{1,0:T(8,128)(2,1)S(1)}, bf16[128,1280]{1,0:T(8,128)(2,1)S(1)}, u32[]{:S(2)}, u32[]{:S(2)}) collective-permute-start(bf16[128,1280]{1,0:T(8,128)(2,1)S(1)} %get-tuple-element.33.refs_0_), channel_id=1, source_target_pairs={{0,16},{16,0},{1,17},{17,1},{2,18},{18,2},{3,19},{19,3},{4,20},{20... | collective-permute-start | bytes 983048 | tf_op jit(solution)/shard_map/ppermute | solution.py:470
  43.2 23.2 %collective-permute-start.6 = (bf16[128,1280]{1,0:T(8,128)(2,1)S(1)}, bf16[128,1280]{1,0:T(8,128)(2,1)S(1)}, u32[]{:S(2)}, u32[]{:S(2)}) collective-permute-start(bf16[128,1280]{1,0:T(8,128)(2,1)S(1)} %collective-permute-done.2.refs_1_), channel_id=1, source_target_pairs={{0,16},{16,0},{1,17},{17,1},{2,18},{18,2},{3,19},{19,3},{4,20},{20... | collective-permute-start | bytes 983048 | tf_op jit(solution)/shard_map/ppermute | solution.py:470
  52.8 16.8 %collective-permute-start.7 = (bf16[128,1280]{1,0:T(8,128)(2,1)S(1)}, bf16[128,1280]{1,0:T(8,128)(2,1)S(1)}, u32[]{:S(2)}, u32[]{:S(2)}) collective-permute-start(bf16[128,1280]{1,0:T(8,128)(2,1)S(1)} %collective-permute-done.3.refs_2_), channel_id=1, source_target_pairs={{0,16},{16,0},{1,17},{17,1},{2,18},{18,2},{3,19},{19,3},{4,20},{20... | collective-permute-start | bytes 983048 | tf_op jit(solution)/shard_map/ppermute | solution.py:470
  54.0 16.5 %collective-permute-start.8 = (bf16[128,1280]{1,0:T(8,128)(2,1)S(1)}, bf16[128,1280]{1,0:T(8,128)(2,1)S(1)}, u32[]{:S(2)}, u32[]{:S(2)}) collective-permute-start(bf16[128,1280]{1,0:T(8,128)(2,1)S(1)} %collective-permute-done.4.refs_3_), channel_id=1, source_target_pairs={{0,16},{16,0},{1,17},{17,1},{2,18},{18,2},{3,19},{19,3},{4,20},{20... | collective-permute-start | bytes 983048 | tf_op jit(solution)/shard_map/ppermute | solution.py:470
  64.0 33.0 %collective-permute-start.15 = (bf16[1024,256]{1,0:T(8,128)(2,1)S(1)}, bf16[1024,256]{1,0:T(8,128)(2,1)S(1)}, u32[]{:S(2)}, u32[]{:S(2)}) collective-permute-start(bf16[1024,256]{1,0:T(8,128)(2,1)S(1)} %get-tuple-element.45), channel_id=1, source_target_pairs={{16,0},{32,16},{48,32},{64,48},{80,64},{96,80},{112,96},{128,112},... | collective-permute-start | bytes 1572872 | tf_op jit(solution)/shard_map/ppermute | solution.py:515
  66.4 30.7 %collective-permute-start.16 = (bf16[1024,256]{1,0:T(8,128)(2,1)S(1)}, bf16[1024,256]{1,0:T(8,128)(2,1)S(1)}, u32[]{:S(2)}, u32[]{:S(2)}) collective-permute-start(bf16[1024,256]{1,0:T(8,128)(2,1)S(1)} %get-tuple-element.46), channel_id=1, source_target_pairs={{0,16},{16,32},{32,48},{48,64},{64,80},{80,96},{96,112},{112,128},... | collective-permute-start | bytes 1572872 | tf_op jit(solution)/shard_map/ppermute | solution.py:516
  69.6 10.6 %collective-permute-start.11 = (bf16[512,256]{1,0:T(8,128)(2,1)S(1)}, bf16[512,256]{1,0:T(8,128)(2,1)S(1)}, u32[]{:S(2)}, u32[]{:S(2)}) collective-permute-start(bf16[512,256]{1,0:T(8,128)(2,1)S(1)} %get-tuple-element.37.refs_8_.att), channel_id=1, source_target_pairs={{0,9},{1,8},{8,1},{9,0},{2,11},{3,10},{10,3},{11,2},{4,13},{5,12},... | collective-permute-start | bytes 786440 | tf_op jit(solution)/shard_map/ppermute | solution.py:478
  70.6 15.3 %collective-permute-start.10 = (bf16[512,256]{1,0:T(8,128)(2,1)S(1)}, bf16[512,256]{1,0:T(8,128)(2,1)S(1)}, u32[]{:S(2)}, u32[]{:S(2)}) collective-permute-start(bf16[512,256]{1,0:T(8,128)(2,1)S(1)} %get-tuple-element.37.refs_8_.att), channel_id=1, source_target_pairs={{0,8},{1,9},{8,0},{9,1},{2,10},{3,11},{10,2},{11,3},{4,12},{5,13},... | collective-permute-start | bytes 786440 | tf_op jit(solution)/shard_map/ppermute | solution.py:478
  72.5 13.4 %collective-permute-start.9 = (bf16[512,256]{1,0:T(8,128)(2,1)S(1)}, bf16[512,256]{1,0:T(8,128)(2,1)S(1)}, u32[]{:S(2)}, u32[]{:S(2)}) collective-permute-start(bf16[512,256]{1,0:T(8,128)(2,1)S(1)} %get-tuple-element.37.refs_8_.att), channel_id=1, source_target_pairs={{0,1},{1,0},{8,9},{9,8},{2,3},{3,2},{10,11},{11,10},{4,5},{5,4},{1... | collective-permute-start | bytes 786440 | tf_op jit(solution)/shard_map/ppermute | solution.py:478
  80.2 17.9 %collective-permute-start.18 = (bf16[256,1280]{1,0:T(8,128)(2,1)S(1)}, bf16[256,1280]{1,0:T(8,128)(2,1)S(1)}, u32[]{:S(2)}, u32[]{:S(2)}) collective-permute-start(bf16[256,1280]{1,0:T(8,128)(2,1)S(1)} %get-tuple-element.50), channel_id=1, source_target_pairs={{0,128},{128,0},{1,129},{129,1},{2,130},{130,2},{3,131},{131,3},{4... | collective-permute-start | bytes 1966088 | tf_op jit(solution)/shard_map/ppermute | solution.py:483
  87.8 14.9 %collective-permute-start.12 = (bf16[320,512]{1,0:T(8,128)(2,1)S(1)}, bf16[320,512]{1,0:T(8,128)(2,1)S(1)}, u32[]{:S(2)}, u32[]{:S(2)}) collective-permute-start(bf16[320,512]{1,0:T(8,128)(2,1)S(1)} %get-tuple-element.39), channel_id=1, source_target_pairs={{0,4},{2,6},{4,0},{6,2},{1,5},{3,7},{5,1},{7,3},{8,12},{10,14},{12... | collective-permute-start | bytes 983048 | tf_op jit(solution)/shard_map/ppermute | solution.py:497
  93.8 29.8 %collective-permute-start.13 = (bf16[320,512]{1,0:T(8,128)(2,1)S(1)}, bf16[320,512]{1,0:T(8,128)(2,1)S(1)}, u32[]{:S(2)}, u32[]{:S(2)}) collective-permute-start(bf16[320,512]{1,0:T(8,128)(2,1)S(1)} %get-tuple-element.40), channel_id=1, source_target_pairs={{0,2},{2,0},{4,6},{6,4},{1,3},{3,1},{5,7},{7,5},{8,10},{10,8},{12,... | collective-permute-start | bytes 983048 | tf_op jit(solution)/shard_map/ppermute | solution.py:497
  97.0 26.7 %collective-permute-start.14 = (bf16[320,512]{1,0:T(8,128)(2,1)S(1)}, bf16[320,512]{1,0:T(8,128)(2,1)S(1)}, u32[]{:S(2)}, u32[]{:S(2)}) collective-permute-start(bf16[320,512]{1,0:T(8,128)(2,1)S(1)} %get-tuple-element.41), channel_id=1, source_target_pairs={{0,6},{2,4},{4,2},{6,0},{1,7},{3,5},{5,3},{7,1},{8,14},{10,12},{12... | collective-permute-start | bytes 983048 | tf_op jit(solution)/shard_map/ppermute | solution.py:497
  98.4 26.1 %collective-permute-start.19 = (bf16[256,320]{1,0:T(8,128)(2,1)S(1)}, bf16[256,320]{1,0:T(8,128)(2,1)S(1)}, u32[]{:S(2)}, u32[]{:S(2)}) collective-permute-start(bf16[256,320]{1,0:T(8,128)(2,1)S(1)} %get-tuple-element.52), channel_id=1, source_target_pairs={{0,64},{32,96},{64,0},{96,32},{1,65},{33,97},{65,1},{97,33},{2,66}... | collective-permute-start | bytes 491528 | tf_op jit(solution)/shard_map/ppermute | solution.py:488
  98.5 26.0 %collective-permute-start.20 = (bf16[256,320]{1,0:T(8,128)(2,1)S(1)}, bf16[256,320]{1,0:T(8,128)(2,1)S(1)}, u32[]{:S(2)}, u32[]{:S(2)}) collective-permute-start(bf16[256,320]{1,0:T(8,128)(2,1)S(1)} %get-tuple-element.53), channel_id=1, source_target_pairs={{0,96},{32,64},{64,32},{96,0},{1,97},{33,65},{65,33},{97,1},{2,98}... | collective-permute-start | bytes 491528 | tf_op jit(solution)/shard_map/ppermute | solution.py:488
  102.7 21.9 %collective-permute-start.21 = (bf16[256,320]{1,0:T(8,128)(2,1)S(1)}, bf16[256,320]{1,0:T(8,128)(2,1)S(1)}, u32[]{:S(2)}, u32[]{:S(2)}) collective-permute-start(bf16[256,320]{1,0:T(8,128)(2,1)S(1)} %get-tuple-element.54), channel_id=1, source_target_pairs={{0,32},{32,0},{64,96},{96,64},{1,33},{33,1},{65,97},{97,65},{2,34}... | collective-permute-start | bytes 491528 | tf_op jit(solution)/shard_map/ppermute | solution.py:488

commit v3 on v2

--- a/solution.py
+++ b/solution.py
@@ -57,40 +57,42 @@
     return (mask[j, tile] == 1) & (key_tile >= 0) & (key_tile < NT)
 
 
-def extend(k, v, before, after, kx, vx):
+def extend(both, before, after, kx, vx):
     head = pl.program_id(0)
     lanes = pl.ds(pl.multiple_of(head * HD, HD), HD)
     value_lanes = pl.ds(pl.multiple_of((2 + head) * HD, HD), HD)
     kx[0:TOK] = before[:, lanes]
-    kx[TOK : 2 * TOK] = k[...]
+    kx[TOK : 2 * TOK] = both[:, lanes]
     kx[2 * TOK : 3 * TOK] = after[:, lanes]
     vx[0:TOK] = before[:, value_lanes]
-    vx[TOK : 2 * TOK] = v[...]
+    vx[TOK : 2 * TOK] = both[:, value_lanes]
     vx[2 * TOK : 3 * TOK] = after[:, value_lanes]
     return lanes
 
 
-def forward_kernel(ids, mask, q, k, v, before, after, att, copy, stat, kx, vx):
+def forward_kernel(ids, mask, q, both, before, after, att, copy, stat, kx, vx):
     head = pl.program_id(0)
-    lanes = extend(k, v, before, after, kx, vx)
+    lanes = extend(both, before, after, kx, vx)
     first_lane = lax.broadcasted_iota(jnp.int32, (8, HD), 1) == 0
     pick = jnp.where(first_lane, jnp.float32(1), jnp.float32(0))
     for i in range(TILES_DEV):
         rows = slice(i * TILE, (i + 1) * TILE)
         parts = []
+        peak = jnp.full((TILE, HD), NEG, jnp.float32)
         for j in range(WIN):
             keys = kx[(i + j) * TILE : (i + j + 1) * TILE]
-            part = dot_nt(q[rows], keys) * jnp.float32(SCALING * LOG2E)
-            parts.append(jnp.where(allowed(ids, mask, i, j), part, jnp.float32(NEG)))
-        peak = parts[0]
-        for part in parts[1:]:
-            peak = jnp.maximum(peak, part)
+            part = dot_nt(q[rows, lanes], keys) * jnp.float32(SCALING * LOG2E)
+            parts.append(part)
+            high = jnp.maximum(part[:, 0:HD], part[:, HD : 2 * HD])
+            high = jnp.where(allowed(ids, mask, i, j), high, jnp.float32(NEG))
+            peak = jnp.maximum(peak, high)
         peak = jnp.max(peak, axis=1, keepdims=True)
         out = jnp.zeros((TILE, HD), jnp.float32)
-        total = jnp.zeros((TILE, TILE), jnp.float32)
+        total = jnp.zeros((TILE, HD), jnp.float32)
         for j in range(WIN):
-            weight = jnp.exp2(parts[j] - peak)
-            total = total + weight
+            level = jnp.where(allowed(ids, mask, i, j), peak, jnp.float32(-NEG))
+            weight = jnp.exp2(parts[j] - level)
+            total = total + (weight[:, 0:HD] + weight[:, HD : 2 * HD])
             values = vx[(i + j) * TILE : (i + j + 1) * TILE]
             out = out + dot_nn(weight.astype(jnp.bfloat16), values)
         total = jnp.sum(total, axis=1, keepdims=True)
@@ -103,10 +105,11 @@
 
 
 def backward_kernel(
-    ids, mask, q, k, v, before, after, grads, att, stat, dq, dl, do, dr, kx, vx, g, dsx, kt
+    ids, mask, queries, both, before, after, grads, att, stat, dq, dl, do, dr, kx, vx, q, g, dsx, kt
 ):
     head = pl.program_id(0)
-    lanes = extend(k, v, before, after, kx, vx)
+    lanes = extend(both, before, after, kx, vx)
+    q[...] = queries[:, lanes]
     g[...] = grads[:, lanes]
     unit = eye(HD)
     for e in range(6):
@@ -152,14 +155,14 @@
     return narrow, whole
 
 
-def attention_forward(ids, mask, q, k, v, before, after):
+def attention_forward(ids, mask, q, both, before, after):
     narrow, whole = attention_specs()
     return pl.pallas_call(
         forward_kernel,
         grid_spec=pltpu.PrefetchScalarGridSpec(
             num_scalar_prefetch=2,
             grid=(2,),
-            in_specs=[narrow] * 3 + [whole] * 2,
+            in_specs=[whole] * 4,
             out_specs=[narrow, whole, whole],
             scratch_shapes=[pltpu.VMEM((3 * TOK, HD), jnp.bfloat16)] * 2,
         ),
@@ -173,20 +176,21 @@
         ),
         compiler_params=pltpu.CompilerParams(vmem_limit_bytes=VMEM_BYTES),
         name="attention_forward",
-    )(ids, mask, q, k, v, before, after)
-
-
-def attention_backward(ids, mask, q, k, v, before, after, g, att, stats):
+    )(ids, mask, q, both, before, after)
+
+
+def attention_backward(ids, mask, q, both, before, after, g, att, stats):
     narrow, whole = attention_specs()
     return pl.pallas_call(
         backward_kernel,
         grid_spec=pltpu.PrefetchScalarGridSpec(
             num_scalar_prefetch=2,
             grid=(2,),
-            in_specs=[narrow] * 3 + [whole] * 5,
+            in_specs=[whole] * 7,
             out_specs=[narrow, whole, whole, whole],
             scratch_shapes=[pltpu.VMEM((3 * TOK, HD), jnp.bfloat16)] * 2
             + [
+                pltpu.VMEM((TOK, HD), jnp.bfloat16),
                 pltpu.VMEM((TOK, HD), jnp.bfloat16),
                 pltpu.VMEM((3 * TOK, TOK), jnp.bfloat16),
                 pltpu.VMEM((HD, 3 * TOK), jnp.bfloat16),
@@ -203,7 +207,7 @@
         ),
         compiler_params=pltpu.CompilerParams(vmem_limit_bytes=VMEM_BYTES),
         name="attention_backward",
-    )(ids, mask, q, k, v, before, after, g, att, stats)
+    )(ids, mask, q, both, before, after, g, att, stats)
 
 
 def pack_kernel(ids, w, o0, o1, o2, o3, buf, strips, sems):
@@ -412,26 +416,32 @@
     )(*parts)
 
 
-def pair_kernel(k, v, out, sems):
-    first = pltpu.make_async_copy(k, out.at[:, 0 : 2 * HD], sems.at[0])
-    second = pltpu.make_async_copy(v, out.at[:, 2 * HD : 4 * HD], sems.at[1])
-    first.start()
-    second.start()
-    first.wait()
-    second.wait()
-
-
-def pair_up(k, v):
+def pair_kernel(q, k, v, queries, both, sems):
+    copies = [
+        pltpu.make_async_copy(k, both.at[:, 0 : 2 * HD], sems.at[0]),
+        pltpu.make_async_copy(v, both.at[:, 2 * HD : 4 * HD], sems.at[1]),
+        pltpu.make_async_copy(q, queries, sems.at[2]),
+    ]
+    for copy in copies:
+        copy.start()
+    for copy in copies:
+        copy.wait()
+
+
+def pair_up(q, k, v):
     return pl.pallas_call(
         pair_kernel,
-        in_specs=[pl.BlockSpec(memory_space=pl.ANY)] * 2,
-        out_specs=pl.BlockSpec(memory_space=pltpu.VMEM),
-        scratch_shapes=[pltpu.SemaphoreType.DMA((2,))],
-        out_shape=jax.ShapeDtypeStruct((TOK, 4 * HD), jnp.bfloat16),
-        cost_estimate=pl.CostEstimate(flops=0, bytes_accessed=1_000_000, transcendentals=0),
+        in_specs=[pl.BlockSpec(memory_space=pl.ANY)] * 3,
+        out_specs=[pl.BlockSpec(memory_space=pltpu.VMEM)] * 2,
+        scratch_shapes=[pltpu.SemaphoreType.DMA((3,))],
+        out_shape=[
+            jax.ShapeDtypeStruct((TOK, 2 * HD), jnp.bfloat16),
+            jax.ShapeDtypeStruct((TOK, 4 * HD), jnp.bfloat16),
+        ],
+        cost_estimate=pl.CostEstimate(flops=0, bytes_accessed=1_500_000, transcendentals=0),
         compiler_params=pltpu.CompilerParams(vmem_limit_bytes=VMEM_BYTES),
         name="pair_up",
-    )(k, v)
+    )(q, k, v)
 
 
 def in_hbm(x):
@@ -454,7 +464,7 @@
     key_states = in_hbm(key_states)
     value_states = in_hbm(value_states)
 
-    both = pair_up(key_states, value_states)
+    queries, both = pair_up(query_states, key_states, value_states)
     before = lax.ppermute(both, FRAME, up)
     after = lax.ppermute(both, FRAME, down)
 
@@ -469,9 +479,7 @@
     for p in range(4):
         strips_other.append(lax.ppermute(strips_mine[p], "core", cores))
 
-    attended, att, stats = attention_forward(
-        ids, mask, query_states, key_states, value_states, before, after
-    )
+    attended, att, stats = attention_forward(ids, mask, queries, both, before, after)
     gathered = [att] * 4
     for p in (3, 2, 1):
         pairs = [(i, i ^ p) for i in range(4)]
@@ -503,9 +511,8 @@
     grad_query, left, own, right = attention_backward(
         ids,
         mask,
-        query_states,
-        key_states,
-        value_states,
+        queries,
+        both,
         before,
         after,
         grad_attended,

time: 127 us -> 125 us (0.984)
  Pallas kernels: 29.5 us -> 27.7 us
  transfers between devices with their start and end apart: 22 -> 22, of which waited for: 8 -> 8; matrix products, arithmetic and copies ran while one was open for 3% -> 3% of each run, Pallas kernels for 12% -> 11%
where the time goes in v3:
time: 125 us
  waiting for transfers between devices  51.2 us (41%)
  starting transfers between devices  41.1 us (33%)
  Pallas kernels  27.7 us (22%)
  local copies, waits for them, and re-layouts  1.61 us (1%)
  matrix products  1.56 us (1%)
    ppermute x3, waiting for transfers between devices, local(): arrived.append(lax.ppermute(partials[place], 'zq', pairs))  20.9 us
    ppermute x3, waiting for transfers between devices, local(): strips_mine[p] = lax.ppermute(strips_mine[p], NEAR, pairs)  12.6 us
    ppermute x3, waiting for transfers between devices, local(): gathered[p] = lax.ppermute(att, NEAR, pairs)  11.7 us
    pallas_call x1, Pallas kernels, attention_backward(): pl.pallas_call(backward_kernel, grid_spec=pltpu.PrefetchScalarGridSpec(nu...  7.36 us
    ppermute x3, starting transfers between devices, local(): arrived.append(lax.ppermute(partials[place], 'zq', pairs))  7.3 us
    ppermute x1, starting transfers between devices, local(): half_near = lax.ppermute(half_other, 'core', cores)  6.21 us
    pallas_call x1, Pallas kernels, weight_grad(): pl.pallas_call(weight_grad_kernel, in_specs=[pl.BlockSpec(memory_space=pl...  5.13 us
    pallas_call x1, Pallas kernels, attention_forward(): pl.pallas_call(forward_kernel, grid_spec=pltpu.PrefetchScalarGridSpec(num...  5.03 us
  transfers between devices with their start and end apart: 22, of which 8 were waited for; matrix products, arithmetic and copies ran while one was open for 3% of the time, Pallas kernels for 11%

profile of v3, /device:TPU:7, one launch (start us, length us, event | category | flops | bytes accessed | tf_op | source)
XLA Modules:
  0.0 125.1 jit_solution(1157229534420439445)
XLA Ops:
  0.6 1.1 pair_up.1
  1.8 2.6 %collective-permute-start.1 = (bf16[512,512]{1,0:T(8,128)(2,1)S(1)}, bf16[512,512]{1,0:T(8,128)(2,1)S(1)}, u32[]{:S(2)}, u32[]{:S(2)}) collective-permute-start(bf16[512,512]{1,0:T(8,128)(2,1)S(1)} %get-tuple-element.35.both), channel_id=1, source_target_pairs={{16,0},{32,16},{48,32},{64,48},{80,64},{96,80},{112,96},{128,112},... | collective-permute-start | bytes 1572872 | tf_op jit(solution)/shard_map/ppermute | solution.py:469
  4.4 3.1 %collective-permute-start = (bf16[512,512]{1,0:T(8,128)(2,1)S(1)}, bf16[512,512]{1,0:T(8,128)(2,1)S(1)}, u32[]{:S(2)}, u32[]{:S(2)}) collective-permute-start(bf16[512,512]{1,0:T(8,128)(2,1)S(1)} %get-tuple-element.35.both), channel_id=1, source_target_pairs={{0,16},{16,32},{32,48},{48,64},{64,80},{80,96},{96,112},{112,128},... | collective-permute-start | bytes 1572872 | tf_op jit(solution)/shard_map/ppermute | solution.py:468
  7.6 4.8 %collective-permute-done.1.after = bf16[512,512]{1,0:T(8,128)(2,1)S(1)} collective-permute-done((bf16[512,512]{1,0:T(8,128)(2,1)S(1)}, bf16[512,512]{1,0:T(8,128)(2,1)S(1)}, u32[]{:S(2)}, u32[]{:S(2)}) %collective-permute-start.1) | collective-permute-done | bytes 524320 | tf_op jit(solution)/shard_map/ppermute | solution.py:469
  12.4 1.2 collective-permute-done.before
  14.3 5.0 %attention_forward.1 = (bf16[512,256]{1,0:T(8,128)(2,1)}, bf16[512,256]{1,0:T(8,128)(2,1)S(1)}, f32[2,8,512]{2,1,0:T(8,128)S(1)}) custom-call(s32[5]{0:T(128)S(1)} %stack.23.ids, s32[5,32]{1,0:T(8,128)S(1)} %bitcast.10, bf16[512,256]{1,0:T(8,128)(2,1)S(1)} %get-tuple-element.34.q.queries, bf16[512,512]{1,0:T(8,128)(2,1)S(1)} %get-tuple-element.35.both, ...), custom_call_target="tpu_custom_call" | custom-call | flops 700000000 | bytes 2400000 | tf_op jit(solution)/shard_map/attention_forward/pallas_call | solution.py:160
  19.3 5.1 %weight_grad.1 = (bf16[256,2560]{1,0:T(8,128)(2,1)S(1)}, bf16[256,2560]{1,0:T(8,128)(2,1)S(1)}) custom-call(s32[5]{0:T(128)S(1)} %stack.23.ids, bf16[512,5120]{1,0:T(8,128)(2,1)} %up.1, bf16[512,256]{1,0:T(8,128)(2,1)S(1)} %get-tuple-element.41.refs_8_.att), custom_call_target="tpu_custom_call" | custom-call | flops 1700000000 | bytes 8000000 | tf_op jit(solution)/shard_map/weight_grad/pallas_call | solution.py:320
  24.4 6.2 %collective-permute-start.17 = (bf16[256,2560]{1,0:T(8,128)(2,1)S(1)}, bf16[256,2560]{1,0:T(8,128)(2,1)S(1)}, u32[]{:S(2)}, u32[]{:S(2)}) collective-permute-start(bf16[256,2560]{1,0:T(8,128)(2,1)S(1)} %get-tuple-element.52), channel_id=1, source_target_pairs={{0,16},{16,0},{1,17},{17,1},{2,18},{18,2},{3,19},{19,3},{4,20},{20... | collective-permute-start | bytes 3932168 | tf_op jit(solution)/shard_map/ppermute | solution.py:489
  30.7 2.2 %pack_weights.1 = (bf16[128,1280]{1,0:T(8,128)(2,1)S(1)}, bf16[128,1280]{1,0:T(8,128)(2,1)S(1)}, bf16[128,1280]{1,0:T(8,128)(2,1)S(1)}, bf16[128,1280]{1,0:T(8,128)(2,1)S(1)}) custom-call(s32[5]{0:T(128)S(1)} %stack.23.ids, bf16[256,5120]{1,0:T(8,128)(2,1)} %w.1), custom_call_target="tpu_custom_call" | custom-call | bytes 2600000 | tf_op jit(solution)/shard_map/pack_weights/pallas_call | solution.py:238
  32.9 1.7 %collective-permute-start.2 = (bf16[128,1280]{1,0:T(8,128)(2,1)S(1)}, bf16[128,1280]{1,0:T(8,128)(2,1)S(1)}, u32[]{:S(2)}, u32[]{:S(2)}) collective-permute-start(bf16[128,1280]{1,0:T(8,128)(2,1)S(1)} %get-tuple-element.38), channel_id=1, source_target_pairs={{0,1},{1,0},{8,9},{9,8},{2,3},{3,2},{10,11},{11,10},{4,5},{5,4},{1... | collective-permute-start | bytes 983048 | tf_op jit(solution)/shard_map/ppermute | solution.py:477
  35.4 2.0 %collective-permute-start.4 = (bf16[128,1280]{1,0:T(8,128)(2,1)S(1)}, bf16[128,1280]{1,0:T(8,128)(2,1)S(1)}, u32[]{:S(2)}, u32[]{:S(2)}) collective-permute-start(bf16[128,1280]{1,0:T(8,128)(2,1)S(1)} %get-tuple-element.40), channel_id=1, source_target_pairs={{0,9},{1,8},{8,1},{9,0},{2,11},{3,10},{10,3},{11,2},{4,13},{5,12},... | collective-permute-start | bytes 983048 | tf_op jit(solution)/shard_map/ppermute | solution.py:477
  38.1 4.3 %collective-permute-done.2.refs_1_ = bf16[128,1280]{1,0:T(8,128)(2,1)S(1)} collective-permute-done((bf16[128,1280]{1,0:T(8,128)(2,1)S(1)}, bf16[128,1280]{1,0:T(8,128)(2,1)S(1)}, u32[]{:S(2)}, u32[]{:S(2)}) %collective-permute-start.2) | collective-permute-done | bytes 327712 | tf_op jit(solution)/shard_map/ppermute | solution.py:477
  42.4 1.2 collective-permute-start.6
  43.7 8.3 %collective-permute-done.3.refs_2_ = bf16[128,1280]{1,0:T(8,128)(2,1)S(1)} collective-permute-done((bf16[128,1280]{1,0:T(8,128)(2,1)S(1)}, bf16[128,1280]{1,0:T(8,128)(2,1)S(1)}, u32[]{:S(2)}, u32[]{:S(2)}) %collective-permute-start.3) | collective-permute-done | bytes 327712 | tf_op jit(solution)/shard_map/ppermute | solution.py:477
  52.0 1.3 %collective-permute-start.7 = (bf16[128,1280]{1,0:T(8,128)(2,1)S(1)}, bf16[128,1280]{1,0:T(8,128)(2,1)S(1)}, u32[]{:S(2)}, u32[]{:S(2)}) collective-permute-start(bf16[128,1280]{1,0:T(8,128)(2,1)S(1)} %collective-permute-done.3.refs_2_), channel_id=1, source_target_pairs={{0,16},{16,0},{1,17},{17,1},{2,18},{18,2},{3,19},{19,3},{4,20},{20... | collective-permute-start | bytes 983048 | tf_op jit(solution)/shard_map/ppermute | solution.py:480
  53.3 1.6 %convolution_convert_fusion.grads = bf16[512,256]{1,0:T(8,128)(2,1)S(1)} fusion(bf16[512,5120]{1,0:T(8,128)(2,1)S(1)} %copy-done.3, bf16[256,5120]{1,0:T(8,128)(2,1)S(1)} %copy-done.2), kind=kOutput, calls=%fused_computation | convolution fusion | flops 1342308352 | bytes 8126464 | tf_op jit(solution)/shard_map/dot_general | solution.py:471
  54.8 7.4 %attention_backward.1 = (bf16[512,256]{1,0:T(8,128)(2,1)}, bf16[1024,256]{1,0:T(8,128)(2,1)S(1)}, f32[1024,256]{1,0:T(8,128)S(1)}, bf16[1024,256]{1,0:T(8,128)(2,1)S(1)}) custom-call(s32[5]{0:T(128)S(1)} %stack.23.ids, s32[5,32]{1,0:T(8,128)S(1)} %bitcast.11, bf16[512,256]{1,0:T(8,128)(2,1)S(1)} %get-tuple-element.34.q.queries, ...), custom_call_target="tpu_custom_call" | custom-call | flops 1800000000 | bytes 5000000 | tf_op jit(solution)/shard_map/attention_backward/pallas_call | solution.py:184
  62.2 2.4 %collective-permute-start.15 = (bf16[1024,256]{1,0:T(8,128)(2,1)S(1)}, bf16[1024,256]{1,0:T(8,128)(2,1)S(1)}, u32[]{:S(2)}, u32[]{:S(2)}) collective-permute-start(bf16[1024,256]{1,0:T(8,128)(2,1)S(1)} %get-tuple-element.49), channel_id=1, source_target_pairs={{16,0},{32,16},{48,32},{64,48},{80,64},{96,80},{112,96},{128,112},... | collective-permute-start | bytes 1572872 | tf_op jit(solution)/shard_map/ppermute | solution.py:522
  64.6 3.2 %collective-permute-start.16 = (bf16[1024,256]{1,0:T(8,128)(2,1)S(1)}, bf16[1024,256]{1,0:T(8,128)(2,1)S(1)}, u32[]{:S(2)}, u32[]{:S(2)}) collective-permute-start(bf16[1024,256]{1,0:T(8,128)(2,1)S(1)} %get-tuple-element.50), channel_id=1, source_target_pairs={{0,16},{16,32},{32,48},{48,64},{64,80},{80,96},{96,112},{112,128},... | collective-permute-start | bytes 1572872 | tf_op jit(solution)/shard_map/ppermute | solution.py:523
  67.8 1.0 collective-permute-start.11
  68.8 1.9 %collective-permute-start.10 = (bf16[512,256]{1,0:T(8,128)(2,1)S(1)}, bf16[512,256]{1,0:T(8,128)(2,1)S(1)}, u32[]{:S(2)}, u32[]{:S(2)}) collective-permute-start(bf16[512,256]{1,0:T(8,128)(2,1)S(1)} %get-tuple-element.41.refs_8_.att), channel_id=1, source_target_pairs={{0,8},{1,9},{8,0},{9,1},{2,10},{3,11},{10,2},{11,3},{4,12},{5,13},... | collective-permute-start | bytes 786440 | tf_op jit(solution)/shard_map/ppermute | solution.py:486
  70.7 1.4 %collective-permute-start.9 = (bf16[512,256]{1,0:T(8,128)(2,1)S(1)}, bf16[512,256]{1,0:T(8,128)(2,1)S(1)}, u32[]{:S(2)}, u32[]{:S(2)}) collective-permute-start(bf16[512,256]{1,0:T(8,128)(2,1)S(1)} %get-tuple-element.41.refs_8_.att), channel_id=1, source_target_pairs={{0,1},{1,0},{8,9},{9,8},{2,3},{3,2},{10,11},{11,10},{4,5},{5,4},{1... | collective-permute-start | bytes 786440 | tf_op jit(solution)/shard_map/ppermute | solution.py:486
  72.3 6.0 %collective-permute-done.11.refs_11_ = bf16[512,256]{1,0:T(8,128)(2,1)S(1)} collective-permute-done((bf16[512,256]{1,0:T(8,128)(2,1)S(1)}, bf16[512,256]{1,0:T(8,128)(2,1)S(1)}, u32[]{:S(2)}, u32[]{:S(2)}) %collective-permute-start.11) | collective-permute-done | bytes 262176 | tf_op jit(solution)/shard_map/ppermute | solution.py:486
  78.4 5.7 %collective-permute-done.10.refs_10_ = bf16[512,256]{1,0:T(8,128)(2,1)S(1)} collective-permute-done((bf16[512,256]{1,0:T(8,128)(2,1)S(1)}, bf16[512,256]{1,0:T(8,128)(2,1)S(1)}, u32[]{:S(2)}, u32[]{:S(2)}) %collective-permute-start.10) | collective-permute-done | bytes 262176 | tf_op jit(solution)/shard_map/ppermute | solution.py:486
  84.0 2.0 %project.3 = (bf16[320,512]{1,0:T(8,128)(2,1)S(1)}, bf16[320,512]{1,0:T(8,128)(2,1)S(1)}) custom-call(s32[5]{0:T(128)S(1)} %stack.23.ids, bf16[128,1280]{1,0:T(8,128)(2,1)S(1)} %get-tuple-element.37.refs_0_, bf16[128,1280]{1,0:T(8,128)(2,1)S(1)} %collective-permute-done.2.refs_1_, bf16[128,1280]{1,0:T(8,128)(2,1)S(1)} %collective-permute-done.3.refs_2_, ...), custom_call_target="tpu_custom_call" | custom-call | flops 670000000 | bytes 3000000 | tf_op jit(solution)/shard_map/project/pallas_call | solution.py:275
  86.0 6.0 %collective-permute-start.12 = (bf16[320,512]{1,0:T(8,128)(2,1)S(1)}, bf16[320,512]{1,0:T(8,128)(2,1)S(1)}, u32[]{:S(2)}, u32[]{:S(2)}) collective-permute-start(bf16[320,512]{1,0:T(8,128)(2,1)S(1)} %get-tuple-element.43), channel_id=1, source_target_pairs={{0,4},{2,6},{4,0},{6,2},{1,5},{3,7},{5,1},{7,3},{8,12},{10,14},{12... | collective-permute-start | bytes 983048 | tf_op jit(solution)/shard_map/ppermute | solution.py:505
  92.0 1.2 collective-permute-start.13
  93.2 2.0 %project.2 = (bf16[320,512]{1,0:T(8,128)(2,1)S(1)}, bf16[320,512]{1,0:T(8,128)(2,1)S(1)}) custom-call(s32[5]{0:T(128)S(1)} %stack.23.ids, bf16[128,1280]{1,0:T(8,128)(2,1)S(1)} %get-tuple-element.37.refs_0_, bf16[128,1280]{1,0:T(8,128)(2,1)S(1)} %collective-permute-done.2.refs_1_, bf16[128,1280]{1,0:T(8,128)(2,1)S(1)} %collective-permute-done.3.refs_2_, ...), custom_call_target="tpu_custom_call" | custom-call | flops 670000000 | bytes 3000000 | tf_op jit(solution)/shard_map/project/pallas_call | solution.py:275
  96.7 3.9 %collective-permute-start.20 = (bf16[256,320]{1,0:T(8,128)(2,1)S(1)}, bf16[256,320]{1,0:T(8,128)(2,1)S(1)}, u32[]{:S(2)}, u32[]{:S(2)}) collective-permute-start(bf16[256,320]{1,0:T(8,128)(2,1)S(1)} %get-tuple-element.57), channel_id=1, source_target_pairs={{0,96},{32,64},{64,32},{96,0},{1,97},{33,65},{65,33},{97,1},{2,98}... | collective-permute-start | bytes 491528 | tf_op jit(solution)/shard_map/ppermute | solution.py:496
  101.1 20.7 %collective-permute-done.13 = bf16[320,512]{1,0:T(8,128)(2,1)S(1)} collective-permute-done((bf16[320,512]{1,0:T(8,128)(2,1)S(1)}, bf16[320,512]{1,0:T(8,128)(2,1)S(1)}, u32[]{:S(2)}, u32[]{:S(2)}) %collective-permute-start.13) | collective-permute-done | bytes 327712 | tf_op jit(solution)/shard_map/ppermute | solution.py:505
  121.8 0.9 fusion
  122.7 2.3 %gram.1 = (f32[2,1,128,128]{3,2,1,0:T(8,128)}, f32[2,1,320,320]{3,2,1,0:T(8,128)}) custom-call(bf16[256,320]{1,0:T(8,128)(2,1)S(1)} %get-tuple-element.55.refs_0_, bf16[256,320]{1,0:T(8,128)(2,1)S(1)} %collective-permute-done.19.refs_1_, bf16[256,320]{1,0:T(8,128)(2,1)S(1)} %collective-permute-done.20.refs_2_, ...), custom_call_target="tpu_custom_call" | custom-call | flops 400000000 | bytes 2000000 | tf_op jit(solution)/shard_map/gram/pallas_call | solution.py:403
  (35 shorter events, 4.6 us)
Async XLA Ops:
  1.8 10.6 %collective-permute-start.1 = (bf16[512,512]{1,0:T(8,128)(2,1)S(1)}, bf16[512,512]{1,0:T(8,128)(2,1)S(1)}, u32[]{:S(2)}, u32[]{:S(2)}) collective-permute-start(bf16[512,512]{1,0:T(8,128)(2,1)S(1)} %get-tuple-element.35.both), channel_id=1, source_target_pairs={{16,0},{32,16},{48,32},{64,48},{80,64},{96,80},{112,96},{128,112},... | collective-permute-start | bytes 1572872 | tf_op jit(solution)/shard_map/ppermute | solution.py:469
  4.4 9.2 %collective-permute-start = (bf16[512,512]{1,0:T(8,128)(2,1)S(1)}, bf16[512,512]{1,0:T(8,128)(2,1)S(1)}, u32[]{:S(2)}, u32[]{:S(2)}) collective-permute-start(bf16[512,512]{1,0:T(8,128)(2,1)S(1)} %get-tuple-element.35.both), channel_id=1, source_target_pairs={{0,16},{16,32},{32,48},{48,64},{64,80},{80,96},{96,112},{112,128},... | collective-permute-start | bytes 1572872 | tf_op jit(solution)/shard_map/ppermute | solution.py:468
  13.6 0.7 copy-start
  19.3 34.0 %copy-start.3 = (bf16[512,5120]{1,0:T(8,128)(2,1)S(1)}, bf16[512,5120]{1,0:T(8,128)(2,1)}, u32[]{:S(2)}) copy-start(bf16[512,5120]{1,0:T(8,128)(2,1)} %up.1) | copy-start | bytes 15728644
  24.4 28.8 %copy-start.2 = (bf16[256,5120]{1,0:T(8,128)(2,1)S(1)}, bf16[256,5120]{1,0:T(8,128)(2,1)}, u32[]{:S(2)}) copy-start(bf16[256,5120]{1,0:T(8,128)(2,1)} %w.1) | copy-start | bytes 7864324
  24.4 46.2 %collective-permute-start.17 = (bf16[256,2560]{1,0:T(8,128)(2,1)S(1)}, bf16[256,2560]{1,0:T(8,128)(2,1)S(1)}, u32[]{:S(2)}, u32[]{:S(2)}) collective-permute-start(bf16[256,2560]{1,0:T(8,128)(2,1)S(1)} %get-tuple-element.52), channel_id=1, source_target_pairs={{0,16},{16,0},{1,17},{17,1},{2,18},{18,2},{3,19},{19,3},{4,20},{20... | collective-permute-start | bytes 3932168 | tf_op jit(solution)/shard_map/ppermute | solution.py:489
  32.9 9.6 %collective-permute-start.2 = (bf16[128,1280]{1,0:T(8,128)(2,1)S(1)}, bf16[128,1280]{1,0:T(8,128)(2,1)S(1)}, u32[]{:S(2)}, u32[]{:S(2)}) collective-permute-start(bf16[128,1280]{1,0:T(8,128)(2,1)S(1)} %get-tuple-element.38), channel_id=1, source_target_pairs={{0,1},{1,0},{8,9},{9,8},{2,3},{3,2},{10,11},{11,10},{4,5},{5,4},{1... | collective-permute-start | bytes 983048 | tf_op jit(solution)/shard_map/ppermute | solution.py:477
  34.6 17.4 %collective-permute-start.3 = (bf16[128,1280]{1,0:T(8,128)(2,1)S(1)}, bf16[128,1280]{1,0:T(8,128)(2,1)S(1)}, u32[]{:S(2)}, u32[]{:S(2)}) collective-permute-start(bf16[128,1280]{1,0:T(8,128)(2,1)S(1)} %get-tuple-element.39), channel_id=1, source_target_pairs={{0,8},{1,9},{8,0},{9,1},{2,10},{3,11},{10,2},{11,3},{4,12},{5,13},... | collective-permute-start | bytes 983048 | tf_op jit(solution)/shard_map/ppermute | solution.py:477
  35.4 17.8 %collective-permute-start.4 = (bf16[128,1280]{1,0:T(8,128)(2,1)S(1)}, bf16[128,1280]{1,0:T(8,128)(2,1)S(1)}, u32[]{:S(2)}, u32[]{:S(2)}) collective-permute-start(bf16[128,1280]{1,0:T(8,128)(2,1)S(1)} %get-tuple-element.40), channel_id=1, source_target_pairs={{0,9},{1,8},{8,1},{9,0},{2,11},{3,10},{10,3},{11,2},{4,13},{5,12},... | collective-permute-start | bytes 983048 | tf_op jit(solution)/shard_map/ppermute | solution.py:477
  37.4 17.5 %copy-start.1 = (s32[32,5]{0,1:T(8,128)S(1)}, s32[32,5]{0,1:T(8,128)}, u32[]{:S(2)}) copy-start(s32[32,5]{0,1:T(8,128)} %param.11) | copy-start | bytes 1924
  37.4 24.8 %collective-permute-start.5 = (bf16[128,1280]{1,0:T(8,128)(2,1)S(1)}, bf16[128,1280]{1,0:T(8,128)(2,1)S(1)}, u32[]{:S(2)}, u32[]{:S(2)}) collective-permute-start(bf16[128,1280]{1,0:T(8,128)(2,1)S(1)} %get-tuple-element.37.refs_0_), channel_id=1, source_target_pairs={{0,16},{16,0},{1,17},{17,1},{2,18},{18,2},{3,19},{19,3},{4,20},{20... | collective-permute-start | bytes 983048 | tf_op jit(solution)/shard_map/ppermute | solution.py:480
  42.4 22.2 %collective-permute-start.6 = (bf16[128,1280]{1,0:T(8,128)(2,1)S(1)}, bf16[128,1280]{1,0:T(8,128)(2,1)S(1)}, u32[]{:S(2)}, u32[]{:S(2)}) collective-permute-start(bf16[128,1280]{1,0:T(8,128)(2,1)S(1)} %collective-permute-done.2.refs_1_), channel_id=1, source_target_pairs={{0,16},{16,0},{1,17},{17,1},{2,18},{18,2},{3,19},{19,3},{4,20},{20... | collective-permute-start | bytes 983048 | tf_op jit(solution)/shard_map/ppermute | solution.py:480
  52.0 15.8 %collective-permute-start.7 = (bf16[128,1280]{1,0:T(8,128)(2,1)S(1)}, bf16[128,1280]{1,0:T(8,128)(2,1)S(1)}, u32[]{:S(2)}, u32[]{:S(2)}) collective-permute-start(bf16[128,1280]{1,0:T(8,128)(2,1)S(1)} %collective-permute-done.3.refs_2_), channel_id=1, source_target_pairs={{0,16},{16,0},{1,17},{17,1},{2,18},{18,2},{3,19},{19,3},{4,20},{20... | collective-permute-start | bytes 983048 | tf_op jit(solution)/shard_map/ppermute | solution.py:480
  53.2 15.5 %collective-permute-start.8 = (bf16[128,1280]{1,0:T(8,128)(2,1)S(1)}, bf16[128,1280]{1,0:T(8,128)(2,1)S(1)}, u32[]{:S(2)}, u32[]{:S(2)}) collective-permute-start(bf16[128,1280]{1,0:T(8,128)(2,1)S(1)} %collective-permute-done.4.refs_3_), channel_id=1, source_target_pairs={{0,16},{16,0},{1,17},{17,1},{2,18},{18,2},{3,19},{19,3},{4,20},{20... | collective-permute-start | bytes 983048 | tf_op jit(solution)/shard_map/ppermute | solution.py:480
  62.2 33.0 %collective-permute-start.15 = (bf16[1024,256]{1,0:T(8,128)(2,1)S(1)}, bf16[1024,256]{1,0:T(8,128)(2,1)S(1)}, u32[]{:S(2)}, u32[]{:S(2)}) collective-permute-start(bf16[1024,256]{1,0:T(8,128)(2,1)S(1)} %get-tuple-element.49), channel_id=1, source_target_pairs={{16,0},{32,16},{48,32},{64,48},{80,64},{96,80},{112,96},{128,112},... | collective-permute-start | bytes 1572872 | tf_op jit(solution)/shard_map/ppermute | solution.py:522
  64.6 30.7 %collective-permute-start.16 = (bf16[1024,256]{1,0:T(8,128)(2,1)S(1)}, bf16[1024,256]{1,0:T(8,128)(2,1)S(1)}, u32[]{:S(2)}, u32[]{:S(2)}) collective-permute-start(bf16[1024,256]{1,0:T(8,128)(2,1)S(1)} %get-tuple-element.50), channel_id=1, source_target_pairs={{0,16},{16,32},{32,48},{48,64},{64,80},{80,96},{96,112},{112,128},... | collective-permute-start | bytes 1572872 | tf_op jit(solution)/shard_map/ppermute | solution.py:523
  67.8 10.6 %collective-permute-start.11 = (bf16[512,256]{1,0:T(8,128)(2,1)S(1)}, bf16[512,256]{1,0:T(8,128)(2,1)S(1)}, u32[]{:S(2)}, u32[]{:S(2)}) collective-permute-start(bf16[512,256]{1,0:T(8,128)(2,1)S(1)} %get-tuple-element.41.refs_8_.att), channel_id=1, source_target_pairs={{0,9},{1,8},{8,1},{9,0},{2,11},{3,10},{10,3},{11,2},{4,13},{5,12},... | collective-permute-start | bytes 786440 | tf_op jit(solution)/shard_map/ppermute | solution.py:486
  68.8 15.3 %collective-permute-start.10 = (bf16[512,256]{1,0:T(8,128)(2,1)S(1)}, bf16[512,256]{1,0:T(8,128)(2,1)S(1)}, u32[]{:S(2)}, u32[]{:S(2)}) collective-permute-start(bf16[512,256]{1,0:T(8,128)(2,1)S(1)} %get-tuple-element.41.refs_8_.att), channel_id=1, source_target_pairs={{0,8},{1,9},{8,0},{9,1},{2,10},{3,11},{10,2},{11,3},{4,12},{5,13},... | collective-permute-start | bytes 786440 | tf_op jit(solution)/shard_map/ppermute | solution.py:486
  70.7 13.4 %collective-permute-start.9 = (bf16[512,256]{1,0:T(8,128)(2,1)S(1)}, bf16[512,256]{1,0:T(8,128)(2,1)S(1)}, u32[]{:S(2)}, u32[]{:S(2)}) collective-permute-start(bf16[512,256]{1,0:T(8,128)(2,1)S(1)} %get-tuple-element.41.refs_8_.att), channel_id=1, source_target_pairs={{0,1},{1,0},{8,9},{9,8},{2,3},{3,2},{10,11},{11,10},{4,5},{5,4},{1... | collective-permute-start | bytes 786440 | tf_op jit(solution)/shard_map/ppermute | solution.py:486
  78.3 17.9 %collective-permute-start.18 = (bf16[256,1280]{1,0:T(8,128)(2,1)S(1)}, bf16[256,1280]{1,0:T(8,128)(2,1)S(1)}, u32[]{:S(2)}, u32[]{:S(2)}) collective-permute-start(bf16[256,1280]{1,0:T(8,128)(2,1)S(1)} %get-tuple-element.54), channel_id=1, source_target_pairs={{0,128},{128,0},{1,129},{129,1},{2,130},{130,2},{3,131},{131,3},{4... | collective-permute-start | bytes 1966088 | tf_op jit(solution)/shard_map/ppermute | solution.py:491
  86.0 14.8 %collective-permute-start.12 = (bf16[320,512]{1,0:T(8,128)(2,1)S(1)}, bf16[320,512]{1,0:T(8,128)(2,1)S(1)}, u32[]{:S(2)}, u32[]{:S(2)}) collective-permute-start(bf16[320,512]{1,0:T(8,128)(2,1)S(1)} %get-tuple-element.43), channel_id=1, source_target_pairs={{0,4},{2,6},{4,0},{6,2},{1,5},{3,7},{5,1},{7,3},{8,12},{10,14},{12... | collective-permute-start | bytes 983048 | tf_op jit(solution)/shard_map/ppermute | solution.py:505
  92.0 29.8 %collective-permute-start.13 = (bf16[320,512]{1,0:T(8,128)(2,1)S(1)}, bf16[320,512]{1,0:T(8,128)(2,1)S(1)}, u32[]{:S(2)}, u32[]{:S(2)}) collective-permute-start(bf16[320,512]{1,0:T(8,128)(2,1)S(1)} %get-tuple-element.44), channel_id=1, source_target_pairs={{0,2},{2,0},{4,6},{6,4},{1,3},{3,1},{5,7},{7,5},{8,10},{10,8},{12,... | collective-permute-start | bytes 983048 | tf_op jit(solution)/shard_map/ppermute | solution.py:505
  95.2 26.7 %collective-permute-start.14 = (bf16[320,512]{1,0:T(8,128)(2,1)S(1)}, bf16[320,512]{1,0:T(8,128)(2,1)S(1)}, u32[]{:S(2)}, u32[]{:S(2)}) collective-permute-start(bf16[320,512]{1,0:T(8,128)(2,1)S(1)} %get-tuple-element.45), channel_id=1, source_target_pairs={{0,6},{2,4},{4,2},{6,0},{1,7},{3,5},{5,3},{7,1},{8,14},{10,12},{12... | collective-permute-start | bytes 983048 | tf_op jit(solution)/shard_map/ppermute | solution.py:505
  96.6 26.1 %collective-permute-start.19 = (bf16[256,320]{1,0:T(8,128)(2,1)S(1)}, bf16[256,320]{1,0:T(8,128)(2,1)S(1)}, u32[]{:S(2)}, u32[]{:S(2)}) collective-permute-start(bf16[256,320]{1,0:T(8,128)(2,1)S(1)} %get-tuple-element.56), channel_id=1, source_target_pairs={{0,64},{32,96},{64,0},{96,32},{1,65},{33,97},{65,1},{97,33},{2,66}... | collective-permute-start | bytes 491528 | tf_op jit(solution)/shard_map/ppermute | solution.py:496
  96.7 26.0 %collective-permute-start.20 = (bf16[256,320]{1,0:T(8,128)(2,1)S(1)}, bf16[256,320]{1,0:T(8,128)(2,1)S(1)}, u32[]{:S(2)}, u32[]{:S(2)}) collective-permute-start(bf16[256,320]{1,0:T(8,128)(2,1)S(1)} %get-tuple-element.57), channel_id=1, source_target_pairs={{0,96},{32,64},{64,32},{96,0},{1,97},{33,65},{65,33},{97,1},{2,98}... | collective-permute-start | bytes 491528 | tf_op jit(solution)/shard_map/ppermute | solution.py:496
  100.8 21.9 %collective-permute-start.21 = (bf16[256,320]{1,0:T(8,128)(2,1)S(1)}, bf16[256,320]{1,0:T(8,128)(2,1)S(1)}, u32[]{:S(2)}, u32[]{:S(2)}) collective-permute-start(bf16[256,320]{1,0:T(8,128)(2,1)S(1)} %get-tuple-element.58), channel_id=1, source_target_pairs={{0,32},{32,0},{64,96},{96,64},{1,33},{33,1},{65,97},{97,65},{2,34}... | collective-permute-start | bytes 491528 | tf_op jit(solution)/shard_map/ppermute | solution.py:496

commit v4 on v3

--- a/solution.py
+++ b/solution.py
@@ -416,6 +416,27 @@
     )(*parts)
 
 
+def settle_kernel(own, first, second, dk, dv):
+    total = own[...] + first[...].astype(jnp.float32) + second[...].astype(jnp.float32)
+    dk[...] = total[0:TOK].astype(jnp.bfloat16)
+    dv[...] = total[TOK : 2 * TOK].astype(jnp.bfloat16)
+
+
+def settle(own, first, second):
+    whole = pl.BlockSpec(memory_space=pltpu.VMEM)
+    return pl.pallas_call(
+        settle_kernel,
+        in_specs=[whole] * 3,
+        out_specs=[whole] * 2,
+        out_shape=[jax.ShapeDtypeStruct((TOK, 2 * HD), jnp.bfloat16)] * 2,
+        cost_estimate=pl.CostEstimate(
+            flops=1_000_000, bytes_accessed=3_000_000, transcendentals=0
+        ),
+        compiler_params=pltpu.CompilerParams(vmem_limit_bytes=VMEM_BYTES),
+        name="settle",
+    )(own, first, second)
+
+
 def pair_kernel(q, k, v, queries, both, sems):
     copies = [
         pltpu.make_async_copy(k, both.at[:, 0 : 2 * HD], sems.at[0]),
@@ -521,9 +542,7 @@
     )
     from_right = lax.ppermute(left, FRAME, down)
     from_left = lax.ppermute(right, FRAME, up)
-    summed = own + from_right.astype(jnp.float32) + from_left.astype(jnp.float32)
-    grad_key = summed[:TOK].astype(jnp.bfloat16)
-    grad_value = summed[TOK:].astype(jnp.bfloat16)
+    grad_key, grad_value = settle(own, from_right, from_left)
 
     gram_left, gram_right = gram(grad_parts)
     return (attended, projected, grad_query, grad_key, grad_value, gram_left, gram_right)

time: 125 us -> 123 us (0.984)
  waiting for transfers between devices: 51.2 us -> 49.8 us
    ppermute x3, waiting for transfers between devices: 11.7 us -> 8.65 us  [local(): gathered[p] = lax.ppermute(att, NEAR, pairs)]
    ppermute x3, starting transfers between devices: 4.33 us -> 2.71 us  [local(): grad_parts.append(lax.ppermute(quarters[p], 'y', pairs))]
    ppermute x3, waiting for transfers between devices: 20.9 us -> 22.5 us  [local(): arrived.append(lax.ppermute(partials[place], 'zq', pairs))]
    ppermute x3, starting transfers between devices: 7.3 us -> 8.56 us  [local(): arrived.append(lax.ppermute(partials[place], 'zq', pairs))]
  transfers between devices with their start and end apart: 22 -> 22, of which waited for: 8 -> 7; matrix products, arithmetic and copies ran while one was open for 3% -> 2% of each run, Pallas kernels for 11% -> 12%
where the time goes in v4:
time: 123 us; the launch traced here: 122 us
  waiting for transfers between devices  49.8 us (40%)
  starting transfers between devices  40 us (33%)
  Pallas kernels  28.6 us (23%)
  matrix products  1.55 us (1%)
    ppermute x3, waiting for transfers between devices, local(): arrived.append(lax.ppermute(partials[place], 'zq', pairs))  22.5 us
    ppermute x3, waiting for transfers between devices, local(): strips_mine[p] = lax.ppermute(strips_mine[p], NEAR, pairs)  12.6 us
    ppermute x3, waiting for transfers between devices, local(): gathered[p] = lax.ppermute(att, NEAR, pairs)  8.65 us
    ppermute x3, starting transfers between devices, local(): arrived.append(lax.ppermute(partials[place], 'zq', pairs))  8.56 us
    pallas_call x1, Pallas kernels, attention_backward(): pl.pallas_call(backward_kernel, grid_spec=pltpu.PrefetchScalarGridSpec(nu...  7.34 us
    ppermute x1, starting transfers between devices, local(): half_near = lax.ppermute(half_other, 'core', cores)  6.21 us
    pallas_call x1, Pallas kernels, weight_grad(): pl.pallas_call(weight_grad_kernel, in_specs=[pl.BlockSpec(memory_space=pl...  5.13 us
    pallas_call x1, Pallas kernels, attention_forward(): pl.pallas_call(forward_kernel, grid_spec=pltpu.PrefetchScalarGridSpec(num...  5.03 us
  transfers between devices with their start and end apart: 22, of which 7 were waited for; matrix products, arithmetic and copies ran while one was open for 2% of the time, Pallas kernels for 12%

profile of v4, /device:TPU:7, one launch (start us, length us, event | category | flops | bytes accessed | tf_op | source)
XLA Modules:
  0.0 122.4 jit_solution(12458222915541748354)
XLA Ops:
  0.6 1.1 pair_up.1
  1.8 2.6 %collective-permute-start.1 = (bf16[512,512]{1,0:T(8,128)(2,1)S(1)}, bf16[512,512]{1,0:T(8,128)(2,1)S(1)}, u32[]{:S(2)}, u32[]{:S(2)}) collective-permute-start(bf16[512,512]{1,0:T(8,128)(2,1)S(1)} %get-tuple-element.37.both), channel_id=1, source_target_pairs={{16,0},{32,16},{48,32},{64,48},{80,64},{96,80},{112,96},{128,112},... | collective-permute-start | bytes 1572872 | tf_op jit(solution)/shard_map/ppermute | solution.py:490
  4.4 3.1 %collective-permute-start = (bf16[512,512]{1,0:T(8,128)(2,1)S(1)}, bf16[512,512]{1,0:T(8,128)(2,1)S(1)}, u32[]{:S(2)}, u32[]{:S(2)}) collective-permute-start(bf16[512,512]{1,0:T(8,128)(2,1)S(1)} %get-tuple-element.37.both), channel_id=1, source_target_pairs={{0,16},{16,32},{32,48},{48,64},{64,80},{80,96},{96,112},{112,128},... | collective-permute-start | bytes 1572872 | tf_op jit(solution)/shard_map/ppermute | solution.py:489
  7.6 4.8 %collective-permute-done.1.after = bf16[512,512]{1,0:T(8,128)(2,1)S(1)} collective-permute-done((bf16[512,512]{1,0:T(8,128)(2,1)S(1)}, bf16[512,512]{1,0:T(8,128)(2,1)S(1)}, u32[]{:S(2)}, u32[]{:S(2)}) %collective-permute-start.1) | collective-permute-done | bytes 524320 | tf_op jit(solution)/shard_map/ppermute | solution.py:490
  12.4 1.2 collective-permute-done.before
  14.3 5.0 %attention_forward.1 = (bf16[512,256]{1,0:T(8,128)(2,1)}, bf16[512,256]{1,0:T(8,128)(2,1)S(1)}, f32[2,8,512]{2,1,0:T(8,128)S(1)}) custom-call(s32[5]{0:T(128)S(1)} %stack.23.ids, s32[5,32]{1,0:T(8,128)S(1)} %bitcast.10, bf16[512,256]{1,0:T(8,128)(2,1)S(1)} %get-tuple-element.36.q.queries, bf16[512,512]{1,0:T(8,128)(2,1)S(1)} %get-tuple-element.37.both, ...), custom_call_target="tpu_custom_call" | custom-call | flops 700000000 | bytes 2400000 | tf_op jit(solution)/shard_map/attention_forward/pallas_call | solution.py:160
  19.3 5.1 %weight_grad.1 = (bf16[256,2560]{1,0:T(8,128)(2,1)S(1)}, bf16[256,2560]{1,0:T(8,128)(2,1)S(1)}) custom-call(s32[5]{0:T(128)S(1)} %stack.23.ids, bf16[512,5120]{1,0:T(8,128)(2,1)} %up.1, bf16[512,256]{1,0:T(8,128)(2,1)S(1)} %get-tuple-element.43.refs_8_.att), custom_call_target="tpu_custom_call" | custom-call | flops 1700000000 | bytes 8000000 | tf_op jit(solution)/shard_map/weight_grad/pallas_call | solution.py:320
  24.4 6.2 %collective-permute-start.17 = (bf16[256,2560]{1,0:T(8,128)(2,1)S(1)}, bf16[256,2560]{1,0:T(8,128)(2,1)S(1)}, u32[]{:S(2)}, u32[]{:S(2)}) collective-permute-start(bf16[256,2560]{1,0:T(8,128)(2,1)S(1)} %get-tuple-element.56), channel_id=1, source_target_pairs={{0,16},{16,0},{1,17},{17,1},{2,18},{18,2},{3,19},{19,3},{4,20},{20... | collective-permute-start | bytes 3932168 | tf_op jit(solution)/shard_map/ppermute | solution.py:510
  30.7 2.2 %pack_weights.1 = (bf16[128,1280]{1,0:T(8,128)(2,1)S(1)}, bf16[128,1280]{1,0:T(8,128)(2,1)S(1)}, bf16[128,1280]{1,0:T(8,128)(2,1)S(1)}, bf16[128,1280]{1,0:T(8,128)(2,1)S(1)}) custom-call(s32[5]{0:T(128)S(1)} %stack.23.ids, bf16[256,5120]{1,0:T(8,128)(2,1)} %w.1), custom_call_target="tpu_custom_call" | custom-call | bytes 2600000 | tf_op jit(solution)/shard_map/pack_weights/pallas_call | solution.py:238
  32.9 1.7 %collective-permute-start.2 = (bf16[128,1280]{1,0:T(8,128)(2,1)S(1)}, bf16[128,1280]{1,0:T(8,128)(2,1)S(1)}, u32[]{:S(2)}, u32[]{:S(2)}) collective-permute-start(bf16[128,1280]{1,0:T(8,128)(2,1)S(1)} %get-tuple-element.40), channel_id=1, source_target_pairs={{0,1},{1,0},{8,9},{9,8},{2,3},{3,2},{10,11},{11,10},{4,5},{5,4},{1... | collective-permute-start | bytes 983048 | tf_op jit(solution)/shard_map/ppermute | solution.py:498
  35.4 2.0 %collective-permute-start.4 = (bf16[128,1280]{1,0:T(8,128)(2,1)S(1)}, bf16[128,1280]{1,0:T(8,128)(2,1)S(1)}, u32[]{:S(2)}, u32[]{:S(2)}) collective-permute-start(bf16[128,1280]{1,0:T(8,128)(2,1)S(1)} %get-tuple-element.42), channel_id=1, source_target_pairs={{0,9},{1,8},{8,1},{9,0},{2,11},{3,10},{10,3},{11,2},{4,13},{5,12},... | collective-permute-start | bytes 983048 | tf_op jit(solution)/shard_map/ppermute | solution.py:498
  38.1 4.3 %collective-permute-done.2.refs_1_ = bf16[128,1280]{1,0:T(8,128)(2,1)S(1)} collective-permute-done((bf16[128,1280]{1,0:T(8,128)(2,1)S(1)}, bf16[128,1280]{1,0:T(8,128)(2,1)S(1)}, u32[]{:S(2)}, u32[]{:S(2)}) %collective-permute-start.2) | collective-permute-done | bytes 327712 | tf_op jit(solution)/shard_map/ppermute | solution.py:498
  42.4 1.2 %collective-permute-start.6 = (bf16[128,1280]{1,0:T(8,128)(2,1)S(1)}, bf16[128,1280]{1,0:T(8,128)(2,1)S(1)}, u32[]{:S(2)}, u32[]{:S(2)}) collective-permute-start(bf16[128,1280]{1,0:T(8,128)(2,1)S(1)} %collective-permute-done.2.refs_1_), channel_id=1, source_target_pairs={{0,16},{16,0},{1,17},{17,1},{2,18},{18,2},{3,19},{19,3},{4,20},{20... | collective-permute-start | bytes 983048 | tf_op jit(solution)/shard_map/ppermute | solution.py:501
  43.7 8.3 %collective-permute-done.3.refs_2_ = bf16[128,1280]{1,0:T(8,128)(2,1)S(1)} collective-permute-done((bf16[128,1280]{1,0:T(8,128)(2,1)S(1)}, bf16[128,1280]{1,0:T(8,128)(2,1)S(1)}, u32[]{:S(2)}, u32[]{:S(2)}) %collective-permute-start.3) | collective-permute-done | bytes 327712 | tf_op jit(solution)/shard_map/ppermute | solution.py:498
  52.0 1.3 %collective-permute-start.7 = (bf16[128,1280]{1,0:T(8,128)(2,1)S(1)}, bf16[128,1280]{1,0:T(8,128)(2,1)S(1)}, u32[]{:S(2)}, u32[]{:S(2)}) collective-permute-start(bf16[128,1280]{1,0:T(8,128)(2,1)S(1)} %collective-permute-done.3.refs_2_), channel_id=1, source_target_pairs={{0,16},{16,0},{1,17},{17,1},{2,18},{18,2},{3,19},{19,3},{4,20},{20... | collective-permute-start | bytes 983048 | tf_op jit(solution)/shard_map/ppermute | solution.py:501
  53.2 1.6 %convolution_convert_fusion.grads = bf16[512,256]{1,0:T(8,128)(2,1)S(1)} fusion(bf16[512,5120]{1,0:T(8,128)(2,1)S(1)} %copy-done.3, bf16[256,5120]{1,0:T(8,128)(2,1)S(1)} %copy-done.2), kind=kOutput, calls=%fused_computation | convolution fusion | flops 1342308352 | bytes 8126464 | tf_op jit(solution)/shard_map/dot_general | solution.py:492
  55.1 7.3 %attention_backward.1 = (bf16[512,256]{1,0:T(8,128)(2,1)}, bf16[1024,256]{1,0:T(8,128)(2,1)S(1)}, f32[1024,256]{1,0:T(8,128)S(1)}, bf16[1024,256]{1,0:T(8,128)(2,1)S(1)}) custom-call(s32[5]{0:T(128)S(1)} %stack.23.ids, s32[5,32]{1,0:T(8,128)S(1)} %bitcast.11, bf16[512,256]{1,0:T(8,128)(2,1)S(1)} %get-tuple-element.36.q.queries, ...), custom_call_target="tpu_custom_call" | custom-call | flops 1800000000 | bytes 5000000 | tf_op jit(solution)/shard_map/attention_backward/pallas_call | solution.py:184
  62.5 2.4 %collective-permute-start.15 = (bf16[1024,256]{1,0:T(8,128)(2,1)S(1)}, bf16[1024,256]{1,0:T(8,128)(2,1)S(1)}, u32[]{:S(2)}, u32[]{:S(2)}) collective-permute-start(bf16[1024,256]{1,0:T(8,128)(2,1)S(1)} %get-tuple-element.51), channel_id=1, source_target_pairs={{16,0},{32,16},{48,32},{64,48},{80,64},{96,80},{112,96},{128,112},... | collective-permute-start | bytes 1572872 | tf_op jit(solution)/shard_map/ppermute | solution.py:543
  65.0 2.8 %collective-permute-start.10 = (bf16[512,256]{1,0:T(8,128)(2,1)S(1)}, bf16[512,256]{1,0:T(8,128)(2,1)S(1)}, u32[]{:S(2)}, u32[]{:S(2)}) collective-permute-start(bf16[512,256]{1,0:T(8,128)(2,1)S(1)} %get-tuple-element.43.refs_8_.att), channel_id=1, source_target_pairs={{0,8},{1,9},{8,0},{9,1},{2,10},{3,11},{10,2},{11,3},{4,12},{5,13},... | collective-permute-start | bytes 786440 | tf_op jit(solution)/shard_map/ppermute | solution.py:507
  67.7 1.4 %collective-permute-start.9 = (bf16[512,256]{1,0:T(8,128)(2,1)S(1)}, bf16[512,256]{1,0:T(8,128)(2,1)S(1)}, u32[]{:S(2)}, u32[]{:S(2)}) collective-permute-start(bf16[512,256]{1,0:T(8,128)(2,1)S(1)} %get-tuple-element.43.refs_8_.att), channel_id=1, source_target_pairs={{0,1},{1,0},{8,9},{9,8},{2,3},{3,2},{10,11},{11,10},{4,5},{5,4},{1... | collective-permute-start | bytes 786440 | tf_op jit(solution)/shard_map/ppermute | solution.py:507
  69.5 5.7 %collective-permute-done.11.refs_11_ = bf16[512,256]{1,0:T(8,128)(2,1)S(1)} collective-permute-done((bf16[512,256]{1,0:T(8,128)(2,1)S(1)}, bf16[512,256]{1,0:T(8,128)(2,1)S(1)}, u32[]{:S(2)}, u32[]{:S(2)}) %collective-permute-start.11) | collective-permute-done | bytes 262176 | tf_op jit(solution)/shard_map/ppermute | solution.py:507
  75.3 2.0 %collective-permute-start.16 = (bf16[1024,256]{1,0:T(8,128)(2,1)S(1)}, bf16[1024,256]{1,0:T(8,128)(2,1)S(1)}, u32[]{:S(2)}, u32[]{:S(2)}) collective-permute-start(bf16[1024,256]{1,0:T(8,128)(2,1)S(1)} %get-tuple-element.52), channel_id=1, source_target_pairs={{0,16},{16,32},{32,48},{48,64},{64,80},{80,96},{96,112},{112,128},... | collective-permute-start | bytes 1572872 | tf_op jit(solution)/shard_map/ppermute | solution.py:544
  77.3 2.9 %collective-permute-done.10.refs_10_ = bf16[512,256]{1,0:T(8,128)(2,1)S(1)} collective-permute-done((bf16[512,256]{1,0:T(8,128)(2,1)S(1)}, bf16[512,256]{1,0:T(8,128)(2,1)S(1)}, u32[]{:S(2)}, u32[]{:S(2)}) %collective-permute-start.10) | collective-permute-done | bytes 262176 | tf_op jit(solution)/shard_map/ppermute | solution.py:507
  80.2 2.0 %project.3 = (bf16[320,512]{1,0:T(8,128)(2,1)S(1)}, bf16[320,512]{1,0:T(8,128)(2,1)S(1)}) custom-call(s32[5]{0:T(128)S(1)} %stack.23.ids, bf16[128,1280]{1,0:T(8,128)(2,1)S(1)} %get-tuple-element.39.refs_0_, bf16[128,1280]{1,0:T(8,128)(2,1)S(1)} %collective-permute-done.2.refs_1_, bf16[128,1280]{1,0:T(8,128)(2,1)S(1)} %collective-permute-done.3.refs_2_, ...), custom_call_target="tpu_custom_call" | custom-call | flops 670000000 | bytes 3000000 | tf_op jit(solution)/shard_map/project/pallas_call | solution.py:275
  82.2 7.3 %collective-permute-start.12 = (bf16[320,512]{1,0:T(8,128)(2,1)S(1)}, bf16[320,512]{1,0:T(8,128)(2,1)S(1)}, u32[]{:S(2)}, u32[]{:S(2)}) collective-permute-start(bf16[320,512]{1,0:T(8,128)(2,1)S(1)} %get-tuple-element.45), channel_id=1, source_target_pairs={{0,4},{2,6},{4,0},{6,2},{1,5},{3,7},{5,1},{7,3},{8,12},{10,14},{12... | collective-permute-start | bytes 983048 | tf_op jit(solution)/shard_map/ppermute | solution.py:526
  89.4 1.2 collective-permute-start.13
  90.7 1.9 %project.2 = (bf16[320,512]{1,0:T(8,128)(2,1)S(1)}, bf16[320,512]{1,0:T(8,128)(2,1)S(1)}) custom-call(s32[5]{0:T(128)S(1)} %stack.23.ids, bf16[128,1280]{1,0:T(8,128)(2,1)S(1)} %get-tuple-element.39.refs_0_, bf16[128,1280]{1,0:T(8,128)(2,1)S(1)} %collective-permute-done.2.refs_1_, bf16[128,1280]{1,0:T(8,128)(2,1)S(1)} %collective-permute-done.3.refs_2_, ...), custom_call_target="tpu_custom_call" | custom-call | flops 670000000 | bytes 3000000 | tf_op jit(solution)/shard_map/project/pallas_call | solution.py:275
  92.7 0.9 settle.1
  94.2 2.5 %collective-permute-start.21 = (bf16[256,320]{1,0:T(8,128)(2,1)S(1)}, bf16[256,320]{1,0:T(8,128)(2,1)S(1)}, u32[]{:S(2)}, u32[]{:S(2)}) collective-permute-start(bf16[256,320]{1,0:T(8,128)(2,1)S(1)} %get-tuple-element.62), channel_id=1, source_target_pairs={{0,32},{32,0},{64,96},{96,64},{1,33},{33,1},{65,97},{97,65},{2,34}... | collective-permute-start | bytes 491528 | tf_op jit(solution)/shard_map/ppermute | solution.py:517
  96.7 22.5 %collective-permute-done.13 = bf16[320,512]{1,0:T(8,128)(2,1)S(1)} collective-permute-done((bf16[320,512]{1,0:T(8,128)(2,1)S(1)}, bf16[320,512]{1,0:T(8,128)(2,1)S(1)}, u32[]{:S(2)}, u32[]{:S(2)}) %collective-permute-start.13) | collective-permute-done | bytes 327712 | tf_op jit(solution)/shard_map/ppermute | solution.py:526
  119.2 0.9 fusion
  120.1 2.3 %gram.1 = (f32[2,1,128,128]{3,2,1,0:T(8,128)}, f32[2,1,320,320]{3,2,1,0:T(8,128)}) custom-call(bf16[256,320]{1,0:T(8,128)(2,1)S(1)} %get-tuple-element.59.refs_0_, bf16[256,320]{1,0:T(8,128)(2,1)S(1)} %collective-permute-done.19.refs_1_, bf16[256,320]{1,0:T(8,128)(2,1)S(1)} %collective-permute-done.20.refs_2_, ...), custom_call_target="tpu_custom_call" | custom-call | flops 400000000 | bytes 2000000 | tf_op jit(solution)/shard_map/gram/pallas_call | solution.py:403
  (34 shorter events, 3.7 us)
Async XLA Ops:
  1.8 10.6 %collective-permute-start.1 = (bf16[512,512]{1,0:T(8,128)(2,1)S(1)}, bf16[512,512]{1,0:T(8,128)(2,1)S(1)}, u32[]{:S(2)}, u32[]{:S(2)}) collective-permute-start(bf16[512,512]{1,0:T(8,128)(2,1)S(1)} %get-tuple-element.37.both), channel_id=1, source_target_pairs={{16,0},{32,16},{48,32},{64,48},{80,64},{96,80},{112,96},{128,112},... | collective-permute-start | bytes 1572872 | tf_op jit(solution)/shard_map/ppermute | solution.py:490
  4.4 9.2 %collective-permute-start = (bf16[512,512]{1,0:T(8,128)(2,1)S(1)}, bf16[512,512]{1,0:T(8,128)(2,1)S(1)}, u32[]{:S(2)}, u32[]{:S(2)}) collective-permute-start(bf16[512,512]{1,0:T(8,128)(2,1)S(1)} %get-tuple-element.37.both), channel_id=1, source_target_pairs={{0,16},{16,32},{32,48},{48,64},{64,80},{80,96},{96,112},{112,128},... | collective-permute-start | bytes 1572872 | tf_op jit(solution)/shard_map/ppermute | solution.py:489
  13.6 0.7 copy-start
  19.3 33.9 %copy-start.3 = (bf16[512,5120]{1,0:T(8,128)(2,1)S(1)}, bf16[512,5120]{1,0:T(8,128)(2,1)}, u32[]{:S(2)}) copy-start(bf16[512,5120]{1,0:T(8,128)(2,1)} %up.1) | copy-start | bytes 15728644
  24.4 28.8 %copy-start.2 = (bf16[256,5120]{1,0:T(8,128)(2,1)S(1)}, bf16[256,5120]{1,0:T(8,128)(2,1)}, u32[]{:S(2)}) copy-start(bf16[256,5120]{1,0:T(8,128)(2,1)} %w.1) | copy-start | bytes 7864324
  24.4 43.3 %collective-permute-start.17 = (bf16[256,2560]{1,0:T(8,128)(2,1)S(1)}, bf16[256,2560]{1,0:T(8,128)(2,1)S(1)}, u32[]{:S(2)}, u32[]{:S(2)}) collective-permute-start(bf16[256,2560]{1,0:T(8,128)(2,1)S(1)} %get-tuple-element.56), channel_id=1, source_target_pairs={{0,16},{16,0},{1,17},{17,1},{2,18},{18,2},{3,19},{19,3},{4,20},{20... | collective-permute-start | bytes 3932168 | tf_op jit(solution)/shard_map/ppermute | solution.py:510
  32.9 9.6 %collective-permute-start.2 = (bf16[128,1280]{1,0:T(8,128)(2,1)S(1)}, bf16[128,1280]{1,0:T(8,128)(2,1)S(1)}, u32[]{:S(2)}, u32[]{:S(2)}) collective-permute-start(bf16[128,1280]{1,0:T(8,128)(2,1)S(1)} %get-tuple-element.40), channel_id=1, source_target_pairs={{0,1},{1,0},{8,9},{9,8},{2,3},{3,2},{10,11},{11,10},{4,5},{5,4},{1... | collective-permute-start | bytes 983048 | tf_op jit(solution)/shard_map/ppermute | solution.py:498
  34.6 17.4 %collective-permute-start.3 = (bf16[128,1280]{1,0:T(8,128)(2,1)S(1)}, bf16[128,1280]{1,0:T(8,128)(2,1)S(1)}, u32[]{:S(2)}, u32[]{:S(2)}) collective-permute-start(bf16[128,1280]{1,0:T(8,128)(2,1)S(1)} %get-tuple-element.41), channel_id=1, source_target_pairs={{0,8},{1,9},{8,0},{9,1},{2,10},{3,11},{10,2},{11,3},{4,12},{5,13},... | collective-permute-start | bytes 983048 | tf_op jit(solution)/shard_map/ppermute | solution.py:498
  35.4 19.4 %collective-permute-start.4 = (bf16[128,1280]{1,0:T(8,128)(2,1)S(1)}, bf16[128,1280]{1,0:T(8,128)(2,1)S(1)}, u32[]{:S(2)}, u32[]{:S(2)}) collective-permute-start(bf16[128,1280]{1,0:T(8,128)(2,1)S(1)} %get-tuple-element.42), channel_id=1, source_target_pairs={{0,9},{1,8},{8,1},{9,0},{2,11},{3,10},{10,3},{11,2},{4,13},{5,12},... | collective-permute-start | bytes 983048 | tf_op jit(solution)/shard_map/ppermute | solution.py:498
  37.4 17.7 %copy-start.1 = (s32[32,5]{0,1:T(8,128)S(1)}, s32[32,5]{0,1:T(8,128)}, u32[]{:S(2)}) copy-start(s32[32,5]{0,1:T(8,128)} %param.11) | copy-start | bytes 1924
  37.4 25.1 %collective-permute-start.5 = (bf16[128,1280]{1,0:T(8,128)(2,1)S(1)}, bf16[128,1280]{1,0:T(8,128)(2,1)S(1)}, u32[]{:S(2)}, u32[]{:S(2)}) collective-permute-start(bf16[128,1280]{1,0:T(8,128)(2,1)S(1)} %get-tuple-element.39.refs_0_), channel_id=1, source_target_pairs={{0,16},{16,0},{1,17},{17,1},{2,18},{18,2},{3,19},{19,3},{4,20},{20... | collective-permute-start | bytes 983048 | tf_op jit(solution)/shard_map/ppermute | solution.py:501
  42.4 22.4 %collective-permute-start.6 = (bf16[128,1280]{1,0:T(8,128)(2,1)S(1)}, bf16[128,1280]{1,0:T(8,128)(2,1)S(1)}, u32[]{:S(2)}, u32[]{:S(2)}) collective-permute-start(bf16[128,1280]{1,0:T(8,128)(2,1)S(1)} %collective-permute-done.2.refs_1_), channel_id=1, source_target_pairs={{0,16},{16,0},{1,17},{17,1},{2,18},{18,2},{3,19},{19,3},{4,20},{20... | collective-permute-start | bytes 983048 | tf_op jit(solution)/shard_map/ppermute | solution.py:501
  52.0 13.0 %collective-permute-start.7 = (bf16[128,1280]{1,0:T(8,128)(2,1)S(1)}, bf16[128,1280]{1,0:T(8,128)(2,1)S(1)}, u32[]{:S(2)}, u32[]{:S(2)}) collective-permute-start(bf16[128,1280]{1,0:T(8,128)(2,1)S(1)} %collective-permute-done.3.refs_2_), channel_id=1, source_target_pairs={{0,16},{16,0},{1,17},{17,1},{2,18},{18,2},{3,19},{19,3},{4,20},{20... | collective-permute-start | bytes 983048 | tf_op jit(solution)/shard_map/ppermute | solution.py:501
  54.8 14.6 %collective-permute-start.8 = (bf16[128,1280]{1,0:T(8,128)(2,1)S(1)}, bf16[128,1280]{1,0:T(8,128)(2,1)S(1)}, u32[]{:S(2)}, u32[]{:S(2)}) collective-permute-start(bf16[128,1280]{1,0:T(8,128)(2,1)S(1)} %collective-permute-done.4.refs_3_), channel_id=1, source_target_pairs={{0,16},{16,0},{1,17},{17,1},{2,18},{18,2},{3,19},{19,3},{4,20},{20... | collective-permute-start | bytes 983048 | tf_op jit(solution)/shard_map/ppermute | solution.py:501
  62.5 30.2 %collective-permute-start.15 = (bf16[1024,256]{1,0:T(8,128)(2,1)S(1)}, bf16[1024,256]{1,0:T(8,128)(2,1)S(1)}, u32[]{:S(2)}, u32[]{:S(2)}) collective-permute-start(bf16[1024,256]{1,0:T(8,128)(2,1)S(1)} %get-tuple-element.51), channel_id=1, source_target_pairs={{16,0},{32,16},{48,32},{64,48},{80,64},{96,80},{112,96},{128,112},... | collective-permute-start | bytes 1572872 | tf_op jit(solution)/shard_map/ppermute | solution.py:543
  64.9 10.4 %collective-permute-start.11 = (bf16[512,256]{1,0:T(8,128)(2,1)S(1)}, bf16[512,256]{1,0:T(8,128)(2,1)S(1)}, u32[]{:S(2)}, u32[]{:S(2)}) collective-permute-start(bf16[512,256]{1,0:T(8,128)(2,1)S(1)} %get-tuple-element.43.refs_8_.att), channel_id=1, source_target_pairs={{0,9},{1,8},{8,1},{9,0},{2,11},{3,10},{10,3},{11,2},{4,13},{5,12},... | collective-permute-start | bytes 786440 | tf_op jit(solution)/shard_map/ppermute | solution.py:507
  65.0 15.2 %collective-permute-start.10 = (bf16[512,256]{1,0:T(8,128)(2,1)S(1)}, bf16[512,256]{1,0:T(8,128)(2,1)S(1)}, u32[]{:S(2)}, u32[]{:S(2)}) collective-permute-start(bf16[512,256]{1,0:T(8,128)(2,1)S(1)} %get-tuple-element.43.refs_8_.att), channel_id=1, source_target_pairs={{0,8},{1,9},{8,0},{9,1},{2,10},{3,11},{10,2},{11,3},{4,12},{5,13},... | collective-permute-start | bytes 786440 | tf_op jit(solution)/shard_map/ppermute | solution.py:507
  67.7 12.5 %collective-permute-start.9 = (bf16[512,256]{1,0:T(8,128)(2,1)S(1)}, bf16[512,256]{1,0:T(8,128)(2,1)S(1)}, u32[]{:S(2)}, u32[]{:S(2)}) collective-permute-start(bf16[512,256]{1,0:T(8,128)(2,1)S(1)} %get-tuple-element.43.refs_8_.att), channel_id=1, source_target_pairs={{0,1},{1,0},{8,9},{9,8},{2,3},{3,2},{10,11},{11,10},{4,5},{5,4},{1... | collective-permute-start | bytes 786440 | tf_op jit(solution)/shard_map/ppermute | solution.py:507
  69.4 24.2 %collective-permute-start.18 = (bf16[256,1280]{1,0:T(8,128)(2,1)S(1)}, bf16[256,1280]{1,0:T(8,128)(2,1)S(1)}, u32[]{:S(2)}, u32[]{:S(2)}) collective-permute-start(bf16[256,1280]{1,0:T(8,128)(2,1)S(1)} %get-tuple-element.58), channel_id=1, source_target_pairs={{0,128},{128,0},{1,129},{129,1},{2,130},{130,2},{3,131},{131,3},{4... | collective-permute-start | bytes 1966088 | tf_op jit(solution)/shard_map/ppermute | solution.py:512
  75.3 17.5 %collective-permute-start.16 = (bf16[1024,256]{1,0:T(8,128)(2,1)S(1)}, bf16[1024,256]{1,0:T(8,128)(2,1)S(1)}, u32[]{:S(2)}, u32[]{:S(2)}) collective-permute-start(bf16[1024,256]{1,0:T(8,128)(2,1)S(1)} %get-tuple-element.52), channel_id=1, source_target_pairs={{0,16},{16,32},{32,48},{48,64},{64,80},{80,96},{96,112},{112,128},... | collective-permute-start | bytes 1572872 | tf_op jit(solution)/shard_map/ppermute | solution.py:544
  82.2 12.0 %collective-permute-start.12 = (bf16[320,512]{1,0:T(8,128)(2,1)S(1)}, bf16[320,512]{1,0:T(8,128)(2,1)S(1)}, u32[]{:S(2)}, u32[]{:S(2)}) collective-permute-start(bf16[320,512]{1,0:T(8,128)(2,1)S(1)} %get-tuple-element.45), channel_id=1, source_target_pairs={{0,4},{2,6},{4,0},{6,2},{1,5},{3,7},{5,1},{7,3},{8,12},{10,14},{12... | collective-permute-start | bytes 983048 | tf_op jit(solution)/shard_map/ppermute | solution.py:526
  89.4 29.7 %collective-permute-start.13 = (bf16[320,512]{1,0:T(8,128)(2,1)S(1)}, bf16[320,512]{1,0:T(8,128)(2,1)S(1)}, u32[]{:S(2)}, u32[]{:S(2)}) collective-permute-start(bf16[320,512]{1,0:T(8,128)(2,1)S(1)} %get-tuple-element.46), channel_id=1, source_target_pairs={{0,2},{2,0},{4,6},{6,4},{1,3},{3,1},{5,7},{7,5},{8,10},{10,8},{12,... | collective-permute-start | bytes 983048 | tf_op jit(solution)/shard_map/ppermute | solution.py:526
  92.6 26.6 %collective-permute-start.14 = (bf16[320,512]{1,0:T(8,128)(2,1)S(1)}, bf16[320,512]{1,0:T(8,128)(2,1)S(1)}, u32[]{:S(2)}, u32[]{:S(2)}) collective-permute-start(bf16[320,512]{1,0:T(8,128)(2,1)S(1)} %get-tuple-element.47), channel_id=1, source_target_pairs={{0,6},{2,4},{4,2},{6,0},{1,7},{3,5},{5,3},{7,1},{8,14},{10,12},{12... | collective-permute-start | bytes 983048 | tf_op jit(solution)/shard_map/ppermute | solution.py:526
  93.9 26.1 %collective-permute-start.19 = (bf16[256,320]{1,0:T(8,128)(2,1)S(1)}, bf16[256,320]{1,0:T(8,128)(2,1)S(1)}, u32[]{:S(2)}, u32[]{:S(2)}) collective-permute-start(bf16[256,320]{1,0:T(8,128)(2,1)S(1)} %get-tuple-element.60), channel_id=1, source_target_pairs={{0,64},{32,96},{64,0},{96,32},{1,65},{33,97},{65,1},{97,33},{2,66}... | collective-permute-start | bytes 491528 | tf_op jit(solution)/shard_map/ppermute | solution.py:517
  94.0 26.0 %collective-permute-start.20 = (bf16[256,320]{1,0:T(8,128)(2,1)S(1)}, bf16[256,320]{1,0:T(8,128)(2,1)S(1)}, u32[]{:S(2)}, u32[]{:S(2)}) collective-permute-start(bf16[256,320]{1,0:T(8,128)(2,1)S(1)} %get-tuple-element.61), channel_id=1, source_target_pairs={{0,96},{32,64},{64,32},{96,0},{1,97},{33,65},{65,33},{97,1},{2,98}... | collective-permute-start | bytes 491528 | tf_op jit(solution)/shard_map/ppermute | solution.py:517
  94.2 25.9 %collective-permute-start.21 = (bf16[256,320]{1,0:T(8,128)(2,1)S(1)}, bf16[256,320]{1,0:T(8,128)(2,1)S(1)}, u32[]{:S(2)}, u32[]{:S(2)}) collective-permute-start(bf16[256,320]{1,0:T(8,128)(2,1)S(1)} %get-tuple-element.62), channel_id=1, source_target_pairs={{0,32},{32,0},{64,96},{96,64},{1,33},{33,1},{65,97},{97,65},{2,34}... | collective-permute-start | bytes 491528 | tf_op jit(solution)/shard_map/ppermute | solution.py:517
